TPU v7x, 256 devices: a whole 4x4x8 slice. The times are simulated.
256 devices in a mesh: section: 8 (over y, core), ctx: 32 (over z, x).
Axes of the slice: x: 4, y: 4, z: 8, core: 2. Of those that a mesh axis runs over, the one named last changes fastest.
Arguments:
- section_input: bfloat16 [2, 4096, 2048], P(None, 'ctx'), may hold values from -6 to 6
- cotangent: bfloat16 [2, 4096, 2048], P(None, 'ctx'), may hold values from -6 to 6
- w_query: bfloat16 [8, 2048, 1024], P('section', 'ctx'), may hold values from -0.125 to 0.125
- w_key: bfloat16 [8, 2048, 1024], P('section', 'ctx'), may hold values from -0.125 to 0.125
- w_value: bfloat16 [8, 2048, 1024], P('section', 'ctx'), may hold values from -0.125 to 0.125
- w_out: bfloat16 [8, 1024, 2048], P('section', 'ctx'), may hold values from -0.1875 to 0.1875
- block_mask: int32 [2, 128, 2], P(None, 'ctx'), may hold values 0 or 1
Outputs:
- section_output: bfloat16 [8, 2, 4096, 2048], P('section', None, 'ctx')
- input_grad: bfloat16 [8, 2, 4096, 2048], P('section', None, 'ctx')
Inputs may be any that keep to these rules, and one draw needn't show every extreme that they name: A block always attends to itself; column 0 and 1 of block_mask choose its two neighbour blocks.
All inputs are finite; a program needn't handle non-finite values.
Results may differ from a plain program's by a relative error of at most 0.03.
Values may be sent and summed in bfloat16 or wider, within the bound.
No kernel may reach another device: no remote copies, remote signals or barrier semaphores. Data moves between devices by JAX's collectives and lax.ppermute only.
A program may use at most 128 MiB of HBM per device.

v0:
```python
import jax
import jax.numpy as jnp
from jax import lax
from jax.sharding import PartitionSpec as P

D = 2048
HEADS = 8
HDIM = 128
BLOCKS_DEV = 4
BLK = 32


def padded(block, sides, width):
    for axis, dim in sides:
        count = lax.axis_size(axis)
        forward = [(i, i + 1) for i in range(count - 1)]
        backward = [(target, source) for source, target in forward]
        low = lax.ppermute(
            lax.slice_in_dim(block, block.shape[dim] - width, None, axis=dim), axis, forward
        )
        high = lax.ppermute(lax.slice_in_dim(block, 0, width, axis=dim), axis, backward)
        block = jnp.concatenate([low, block, high], axis=dim)
    return block


def shifted(block, axis, distance):
    devices = range(lax.axis_size(axis))
    route = [(i - distance, i) for i in devices if i - distance in devices]
    return lax.ppermute(block, axis, route)


def rms_scale(values):
    return values * lax.rsqrt(jnp.mean(values * values, axis=-1, keepdims=True) + 1e-06)


def allowed_keys(mask_rows, block_ids, block_count):
    mask_float = mask_rows.astype(jnp.float32)
    left = mask_float[:, 0] * (block_ids > 0).astype(jnp.float32)
    right = mask_float[:, 1] * (block_ids < block_count - 1).astype(jnp.float32)
    return jnp.stack([left, jnp.ones_like(left), right], axis=1)


def project(layer_in, w_query, w_key, w_value):
    length = layer_in.shape[0]
    normed = rms_scale(layer_in.astype(jnp.float32)).astype(jnp.bfloat16)

    def head_normed(weight):
        out = jnp.dot(normed, weight, preferred_element_type=jnp.float32)
        out = rms_scale(out.reshape(length, HEADS, HDIM))
        return out.reshape(length, HEADS * HDIM).astype(jnp.bfloat16)

    query = head_normed(w_query)
    key = head_normed(w_key)
    value = jnp.dot(normed, w_value, preferred_element_type=jnp.float32).astype(jnp.bfloat16)
    return (query, key, value)


def attend(query, keys_ext, values_ext, allow, layer_in, w_out):
    length = query.shape[0]
    nblock = length // BLK
    queries = query.reshape(nblock, BLK, HEADS, HDIM)

    def windows(extended):
        grid = extended.reshape(nblock + 2, BLK, HEADS, HDIM)
        return jnp.concatenate([grid[:-2], grid[1:-1], grid[2:]], axis=1)

    keys = windows(keys_ext)
    values = windows(values_ext)
    scores = jnp.einsum(
        "bqhd,bkhd->bhqk", queries, keys, preferred_element_type=jnp.float32
    ) * HDIM ** (-0.5)
    weight = jnp.repeat(allow, BLK, axis=1)[:, None, None, :]
    probs = jnp.exp(scores) * weight
    total = jnp.sum(probs, axis=-1)
    attended = jnp.einsum(
        "bhqk,bkhd->bqhd", probs.astype(jnp.bfloat16), values, preferred_element_type=jnp.float32
    )
    attended = attended / jnp.transpose(total, (0, 2, 1))[..., None]
    attended = attended.reshape(length, HEADS * HDIM).astype(jnp.bfloat16)
    update = jnp.dot(attended, w_out, preferred_element_type=jnp.float32)
    return (layer_in.astype(jnp.float32) + update).astype(jnp.bfloat16)


def put_slot(buffer, value, slot, active):
    return jnp.where(active, lax.dynamic_update_index_in_dim(buffer, value, slot, 0), buffer)


def take_slot(buffer, slot):
    return lax.dynamic_index_in_dim(buffer, slot, 0, keepdims=False)


def per_device(section_input, cotangent, w_query, w_key, w_value, w_out, block_mask):
    n_section = lax.axis_size("section")
    n_ctx = lax.axis_size("ctx")
    section = lax.axis_index("section")
    place = lax.axis_index("ctx")
    micro = section_input.shape[0]
    length = section_input.shape[1]
    width = HEADS * HDIM
    full_query, full_key, full_value, full_out = (
        lax.all_gather(w_query[0], "ctx", axis=0, tiled=True),
        lax.all_gather(w_key[0], "ctx", axis=0, tiled=True),
        lax.all_gather(w_value[0], "ctx", axis=0, tiled=True),
        lax.all_gather(w_out[0], "ctx", axis=0, tiled=True),
    )
    block_ids = place * BLOCKS_DEV + jnp.arange(BLOCKS_DEV)
    allows = jax.vmap(lambda rows_mask: allowed_keys(rows_mask, block_ids, BLOCKS_DEV * n_ctx))(
        block_mask
    )
    zero_rows = jnp.zeros((length, D), jnp.bfloat16)
    zero_heads = jnp.zeros((length, width), jnp.bfloat16)
    zero_wide = jnp.zeros((length + 2 * BLK, width), jnp.bfloat16)
    steps_total = n_section + micro - 1

    def run_project(values):
        return project(values, full_query, full_key, full_value)

    def skip_project(values):
        return (zero_heads, zero_heads, zero_heads)

    def run_attend(query, extended, layer_in, allow):
        return attend(query, extended[0], extended[1], allow, layer_in, full_out)

    def skip_attend(query, extended, layer_in, allow):
        return zero_rows

    kv_store = jnp.zeros((micro, 2, length, width), jnp.bfloat16)
    inputs = jnp.zeros((micro, length, D), jnp.bfloat16)
    outputs = jnp.zeros((micro, length, D), jnp.bfloat16)
    queries = jnp.zeros((micro, length, width), jnp.bfloat16)

    def forward_step(step, carry):
        incoming, inputs, outputs, queries, kv_store = carry
        micro_id = step - section
        active = (micro_id >= 0) & (micro_id < micro)
        slot = jnp.clip(micro_id, 0, micro - 1)
        layer_in = jnp.where(section == 0, take_slot(section_input, slot), incoming)
        query, key, value = lax.cond(active, run_project, skip_project, layer_in)
        local_kv = jnp.stack([key, value])
        extended = padded(local_kv, (("ctx", 1),), BLK)
        allow = take_slot(allows, slot)
        result = lax.cond(active, run_attend, skip_attend, query, extended, layer_in, allow)
        inputs = put_slot(inputs, layer_in, slot, active)
        outputs = put_slot(outputs, result, slot, active)
        queries = put_slot(queries, query, slot, active)
        kv_store = put_slot(kv_store, local_kv, slot, active)
        incoming = shifted(result, "section", 1)
        return (incoming, inputs, outputs, queries, kv_store)

    carry = (zero_rows, inputs, outputs, queries, kv_store)
    _, inputs, outputs, queries, kv_store = lax.fori_loop(0, steps_total, forward_step, carry)

    def pull_attend(query, extended, layer_in, allow, grad_in):

        def local_attend(query_in, keys_in, values_in, rows_in):
            return attend(query_in, keys_in, values_in, allow, rows_in, full_out)

        _, pull = jax.vjp(local_attend, query, extended[0], extended[1], layer_in)
        return pull(grad_in)

    def skip_pull(query, extended, layer_in, allow, grad_in):
        return (zero_heads, zero_wide, zero_wide, zero_rows)

    def pull_project(layer_in, d_query, own):
        _, pull = jax.vjp(run_project, layer_in)
        return pull((d_query, own[0], own[1]))[0]

    def skip_pull_project(layer_in, d_query, own):
        return zero_rows

    grads = jnp.zeros((micro, length, D), jnp.bfloat16)

    def backward_step(step, carry):
        incoming, grads = carry
        micro_id = step - (n_section - 1 - section)
        active = (micro_id >= 0) & (micro_id < micro)
        slot = jnp.clip(micro_id, 0, micro - 1)
        grad_in = jnp.where(section == n_section - 1, take_slot(cotangent, slot), incoming)
        layer_in = take_slot(inputs, slot)
        query = take_slot(queries, slot)
        extended = padded(take_slot(kv_store, slot), (("ctx", 1),), BLK)
        allow = take_slot(allows, slot)
        d_query, d_keys, d_values, d_direct = lax.cond(
            active, pull_attend, skip_pull, query, extended, layer_in, allow, grad_in
        )
        d_wide = jnp.stack([d_keys, d_values])
        rims = jnp.concatenate([d_wide[:, :BLK], d_wide[:, -BLK:]], axis=1)
        returned = padded(rims, (("ctx", 1),), BLK)
        own = d_wide[:, BLK:-BLK]
        own = own.at[:, :BLK].add(returned[:, :BLK])
        own = own.at[:, -BLK:].add(returned[:, -BLK:])
        d_projected = lax.cond(active, pull_project, skip_pull_project, layer_in, d_query, own)
        d_input = d_direct + d_projected
        grads = put_slot(grads, d_input, slot, active)
        incoming = shifted(d_input, "section", -1)
        return (incoming, grads)

    _, grads = lax.fori_loop(0, steps_total, backward_step, (zero_rows, grads))
    return (outputs[None], grads[None])


def solution(mesh):
    return jax.shard_map(
        per_device,
        mesh=mesh,
        in_specs=(
            P(None, "ctx", None),
            P(None, "ctx", None),
            P("section", "ctx", None),
            P("section", "ctx", None),
            P("section", "ctx", None),
            P("section", "ctx", None),
            P(None, "ctx", None),
        ),
        out_specs=(P("section", None, "ctx", None), P("section", None, "ctx", None)),
        check_vma=False,
    )
```

profile of v0, /device:TPU:100, one launch (start us, length us, event | category | flops | bytes accessed | tf_op | source)
XLA Modules:
  0.0 1310.9 jit_solution(2852460559565105699)
XLA Ops:
  11.0 81.4 %all-gather.9.cloned.1.call-done = bf16[1,2048,1024]{2,1,0:T(8,128)(2,1)} async-done(((bf16[1,64,1024]{2,1,0:T(8,128)(2,1)}), bf16[1,2048,1024]{2,1,0:T(8,128)(2,1)}) %all-gather.9.cloned.1.call-update) | async-done | bytes 4194320 | tf_op jit(solution)/shard_map/all_gather | solution.py:101
  92.4 81.8 %all-gather.11.cloned.1.call-done = bf16[1,2048,1024]{2,1,0:T(8,128)(2,1)} async-done(((bf16[1,64,1024]{2,1,0:T(8,128)(2,1)}), bf16[1,2048,1024]{2,1,0:T(8,128)(2,1)}) %all-gather.11.cloned.1.call-update) | async-done | bytes 4194320 | tf_op jit(solution)/shard_map/all_gather | solution.py:102
  174.2 81.8 %all-gather.13.cloned.1.call-done = bf16[1,2048,1024]{2,1,0:T(8,128)(2,1)} async-done(((bf16[1,64,1024]{2,1,0:T(8,128)(2,1)}), bf16[1,2048,1024]{2,1,0:T(8,128)(2,1)}) %all-gather.13.cloned.1.call-update) | async-done | bytes 4194320 | tf_op jit(solution)/shard_map/all_gather | solution.py:103
  256.0 81.6 %all-gather.15.cloned.1.call-done = bf16[1,1024,2048]{2,1,0:T(8,128)(2,1)} async-done(((bf16[1,32,2048]{2,1,0:T(8,128)(2,1)}), bf16[1,1024,2048]{2,1,0:T(8,128)(2,1)}) %all-gather.15.cloned.1.call-update) | async-done | bytes 4194320 | tf_op jit(solution)/shard_map/all_gather | solution.py:104
  340.9 287.7 %while.41 = (s32[]{:T(128)}, bf16[128,2048]{1,0:T(8,128)(2,1)S(1)}, bf16[2,128,2048]{2,1,0:T(8,128)(2,1)S(1)}, bf16[2,128,2048]{2,1,0:T(8,128)(2,1)}, bf16[2,128...) while((s32[]{:T(128)}, bf16[128,2048]{1,0:T(8,128)(2,1)S(1)}, ...), condition=%wide.region_9.10_spmd, body=%wide.region_0.9_spmd.sunk | while | flops 2211841024 | bytes 75189416 | solution.py:151
  342.2 10.8 conditional.8
  375.8 10.8 conditional.8
  422.4 18.3 %collective-permute-start.2 = (bf16[128,2048]{1,0:T(8,128)(2,1)}, bf16[128,2048]{1,0:T(8,128)(2,1)S(1)}, u32[]{:S(2)}, u32[]{:S(2)}) collective-permute-start(bf16[128,2048]{1,0:T(8,128)(2,1)} %get-tuple-element.1251), channel_id=1, source_target_pairs={{0,32},{32,64},{64,96},{96,128},{128,160},{160,192},{192,224},{1,3... | collective-permute-start | bytes 1572872 | tf_op jit(solution)/shard_map/while/body/eval_jaxpr/ppermute | solution.py:29
  483.9 23.4 %collective-permute-start.2 = (bf16[128,2048]{1,0:T(8,128)(2,1)}, bf16[128,2048]{1,0:T(8,128)(2,1)S(1)}, u32[]{:S(2)}, u32[]{:S(2)}) collective-permute-start(bf16[128,2048]{1,0:T(8,128)(2,1)} %get-tuple-element.1251), channel_id=1, source_target_pairs={{0,32},{32,64},{64,96},{96,128},{128,160},{160,192},{192,224},{1,3... | collective-permute-start | bytes 1572872 | tf_op jit(solution)/shard_map/while/body/eval_jaxpr/ppermute | solution.py:29
  550.9 10.4 collective-permute-start.2
  605.0 19.9 %collective-permute-start.2 = (bf16[128,2048]{1,0:T(8,128)(2,1)}, bf16[128,2048]{1,0:T(8,128)(2,1)S(1)}, u32[]{:S(2)}, u32[]{:S(2)}) collective-permute-start(bf16[128,2048]{1,0:T(8,128)(2,1)} %get-tuple-element.1251), channel_id=1, source_target_pairs={{0,32},{32,64},{64,96},{96,128},{128,160},{160,192},{192,224},{1,3... | collective-permute-start | bytes 1572872 | tf_op jit(solution)/shard_map/while/body/eval_jaxpr/ppermute | solution.py:29
  630.5 673.9 %while.42 = (s32[]{:T(128)}, bf16[128,2048]{1,0:T(8,128)(2,1)}, bf16[2,128,2048]{2,1,0:T(8,128)(2,1)}, s32[]{:T(128)}, bf16[2,2,128,1024]{3,2,1,0:T(8,128)(2,1)}...) while((s32[]{:T(128)}, bf16[128,2048]{1,0:T(8,128)(2,1)}, ...), condition=%wide.region_24.25_spmd, body=%wide.region_10.24_spmd.sunk | while | flops 3389073152 | bytes 170649296 | solution.py:198
  655.6 8.1 collective-permute-done.6
  709.8 14.3 %collective-permute-done.7 = bf16[128,2048]{1,0:T(8,128)(2,1)S(1)} collective-permute-done((bf16[128,2048]{1,0:T(8,128)(2,1)S(1)}, bf16[128,2048]{1,0:T(8,128)(2,1)S(1)}, u32[]{:S(2)}, u32[]{:S(2)}) %collective-permute-start.7) | collective-permute-done | bytes 524320 | tf_op jit(solution)/shard_map/while/body/eval_jaxpr/ppermute | solution.py:29
  793.5 8.7 collective-permute-done.6
  805.7 20.1 %collective-permute-done.7 = bf16[128,2048]{1,0:T(8,128)(2,1)S(1)} collective-permute-done((bf16[128,2048]{1,0:T(8,128)(2,1)S(1)}, bf16[128,2048]{1,0:T(8,128)(2,1)S(1)}, u32[]{:S(2)}, u32[]{:S(2)}) %collective-permute-start.7) | collective-permute-done | bytes 524320 | tf_op jit(solution)/shard_map/while/body/eval_jaxpr/ppermute | solution.py:29
  906.6 13.0 collective-permute-done.7
  956.3 204.4 %collective-permute-done.7 = bf16[128,2048]{1,0:T(8,128)(2,1)S(1)} collective-permute-done((bf16[128,2048]{1,0:T(8,128)(2,1)S(1)}, bf16[128,2048]{1,0:T(8,128)(2,1)S(1)}, u32[]{:S(2)}, u32[]{:S(2)}) %collective-permute-start.7) | collective-permute-done | bytes 524320 | tf_op jit(solution)/shard_map/while/body/eval_jaxpr/ppermute | solution.py:29
  1174.1 11.2 conditional.10
  1196.9 8.1 collective-permute-done.6
  1205.0 18.6 %conditional.11 = (bf16[128,2048]{1,0:T(8,128)(2,1)S(1)}) conditional(s32[]{:T(128)} %convert_element_type.302, () %tuple.209, (bf16[2,192,1024]{2,1,0:T(8,128)(2,1)S(1)}, bf16[2,32,1024]{2,1,0:T(8,128)(2,1)S(1)}, bf16[2,32,1024]{2,1,0:T(8,128)(2,1)S(1)}, bf16[2048,1024]{1,0:T(8,128)(2,1)}, bf16[2,128,2048]{2,1,0:T(8,128)(2,1)S(1)}, ...), branch_computations={%region_15.15_spmd, %region_16.23_spmd} | conditional | flops 2693800704 | bytes 90314520 | solution.py:192
  1248.1 11.2 conditional.10
  1270.9 8.1 collective-permute-done.6
  1279.0 18.6 %conditional.11 = (bf16[128,2048]{1,0:T(8,128)(2,1)S(1)}) conditional(s32[]{:T(128)} %convert_element_type.302, () %tuple.209, (bf16[2,192,1024]{2,1,0:T(8,128)(2,1)S(1)}, bf16[2,32,1024]{2,1,0:T(8,128)(2,1)S(1)}, bf16[2,32,1024]{2,1,0:T(8,128)(2,1)S(1)}, bf16[2048,1024]{1,0:T(8,128)(2,1)}, bf16[2,128,2048]{2,1,0:T(8,128)(2,1)S(1)}, ...), branch_computations={%region_15.15_spmd, %region_16.23_spmd} | conditional | flops 2693800704 | bytes 90314520 | solution.py:192
  (720 shorter events, 631.3 us)
Async XLA Ops:
  7.2 85.3 %all-gather.9.cloned.1.call-start = ((), (), s32[]{:S(2)}) async-start(), calls=%async_computation | async-start | bytes 4325376 | tf_op jit(solution)/shard_map/all_gather | solution.py:101
  7.9 166.3 %all-gather.11.cloned.1.call-start = ((), (), s32[]{:S(2)}) async-start(), calls=%async_computation.1 | async-start | bytes 4325376 | tf_op jit(solution)/shard_map/all_gather | solution.py:102
  8.6 247.3 %all-gather.13.cloned.1.call-start = ((), (), s32[]{:S(2)}) async-start(), calls=%async_computation.2 | async-start | bytes 4325376 | tf_op jit(solution)/shard_map/all_gather | solution.py:103
  9.4 328.2 %all-gather.15.cloned.1.call-start = ((), (), s32[]{:S(2)}) async-start(), calls=%async_computation.3 | async-start | bytes 4325376 | tf_op jit(solution)/shard_map/all_gather | solution.py:104
  422.4 22.0 %collective-permute-start.2 = (bf16[128,2048]{1,0:T(8,128)(2,1)}, bf16[128,2048]{1,0:T(8,128)(2,1)S(1)}, u32[]{:S(2)}, u32[]{:S(2)}) collective-permute-start(bf16[128,2048]{1,0:T(8,128)(2,1)} %get-tuple-element.1251), channel_id=1, source_target_pairs={{0,32},{32,64},{64,96},{96,128},{128,160},{160,192},{192,224},{1,3... | collective-permute-start | bytes 1572872 | tf_op jit(solution)/shard_map/while/body/eval_jaxpr/ppermute | solution.py:29
  446.0 11.2 collective-permute-start
  458.6 10.7 collective-permute-start.2
  470.9 11.7 collective-permute-start
  483.9 27.1 %collective-permute-start.2 = (bf16[128,2048]{1,0:T(8,128)(2,1)}, bf16[128,2048]{1,0:T(8,128)(2,1)S(1)}, u32[]{:S(2)}, u32[]{:S(2)}) collective-permute-start(bf16[128,2048]{1,0:T(8,128)(2,1)} %get-tuple-element.1251), channel_id=1, source_target_pairs={{0,32},{32,64},{64,96},{96,128},{128,160},{160,192},{192,224},{1,3... | collective-permute-start | bytes 1572872 | tf_op jit(solution)/shard_map/while/body/eval_jaxpr/ppermute | solution.py:29
  512.5 11.7 collective-permute-start
  525.6 10.7 collective-permute-start.2
  537.9 11.7 collective-permute-start
  550.9 14.1 %collective-permute-start.2 = (bf16[128,2048]{1,0:T(8,128)(2,1)}, bf16[128,2048]{1,0:T(8,128)(2,1)S(1)}, u32[]{:S(2)}, u32[]{:S(2)}) collective-permute-start(bf16[128,2048]{1,0:T(8,128)(2,1)} %get-tuple-element.1251), channel_id=1, source_target_pairs={{0,32},{32,64},{64,96},{96,128},{128,160},{160,192},{192,224},{1,3... | collective-permute-start | bytes 1572872 | tf_op jit(solution)/shard_map/while/body/eval_jaxpr/ppermute | solution.py:29
  566.6 11.7 collective-permute-start
  579.7 10.7 collective-permute-start.2
  591.9 11.7 collective-permute-start
  605.0 23.6 %collective-permute-start.2 = (bf16[128,2048]{1,0:T(8,128)(2,1)}, bf16[128,2048]{1,0:T(8,128)(2,1)S(1)}, u32[]{:S(2)}, u32[]{:S(2)}) collective-permute-start(bf16[128,2048]{1,0:T(8,128)(2,1)} %get-tuple-element.1251), channel_id=1, source_target_pairs={{0,32},{32,64},{64,96},{96,128},{128,160},{160,192},{192,224},{1,3... | collective-permute-start | bytes 1572872 | tf_op jit(solution)/shard_map/while/body/eval_jaxpr/ppermute | solution.py:29
  708.5 15.6 %collective-permute-start.7 = (bf16[128,2048]{1,0:T(8,128)(2,1)S(1)}, bf16[128,2048]{1,0:T(8,128)(2,1)S(1)}, u32[]{:S(2)}, u32[]{:S(2)}) collective-permute-start(bf16[128,2048]{1,0:T(8,128)(2,1)S(1)} %get-tuple-element.1276), channel_id=1, source_target_pairs={{32,0},{64,32},{96,64},{128,96},{160,128},{192,160},{224,192},{33,... | collective-permute-start | bytes 1572872 | tf_op jit(solution)/shard_map/while/body/eval_jaxpr/ppermute | solution.py:29
  791.0 11.2 collective-permute-start.6
  804.4 21.4 %collective-permute-start.7 = (bf16[128,2048]{1,0:T(8,128)(2,1)S(1)}, bf16[128,2048]{1,0:T(8,128)(2,1)S(1)}, u32[]{:S(2)}, u32[]{:S(2)}) collective-permute-start(bf16[128,2048]{1,0:T(8,128)(2,1)S(1)} %get-tuple-element.1276), channel_id=1, source_target_pairs={{32,0},{64,32},{96,64},{128,96},{160,128},{192,160},{224,192},{33,... | collective-permute-start | bytes 1572872 | tf_op jit(solution)/shard_map/while/body/eval_jaxpr/ppermute | solution.py:29
  885.2 11.0 collective-permute-start.5
  905.3 14.3 %collective-permute-start.7 = (bf16[128,2048]{1,0:T(8,128)(2,1)S(1)}, bf16[128,2048]{1,0:T(8,128)(2,1)S(1)}, u32[]{:S(2)}, u32[]{:S(2)}) collective-permute-start(bf16[128,2048]{1,0:T(8,128)(2,1)S(1)} %get-tuple-element.1276), channel_id=1, source_target_pairs={{32,0},{64,32},{96,64},{128,96},{160,128},{192,160},{224,192},{33,... | collective-permute-start | bytes 1572872 | tf_op jit(solution)/shard_map/while/body/eval_jaxpr/ppermute | solution.py:29
  955.1 205.7 %collective-permute-start.7 = (bf16[128,2048]{1,0:T(8,128)(2,1)S(1)}, bf16[128,2048]{1,0:T(8,128)(2,1)S(1)}, u32[]{:S(2)}, u32[]{:S(2)}) collective-permute-start(bf16[128,2048]{1,0:T(8,128)(2,1)S(1)} %get-tuple-element.1276), channel_id=1, source_target_pairs={{32,0},{64,32},{96,64},{128,96},{160,128},{192,160},{224,192},{33,... | collective-permute-start | bytes 1572872 | tf_op jit(solution)/shard_map/while/body/eval_jaxpr/ppermute | solution.py:29
  1194.4 10.6 collective-permute-start.6
  (102 other events, 567.5 us)
Sparse Core Ops, SparseCore 0:
  10.6 81.7 all-gather.8
  95.0 79.1 all-gather.10
  176.8 79.1 all-gather.12
  258.4 79.1 all-gather.14
where the time goes:
time: 1320 us; the launch traced here: 1310 us
  waiting for transfers between devices  720 us (55%)
  starting transfers between devices  348 us (26%)
  other arithmetic  89.5 us (7%)
  local copies, waits for them, and re-layouts  75.9 us (6%)
  matrix products  59.4 us (4%)
  between operations  13.8 us (1%)
    ppermute x18, waiting for transfers between devices, shifted(): return lax.ppermute(block, axis, route)  283 us
    ppermute x27, starting transfers between devices, padded(): lax.ppermute(lax.slice_in_dim(block, block.shape[dim] - width, None, axis...  183 us
    ppermute x18, starting transfers between devices, shifted(): return lax.ppermute(block, axis, route)  107 us
    select_n x45, other arithmetic, put_slot(): jnp.where(active, lax.dynamic_update_index_in_dim(buffer, value, slot, 0)...  83.1 us
    all_gather x1, waiting for transfers between devices, per_device(): lax.all_gather(w_value[0], 'ctx', axis=0, tiled=True)  81.8 us
    all_gather x1, waiting for transfers between devices, per_device(): lax.all_gather(w_key[0], 'ctx', axis=0, tiled=True)  81.8 us
    all_gather x1, waiting for transfers between devices, per_device(): lax.all_gather(w_out[0], 'ctx', axis=0, tiled=True)  81.6 us
    all_gather x1, waiting for transfers between devices, per_device(): lax.all_gather(w_query[0], 'ctx', axis=0, tiled=True)  81.4 us
  transfers between devices with their start and end apart: 76, of which 58 were waited for; matrix products, arithmetic and copies ran while one was open for 4% of the time, Pallas kernels for 0%

commit v1 on v0

v1 whole, which is shorter than its diff:
```python
import jax
import jax.numpy as jnp
from jax import lax
from jax.experimental import pallas as pl
from jax.experimental.pallas import tpu as pltpu
from jax.sharding import PartitionSpec as P

D = 2048
HEADS = 8
HDIM = 128
BLOCKS_DEV = 4
BLK = 32
ROWS = BLK * BLOCKS_DEV
EXT = ROWS + 2 * BLK
WIDTH = HEADS * HDIM
PACK = 2 * WIDTH + 128
EPS = 1e-06
VMEM_LIMIT = 24 << 20
SCALE = HDIM ** (-0.5)
F32 = jnp.float32
BF16 = jnp.bfloat16

NT = (((1,), (1,)), ((), ()))
NN = (((1,), (0,)), ((), ()))
TN = (((0,), (0,)), ((), ()))


def dot(a, b, dims=NN):
    return lax.dot_general(a, b, dims, preferred_element_type=F32)


def wtile(w_ref, row, count, col, width):
    tile = w_ref[:, row : row + count, col : col + width]
    return tile.reshape(tile.shape[0] * count, width)


def forward_body(
    flags,
    x0_ref,
    x_ref,
    xl_ref,
    xr_ref,
    mask_ref,
    w_ref,
    xs_in,
    out_in,
    qa_in,
    kv_in,
    rr_in,
    next_ref,
    left_ref,
    right_ref,
    xs_ref,
    out_ref,
    qa_ref,
    kv_ref,
    rr_ref,
    xe,
    normed,
    qa,
    kv,
    rr,
    result,
    sem_in,
    sem_out,
):
    active, slot, first = flags[0], flags[1], flags[2]

    @pl.when(active == 1)
    def _():
        @pl.when(first == 1)
        def _():
            copy = pltpu.make_async_copy(x0_ref.at[slot], xe, sem_in.at[0])
            copy.start()
            copy.wait()

        @pl.when(first == 0)
        def _():
            copies = [
                pltpu.make_async_copy(xl_ref, xe.at[:BLK], sem_in.at[0]),
                pltpu.make_async_copy(x_ref, xe.at[BLK : BLK + ROWS], sem_in.at[1]),
                pltpu.make_async_copy(xr_ref, xe.at[BLK + ROWS :], sem_in.at[2]),
            ]
            for copy in copies:
                copy.start()
            for copy in copies:
                copy.wait()

        saves = [pltpu.make_async_copy(xe.at[BLK : BLK + ROWS], xs_ref.at[slot], sem_out.at[0])]
        saves[0].start()
        for lo in range(0, EXT, BLK):
            rows = xe[lo : lo + BLK].astype(F32)
            scale = lax.rsqrt(jnp.mean(rows * rows, axis=-1, keepdims=True) + EPS)
            normed[lo : lo + BLK] = (rows * scale).astype(BF16)
        lane = lax.broadcasted_iota(jnp.int32, (ROWS, 128), 1)
        r_all = jnp.zeros((ROWS, 128), F32)
        inv_all = jnp.zeros((ROWS, 128), F32)
        mask = mask_ref[slot]

        def project(pair):
            col = pair * 256
            query = dot(normed[BLK : BLK + ROWS], wtile(w_ref, 0, 64, col, 256))
            key = dot(normed[...], wtile(w_ref, 64, 64, col, 256))
            value = dot(normed[...], wtile(w_ref, 128, 64, col, 256))
            return query, key, value

        current = project(0)
        for pair in range(4):
            following = project(pair + 1) if pair < 3 else None
            for half in range(2):
                head = pair * 2 + half
                cols = slice(half * HDIM, (half + 1) * HDIM)
                at = slice(head * HDIM, (head + 1) * HDIM)
                query, key, value = (part[:, cols] for part in current)
                rq = lax.rsqrt(jnp.mean(query * query, axis=-1, keepdims=True) + EPS)
                rk = lax.rsqrt(jnp.mean(key * key, axis=-1, keepdims=True) + EPS)
                query = (query * rq).astype(BF16)
                key = (key * rk).astype(BF16)
                value = value.astype(BF16)
                probs = jnp.exp(dot(query, key, NT) * SCALE) * mask
                inv = 1.0 / jnp.sum(probs, axis=-1, keepdims=True)
                attended = dot(probs.astype(BF16), value) * inv
                qa[:, at] = query
                qa[:, WIDTH + head * HDIM : WIDTH + (head + 1) * HDIM] = attended.astype(BF16)
                kv[:, at] = key
                kv[:, WIDTH + head * HDIM : WIDTH + (head + 1) * HDIM] = value
                high = inv.astype(BF16).astype(F32)
                r_all = jnp.where(lane == head, rq, r_all)
                r_all = jnp.where(lane == HEADS + head, rk[BLK : BLK + ROWS], r_all)
                inv_all = jnp.where(lane == head, high, inv_all)
                inv_all = jnp.where(lane == HEADS + head, inv - high, inv_all)
            current = following
        qa[:, 2 * WIDTH :] = inv_all.astype(BF16)
        rr[...] = r_all
        for index, (source, target) in enumerate(((qa, qa_ref), (kv, kv_ref), (rr, rr_ref))):
            copy = pltpu.make_async_copy(source, target.at[slot], sem_out.at[1 + index])
            copy.start()
            saves.append(copy)
        for tile in range(8):
            col = tile * 256
            update = dot(
                qa[:, WIDTH : 2 * WIDTH],
                wtile(w_ref, 192 + 32 * (tile // 4), 32, col % 1024, 256),
            )
            result[:, col : col + 256] = (
                xe[BLK : BLK + ROWS, col : col + 256].astype(F32) + update
            ).astype(BF16)
        for index, (source, target) in enumerate(
            (
                (result, next_ref),
                (result.at[:BLK], left_ref),
                (result.at[ROWS - BLK :], right_ref),
                (result, out_ref.at[slot]),
            )
        ):
            copy = pltpu.make_async_copy(source, target, sem_out.at[4 + index])
            copy.start()
            saves.append(copy)
        for copy in saves:
            copy.wait()


def spaces(*names):
    table = dict(s=pltpu.SMEM, v=pltpu.VMEM, a=pl.ANY)
    return [pl.BlockSpec(memory_space=table[n]) for n in names]


def shape_of(a):
    return jax.ShapeDtypeStruct(a.shape, a.dtype)


def forward_call(flags, x0, x, xl, xr, mask, w, saved):
    rows = jax.ShapeDtypeStruct((ROWS, D), BF16)
    edge = jax.ShapeDtypeStruct((BLK, D), BF16)
    outs = pl.pallas_call(
        forward_body,
        name="forward_layer",
        out_shape=(rows, edge, edge) + tuple(shape_of(a) for a in saved),
        in_specs=spaces("s", "a", "a", "a", "a", "v", "v", "a", "a", "a", "a", "a"),
        out_specs=spaces(*"aaaaaaaa"),
        scratch_shapes=[
            pltpu.VMEM((EXT, D), BF16),
            pltpu.VMEM((EXT, D), BF16),
            pltpu.VMEM((ROWS, PACK), BF16),
            pltpu.VMEM((EXT, 2 * WIDTH), BF16),
            pltpu.VMEM((ROWS, 128), F32),
            pltpu.VMEM((ROWS, D), BF16),
            pltpu.SemaphoreType.DMA((3,)),
            pltpu.SemaphoreType.DMA((8,)),
        ],
        input_output_aliases={7: 3, 8: 4, 9: 5, 10: 6, 11: 7},
        compiler_params=pltpu.CompilerParams(vmem_limit_bytes=VMEM_LIMIT),
    )(flags, x0, x, xl, xr, mask, w, *saved)
    return outs[:3], outs[3:]

def load_body(g_ref, w_ref, sem):
    copy = pltpu.make_async_copy(g_ref, w_ref, sem)
    copy.start()
    copy.wait()


def load_call(g):
    return pl.pallas_call(
        load_body,
        name="load_weights",
        out_shape=pltpu.VMEM(g.shape, g.dtype),
        in_specs=spaces("a"),
        out_specs=pl.BlockSpec(memory_space=pltpu.VMEM),
        scratch_shapes=[pltpu.SemaphoreType.DMA],
        compiler_params=pltpu.CompilerParams(vmem_limit_bytes=20 << 20),
    )(g)


def backward_body(
    flags,
    c0_ref,
    g_ref,
    gl_ref,
    gr_ref,
    mask_ref,
    w_ref,
    xs_ref,
    qa_ref,
    qal_ref,
    qar_ref,
    kv_ref,
    rr_ref,
    grad_in,
    next_ref,
    left_ref,
    right_ref,
    grad_ref,
    ge,
    xs,
    qa,
    kv,
    rr,
    dz,
    dn,
    result,
    sem_in,
    sem_save,
    sem_out,
):
    active, slot, last = flags[0], flags[1], flags[2]
    own = slice(BLK, BLK + ROWS)

    @pl.when(active == 1)
    def _():
        loads = [
            pltpu.make_async_copy(source.at[slot], target, sem_save.at[index])
            for index, (source, target) in enumerate(
                (
                    (qal_ref, qa.at[:BLK]),
                    (qa_ref, qa.at[own]),
                    (qar_ref, qa.at[BLK + ROWS :]),
                    (kv_ref, kv),
                    (rr_ref, rr),
                    (xs_ref, xs),
                )
            )
        ]

        @pl.when(last == 1)
        def _():
            copy = pltpu.make_async_copy(c0_ref.at[slot], ge, sem_in.at[0])
            copy.start()
            for load in loads:
                load.start()
            copy.wait()

        @pl.when(last == 0)
        def _():
            copies = [
                pltpu.make_async_copy(gl_ref, ge.at[:BLK], sem_in.at[0]),
                pltpu.make_async_copy(g_ref, ge.at[own], sem_in.at[1]),
                pltpu.make_async_copy(gr_ref, ge.at[BLK + ROWS :], sem_in.at[2]),
            ]
            for copy in copies:
                copy.start()
            for load in loads:
                load.start()
            for copy in copies:
                copy.wait()

        for load in loads:
            load.wait()
        mask = mask_ref[slot]

        def spread(pair):
            low = w_ref[8 * pair : 8 * pair + 8, 192:224, :].reshape(256, 1024)
            high = w_ref[8 * pair : 8 * pair + 8, 224:256, :].reshape(256, 1024)
            return dot(ge[:, :1024], low, NT) + dot(ge[:, 1024:], high, NT)

        current = spread(0)
        for pair in range(4):
            following = spread(pair + 1) if pair < 3 else None
            for half in range(2):
                head = pair * 2 + half
                at = slice(head * HDIM, (head + 1) * HDIM)
                beyond = slice(WIDTH + head * HDIM, WIDTH + (head + 1) * HDIM)
                d_att = current[:, half * HDIM : (half + 1) * HDIM]
                d_att = d_att.astype(BF16).astype(F32)
                query, key, value = qa[:, at], kv[:, at], kv[:, beyond]
                col = 2 * WIDTH + head
                inv = qa[:, col : col + 1].astype(F32) + qa[
                    :, col + HEADS : col + HEADS + 1
                ].astype(F32)
                d_sum = (d_att * inv).astype(BF16)
                d_total = -inv * jnp.sum(
                    d_att * qa[:, beyond].astype(F32), axis=-1, keepdims=True
                )
                probs = jnp.exp(dot(query, key, NT) * SCALE) * mask
                d_probs = dot(d_sum, value, NT)
                d_scores = (probs * (d_probs + d_total) * SCALE).astype(BF16)
                d_value = dot(probs.astype(BF16), d_sum, TN)[own]
                d_key = dot(d_scores, query, TN)[own]
                d_query = dot(d_scores[own], key)

                def unnorm(grad, unit, r):
                    grad = grad.astype(BF16).astype(F32)
                    unit = unit.astype(F32)
                    return r * (grad - unit * jnp.mean(grad * unit, axis=-1, keepdims=True))

                dz[:, at] = unnorm(d_query, query[own], rr[:, head : head + 1]).astype(BF16)
                dz[:, beyond] = unnorm(
                    d_key, key[own], rr[:, HEADS + head : HEADS + head + 1]
                ).astype(BF16)
                dz[:, 2 * WIDTH + head * HDIM : 2 * WIDTH + (head + 1) * HDIM] = d_value.astype(BF16)
            current = following
        x = xs[...].astype(F32)
        scale = lax.rsqrt(jnp.mean(x * x, axis=-1, keepdims=True) + EPS)
        inner = jnp.zeros((ROWS, 1), F32)
        for tile in range(8):
            grad = jnp.zeros((ROWS, 256), F32)
            for part in range(3):
                weight = w_ref[4 * tile : 4 * tile + 4, 64 * part : 64 * part + 64, :]
                grad += dot(
                    dz[:, part * WIDTH : (part + 1) * WIDTH], weight.reshape(256, WIDTH), NT
                )
            cols = slice(tile * 256, (tile + 1) * 256)
            grad = grad.astype(BF16).astype(F32)
            dn[:, cols] = grad
            inner += jnp.sum(grad * xs[:, cols].astype(F32), axis=-1, keepdims=True)
        inner = inner * scale * scale * (1.0 / D)
        for tile in range(8):
            cols = slice(tile * 256, (tile + 1) * 256)
            value = dn[:, cols] - xs[:, cols].astype(F32) * inner
            result[:, cols] = (ge[own, cols].astype(F32) + scale * value).astype(BF16)
        saves = [
            pltpu.make_async_copy(source, target, sem_out.at[index])
            for index, (source, target) in enumerate(
                (
                    (result, next_ref),
                    (result.at[:BLK], left_ref),
                    (result.at[ROWS - BLK :], right_ref),
                    (result, grad_ref.at[slot]),
                )
            )
        ]
        for copy in saves:
            copy.start()
        for copy in saves:
            copy.wait()


def backward_call(flags, c0, g, gl, gr, mask, w, xs, qa, qal, qar, kv, rr, grads):
    rows = jax.ShapeDtypeStruct((ROWS, D), BF16)
    edge = jax.ShapeDtypeStruct((BLK, D), BF16)
    outs = pl.pallas_call(
        backward_body,
        name="backward_layer",
        out_shape=(rows, edge, edge, shape_of(grads)),
        in_specs=spaces(*"saaaavvaaaaaaa"),
        out_specs=spaces(*"aaaa"),
        scratch_shapes=[
            pltpu.VMEM((EXT, D), BF16),
            pltpu.VMEM((ROWS, D), BF16),
            pltpu.VMEM((EXT, PACK), BF16),
            pltpu.VMEM((EXT, 2 * WIDTH), BF16),
            pltpu.VMEM((ROWS, 128), F32),
            pltpu.VMEM((ROWS, 3 * WIDTH), BF16),
            pltpu.VMEM((ROWS, D), F32),
            pltpu.VMEM((ROWS, D), BF16),
            pltpu.SemaphoreType.DMA((3,)),
            pltpu.SemaphoreType.DMA((6,)),
            pltpu.SemaphoreType.DMA((4,)),
        ],
        input_output_aliases={13: 3},
        compiler_params=pltpu.CompilerParams(vmem_limit_bytes=VMEM_LIMIT),
    )(flags, c0, g, gl, gr, mask, w, xs, qa, qal, qar, kv, rr, grads)
    return outs[:3], outs[3]


BOTH = ("section", "ctx")


def neighbours(n_ctx, distance):
    return [(c, c + distance) for c in range(n_ctx) if 0 <= c + distance < n_ctx]


def hop(sections, step, n_ctx, distance):
    return [
        (s * n_ctx + source, (s + step) * n_ctx + target)
        for s in sections
        for source, target in neighbours(n_ctx, distance)
    ]


def relay(parts, sections, step, n_ctx):
    rows, left, right = parts
    rows = lax.ppermute(rows, BOTH, hop(sections, step, n_ctx, 0))
    from_left = lax.ppermute(right, BOTH, hop(sections, step, n_ctx, 1))
    from_right = lax.ppermute(left, BOTH, hop(sections, step, n_ctx, -1))
    return rows, from_left, from_right


def edges(block, dim, width, n_ctx):
    size = block.shape[dim]
    tail = lax.slice_in_dim(block, size - width, size, axis=dim)
    head = lax.slice_in_dim(block, 0, width, axis=dim)
    from_left = lax.ppermute(tail, "ctx", neighbours(n_ctx, 1))
    from_right = lax.ppermute(head, "ctx", neighbours(n_ctx, -1))
    return from_left, from_right


def key_weights(block_mask, place, n_ctx):
    block_ids = place * BLOCKS_DEV + jnp.arange(BLOCKS_DEV)
    mask = block_mask.astype(F32)
    left = mask[:, :, 0] * (block_ids > 0).astype(F32)
    right = mask[:, :, 1] * (block_ids < BLOCKS_DEV * n_ctx - 1).astype(F32)
    allow = jnp.stack([left, jnp.ones_like(left), right], axis=2)
    before, after = edges(allow, 1, 1, n_ctx)
    allow = jnp.concatenate([before, allow, after], axis=1)
    allow = jnp.repeat(allow, BLK, axis=1)
    block = jnp.arange(EXT) // BLK
    offset = block[None, :] - block[:, None] + 1
    return sum(
        jnp.where(offset == side, allow[:, :, side : side + 1], 0.0) for side in range(3)
    )


def per_device(section_input, cotangent, w_query, w_key, w_value, w_out, block_mask):
    n_section = lax.axis_size("section")
    n_ctx = lax.axis_size("ctx")
    section = lax.axis_index("section")
    place = lax.axis_index("ctx")
    micro = section_input.shape[0]
    steps = n_section + micro - 1

    shard = jnp.concatenate(
        [w_query[0], w_key[0], w_value[0], w_out[0][:, :WIDTH], w_out[0][:, WIDTH:]], axis=0
    )
    gathered = lax.all_gather(shard, "ctx", axis=0, tiled=False)
    before, after = edges(jnp.stack([section_input, cotangent]), 2, BLK, n_ctx)
    extended = jnp.concatenate(
        [before, jnp.stack([section_input, cotangent]), after], axis=2
    )
    mask = key_weights(block_mask, place, n_ctx)
    weights = load_call(gathered)

    def plan(step, position):
        micro_id = step - position
        active = (micro_id >= 0) & (micro_id < micro)
        return jnp.stack(
            [active, jnp.clip(micro_id, 0, micro - 1), position == 0]
        ).astype(jnp.int32)

    saved = (
        jnp.zeros((micro, ROWS, D), BF16),
        jnp.zeros((micro, ROWS, D), BF16),
        jnp.zeros((micro, ROWS, PACK), BF16),
        jnp.zeros((micro, EXT, 2 * WIDTH), BF16),
        jnp.zeros((micro, ROWS, 128), F32),
    )
    zero_rows = jnp.zeros((ROWS, D), BF16)
    zero_edge = jnp.zeros((BLK, D), BF16)
    incoming = (zero_rows, zero_edge, zero_edge)
    forward_mask = mask[:, BLK : BLK + ROWS]
    for step in range(steps):
        parts, saved = forward_call(
            plan(step, section), extended[0], *incoming, forward_mask, weights, saved
        )
        senders = [s for s in range(step - micro + 1, step + 1) if 0 <= s < n_section - 1]
        if senders:
            incoming = relay(parts, senders, 1, n_ctx)
    xs, outputs, qa, kv, rr = saved
    qa_left, qa_right = edges(qa, 1, BLK, n_ctx)
    grads = jnp.zeros((micro, ROWS, D), BF16)
    incoming = (zero_rows, zero_edge, zero_edge)
    for step in range(steps):
        parts, grads = backward_call(
            plan(step, n_section - 1 - section),
            extended[1],
            *incoming,
            mask,
            weights,
            xs,
            qa,
            qa_left,
            qa_right,
            kv,
            rr,
            grads,
        )
        top = n_section - 1 - step
        senders = [s for s in range(top, top + micro) if 0 < s < n_section]
        if senders:
            incoming = relay(parts, senders, -1, n_ctx)
    return (outputs[None], grads[None])


def solution(mesh):
    return jax.shard_map(
        per_device,
        mesh=mesh,
        in_specs=(
            P(None, "ctx", None),
            P(None, "ctx", None),
            P("section", "ctx", None),
            P("section", "ctx", None),
            P("section", "ctx", None),
            P("section", "ctx", None),
            P(None, "ctx", None),
        ),
        out_specs=(P("section", None, "ctx", None), P("section", None, "ctx", None)),
        check_vma=False,
    )
```

time: 1320 us -> 976 us (0.74)
  waiting for transfers between devices: 720 us -> 135 us
  local copies, waits for them, and re-layouts: 75.9 us -> 279 us
  starting transfers between devices: 348 us -> 443 us
  Pallas kernels: 0 us -> 85.7 us
  other arithmetic: 89.5 us -> 4.29 us
  matrix products: 59.4 us -> 0 us
    ppermute x72 -> x54, waiting for transfers between devices: 391 us -> 42.8 us  [the longest x3 12.8 us: edges(): from_left = lax.ppermute(tail, 'ctx', neighbours(n_ctx, 1))]
    unnamed x1 -> x408, local copies, waits for them, and re-layouts: 0.77 us -> 272 us
    all_gather x4 -> x1, waiting for transfers between devices: 327 us -> 92.5 us  [per_device(): gathered = lax.all_gather(shard, 'ctx', axis=0, tiled=False)]
    ppermute x72 -> x54, starting transfers between devices: 348 us -> 443 us  [the longest x16 342 us: relay(): rows = lax.ppermute(rows, BOTH, hop(sections, step, n_ctx, 0))]
    pallas_call x0 -> x19, Pallas kernels: none -> 85.7 us  [the longest x9 47.3 us: backward_call(): pl.pallas_call(backward_body, name='backward_layer', out_shape=(rows, edg...]
    select_n x47 -> x1, other arithmetic: 83.2 us -> 0.01 us  [key_weights(): block = jnp.arange(EXT) // BLK]
    dot_general x36 -> x0, matrix products: 59.4 us -> none  [the longest x12 36.3 us: head_normed(): out = jnp.dot(normed, weight, preferred_element_type=jnp.float32)]
    cond x122 -> x0, local copies, waits for them, and re-layouts: 15.4 us -> none
  transfers between devices with their start and end apart: 76 -> 55, of which waited for: 58 -> 13; matrix products, arithmetic and copies ran while one was open for 4% -> 1% of each run, Pallas kernels for 0% -> 0%
where the time goes in v1:
time: 976 us; the launch traced here: 963 us
  starting transfers between devices  443 us (45%)
  local copies, waits for them, and re-layouts  279 us (29%)
  waiting for transfers between devices  135 us (14%)
  Pallas kernels  85.7 us (9%)
  between operations  15.4 us (2%)
    ppermute x16, starting transfers between devices, relay(): rows = lax.ppermute(rows, BOTH, hop(sections, step, n_ctx, 0))  342 us
    unnamed x408, local copies, waits for them, and re-layouts  272 us
    all_gather x1, waiting for transfers between devices, per_device(): gathered = lax.all_gather(shard, 'ctx', axis=0, tiled=False)  92.5 us
    pallas_call x9, Pallas kernels, backward_call(): pl.pallas_call(backward_body, name='backward_layer', out_shape=(rows, edg...  47.3 us
    pallas_call x9, Pallas kernels, forward_call(): pl.pallas_call(forward_body, name='forward_layer', out_shape=(rows, edge,...  37.2 us
    ppermute x16, starting transfers between devices, relay(): from_left = lax.ppermute(right, BOTH, hop(sections, step, n_ctx, 1))  31.4 us
    ppermute x16, starting transfers between devices, relay(): from_right = lax.ppermute(left, BOTH, hop(sections, step, n_ctx, -1))  31 us
    ppermute x3, starting transfers between devices, edges(): from_left = lax.ppermute(tail, 'ctx', neighbours(n_ctx, 1))  19.7 us
  transfers between devices with their start and end apart: 55, of which 13 were waited for; matrix products, arithmetic and copies ran while one was open for 1% of the time, Pallas kernels for 0%

profile of v1, /device:TPU:100, one launch (start us, length us, event | category | flops | bytes accessed | tf_op | source)
XLA Modules:
  0.0 963.2 jit_solution(18276656963972824531)
XLA Ops:
  12.7 13.4 %collective-permute-start.2 = (f32[2,1,3]{1,2,0:T(4,128)S(1)}, f32[2,1,3]{1,2,0:T(4,128)S(1)}, u32[]{:S(2)}, u32[]{:S(2)}) collective-permute-start(f32[2,1,3]{1,2,0:T(4,128)S(1)} %get-tuple-element.215), channel_id=1, source_target_pairs={{0,1},{1,2},{2,3},{3,4},{4,5},{5,6},{6,7},{7,8},{8,9},{9,10},{10,1... | collective-permute-start | bytes 80 | tf_op jit(solution)/shard_map/ppermute | solution.py:422
  26.2 13.1 %collective-permute-start.3 = (f32[2,1,3]{1,2,0:T(4,128)S(1)}, f32[2,1,3]{1,2,0:T(4,128)S(1)}, u32[]{:S(2)}, u32[]{:S(2)}) collective-permute-start(f32[2,1,3]{1,2,0:T(4,128)S(1)} %get-tuple-element.216), channel_id=1, source_target_pairs={{1,0},{2,1},{3,2},{4,3},{5,4},{6,5},{7,6},{8,7},{9,8},{10,9},{11,1... | collective-permute-start | bytes 80 | tf_op jit(solution)/shard_map/ppermute | solution.py:423
  49.6 8.0 collective-permute-done
  63.9 92.5 %all-gather.3.cloned.1.call-done = bf16[8192,1024]{1,0:T(8,128)(2,1)} async-done(((bf16[256,1024]{1,0:T(8,128)(2,1)}), bf16[8192,1024]{1,0:T(8,128)(2,1)}) %all-gather.3.cloned.1.call-update) | async-done | bytes 16777232 | tf_op jit(solution)/shard_map/all_gather | solution.py:454
  210.0 11.0 %collective-permute-start.7 = (bf16[128,2048]{1,0:T(8,128)(2,1)}, bf16[128,2048]{1,0:T(8,128)(2,1)S(1)}, u32[]{:S(2)}, u32[]{:S(2)}) collective-permute-start(bf16[128,2048]{1,0:T(8,128)(2,1)} %get-tuple-element.112), channel_id=1, source_target_pairs={{0,32},{1,33},{2,34},{3,35},{4,36},{5,37},{6,38},{7,39},{8,40},{9,... | collective-permute-start | bytes 1572872 | tf_op jit(solution)/shard_map/ppermute | solution.py:412
  239.3 7.6 forward_layer.11
  249.8 14.3 %collective-permute-start.10 = (bf16[128,2048]{1,0:T(8,128)(2,1)}, bf16[128,2048]{1,0:T(8,128)(2,1)S(1)}, u32[]{:S(2)}, u32[]{:S(2)}) collective-permute-start(bf16[128,2048]{1,0:T(8,128)(2,1)} %get-tuple-element.120), channel_id=1, source_target_pairs={{32,64},{33,65},{34,66},{35,67},{36,68},{37,69},{38,70},{39,71},{4... | collective-permute-start | bytes 1572872 | tf_op jit(solution)/shard_map/ppermute | solution.py:412
  279.6 27.3 %collective-permute-start.13 = (bf16[128,2048]{1,0:T(8,128)(2,1)}, bf16[128,2048]{1,0:T(8,128)(2,1)S(1)}, u32[]{:S(2)}, u32[]{:S(2)}) collective-permute-start(bf16[128,2048]{1,0:T(8,128)(2,1)} %get-tuple-element.128), channel_id=1, source_target_pairs={{64,96},{65,97},{66,98},{67,99},{68,100},{69,101},{70,102},{71,103... | collective-permute-start | bytes 1572872 | tf_op jit(solution)/shard_map/ppermute | solution.py:412
  322.4 27.3 %collective-permute-start.16 = (bf16[128,2048]{1,0:T(8,128)(2,1)}, bf16[128,2048]{1,0:T(8,128)(2,1)S(1)}, u32[]{:S(2)}, u32[]{:S(2)}) collective-permute-start(bf16[128,2048]{1,0:T(8,128)(2,1)} %get-tuple-element.136), channel_id=1, source_target_pairs={{96,128},{97,129},{98,130},{99,131},{100,132},{101,133},{102,134},... | collective-permute-start | bytes 1572872 | tf_op jit(solution)/shard_map/ppermute | solution.py:412
  361.7 7.8 forward_layer.14
  372.4 23.6 %collective-permute-start.19 = (bf16[128,2048]{1,0:T(8,128)(2,1)}, bf16[128,2048]{1,0:T(8,128)(2,1)S(1)}, u32[]{:S(2)}, u32[]{:S(2)}) collective-permute-start(bf16[128,2048]{1,0:T(8,128)(2,1)} %get-tuple-element.144), channel_id=1, source_target_pairs={{128,160},{129,161},{130,162},{131,163},{132,164},{133,165},{134,1... | collective-permute-start | bytes 1572872 | tf_op jit(solution)/shard_map/ppermute | solution.py:412
  411.5 28.6 %collective-permute-start.22 = (bf16[128,2048]{1,0:T(8,128)(2,1)}, bf16[128,2048]{1,0:T(8,128)(2,1)S(1)}, u32[]{:S(2)}, u32[]{:S(2)}) collective-permute-start(bf16[128,2048]{1,0:T(8,128)(2,1)} %get-tuple-element.152), channel_id=1, source_target_pairs={{160,192},{161,193},{162,194},{163,195},{164,196},{165,197},{166,1... | collective-permute-start | bytes 1572872 | tf_op jit(solution)/shard_map/ppermute | solution.py:412
  468.4 6.7 forward_layer.17
  532.4 7.0 backward_layer.10
  541.5 57.4 %collective-permute-start.33 = (bf16[128,2048]{1,0:T(8,128)(2,1)}, bf16[128,2048]{1,0:T(8,128)(2,1)S(1)}, u32[]{:S(2)}, u32[]{:S(2)}) collective-permute-start(bf16[128,2048]{1,0:T(8,128)(2,1)} %copy-done.181), channel_id=1, source_target_pairs={{192,160},{193,161},{194,162},{195,163},{196,164},{197,165},{198,1... | collective-permute-start | bytes 1572872 | tf_op jit(solution)/shard_map/ppermute | solution.py:412
  598.9 12.9 %collective-permute-start.34 = (bf16[32,2048]{1,0:T(8,128)(2,1)}, bf16[32,2048]{1,0:T(8,128)(2,1)S(1)}, u32[]{:S(2)}, u32[]{:S(2)}) collective-permute-start(bf16[32,2048]{1,0:T(8,128)(2,1)} %copy-done.195), channel_id=1, source_target_pairs={{192,161},{193,162},{194,163},{195,164},{196,165},{197,166},{198,1... | collective-permute-start | bytes 393224 | tf_op jit(solution)/shard_map/ppermute | solution.py:413
  611.8 12.9 %collective-permute-start.35 = (bf16[32,2048]{1,0:T(8,128)(2,1)}, bf16[32,2048]{1,0:T(8,128)(2,1)S(1)}, u32[]{:S(2)}, u32[]{:S(2)}) collective-permute-start(bf16[32,2048]{1,0:T(8,128)(2,1)} %copy-done.188), channel_id=1, source_target_pairs={{193,160},{194,161},{195,162},{196,163},{197,164},{198,165},{199,1... | collective-permute-start | bytes 393224 | tf_op jit(solution)/shard_map/ppermute | solution.py:414
  644.1 28.8 %collective-permute-start.36 = (bf16[128,2048]{1,0:T(8,128)(2,1)}, bf16[128,2048]{1,0:T(8,128)(2,1)S(1)}, u32[]{:S(2)}, u32[]{:S(2)}) collective-permute-start(bf16[128,2048]{1,0:T(8,128)(2,1)} %copy-done.177), channel_id=1, source_target_pairs={{160,128},{161,129},{162,130},{163,131},{164,132},{165,133},{166,1... | collective-permute-start | bytes 1572872 | tf_op jit(solution)/shard_map/ppermute | solution.py:412
  699.7 28.4 %collective-permute-start.39 = (bf16[128,2048]{1,0:T(8,128)(2,1)}, bf16[128,2048]{1,0:T(8,128)(2,1)S(1)}, u32[]{:S(2)}, u32[]{:S(2)}) collective-permute-start(bf16[128,2048]{1,0:T(8,128)(2,1)} %copy-done.178), channel_id=1, source_target_pairs={{128,96},{129,97},{130,98},{131,99},{132,100},{133,101},{134,102},... | collective-permute-start | bytes 1572872 | tf_op jit(solution)/shard_map/ppermute | solution.py:412
  749.0 33.1 %collective-permute-start.42 = (bf16[128,2048]{1,0:T(8,128)(2,1)}, bf16[128,2048]{1,0:T(8,128)(2,1)S(1)}, u32[]{:S(2)}, u32[]{:S(2)}) collective-permute-start(bf16[128,2048]{1,0:T(8,128)(2,1)} %copy-done.179), channel_id=1, source_target_pairs={{96,64},{97,65},{98,66},{99,67},{100,68},{101,69},{102,70},{103,71... | collective-permute-start | bytes 1572872 | tf_op jit(solution)/shard_map/ppermute | solution.py:412
  809.0 27.0 %collective-permute-start.45 = (bf16[128,2048]{1,0:T(8,128)(2,1)}, bf16[128,2048]{1,0:T(8,128)(2,1)S(1)}, u32[]{:S(2)}, u32[]{:S(2)}) collective-permute-start(bf16[128,2048]{1,0:T(8,128)(2,1)} %copy-done.180), channel_id=1, source_target_pairs={{64,32},{65,33},{66,34},{67,35},{68,36},{69,37},{70,38},{71,39},{7... | collective-permute-start | bytes 1572872 | tf_op jit(solution)/shard_map/ppermute | solution.py:412
  856.8 31.5 %collective-permute-start.48 = (bf16[128,2048]{1,0:T(8,128)(2,1)}, bf16[128,2048]{1,0:T(8,128)(2,1)}, u32[]{:S(2)}, u32[]{:S(2)}) collective-permute-start(bf16[128,2048]{1,0:T(8,128)(2,1)} %copy-done.183), channel_id=1, source_target_pairs={{32,0},{33,1},{34,2},{35,3},{36,4},{37,5},{38,6},{39,7},{40,8},{41... | collective-permute-start | bytes 1572872 | tf_op jit(solution)/shard_map/ppermute | solution.py:412
  908.3 12.5 %backward_layer.16 = (bf16[128,2048]{1,0:T(8,128)(2,1)}, bf16[32,2048]{1,0:T(8,128)(2,1)}, bf16[32,2048]{1,0:T(8,128)(2,1)}, bf16[2,128,2048]{2,1,0:T(8,128)(2,1)}) custom-call(s32[3]{0:T(128)S(1)} %add_add_fusion.10.flags, bf16[2,192,2048]{2,1,0:T(8,128)(2,1)S(1)} %copy-done.84, ...), custom_call_target="tpu_custom_call", output_to_operand_aliasing={{3}: (13, {})} | custom-call | tf_op jit(solution)/shard_map/backward_layer/pallas_call | solution.py:370
  944.3 11.8 %backward_layer.17 = (bf16[128,2048]{1,0:T(8,128)(2,1)}, bf16[32,2048]{1,0:T(8,128)(2,1)}, bf16[32,2048]{1,0:T(8,128)(2,1)}, bf16[2,128,2048]{2,1,0:T(8,128)(2,1)}) custom-call(s32[3]{0:T(128)S(1)} %add_add_fusion.9.flags, bf16[2,192,2048]{2,1,0:T(8,128)(2,1)S(1)} %copy-done.85, ...), custom_call_target="tpu_custom_call", output_to_operand_aliasing={{3}: (13, {})} | custom-call | tf_op jit(solution)/shard_map/backward_layer/pallas_call | solution.py:370
  (560 shorter events, 403.2 us)
Async XLA Ops:
  7.2 149.2 %all-gather.3.cloned.1.call-start = ((), (), s32[]{:S(2)}) async-start(), calls=%async_computation | async-start | bytes 17301504 | tf_op jit(solution)/shard_map/all_gather | solution.py:454
  12.7 34.9 %collective-permute-start.2 = (f32[2,1,3]{1,2,0:T(4,128)S(1)}, f32[2,1,3]{1,2,0:T(4,128)S(1)}, u32[]{:S(2)}, u32[]{:S(2)}) collective-permute-start(f32[2,1,3]{1,2,0:T(4,128)S(1)} %get-tuple-element.215), channel_id=1, source_target_pairs={{0,1},{1,2},{2,3},{3,4},{4,5},{5,6},{6,7},{7,8},{8,9},{9,10},{10,1... | collective-permute-start | bytes 80 | tf_op jit(solution)/shard_map/ppermute | solution.py:422
  26.2 21.4 %collective-permute-start.3 = (f32[2,1,3]{1,2,0:T(4,128)S(1)}, f32[2,1,3]{1,2,0:T(4,128)S(1)}, u32[]{:S(2)}, u32[]{:S(2)}) collective-permute-start(f32[2,1,3]{1,2,0:T(4,128)S(1)} %get-tuple-element.216), channel_id=1, source_target_pairs={{1,0},{2,1},{3,2},{4,3},{5,4},{6,5},{7,6},{8,7},{9,8},{10,9},{11,1... | collective-permute-start | bytes 80 | tf_op jit(solution)/shard_map/ppermute | solution.py:423
  41.5 16.1 %collective-permute-start = (bf16[2,2,32,2048]{3,2,1,0:T(8,128)(2,1)}, bf16[2,2,32,2048]{3,2,1,0:T(8,128)(2,1)S(1)}, u32[]{:S(2)}, u32[]{:S(2)}) collective-permute-start(bf16[2,2,32,2048]{3,2,1,0:T(8,128)(2,1)} %get-tuple-element.208), channel_id=1, source_target_pairs={{0,1},{1,2},{2,3},{3,4},{4,5},{5,6},{6,7},{7,8},{8,9},{9,10},{10,1... | collective-permute-start | bytes 1572872 | tf_op jit(solution)/shard_map/ppermute | solution.py:422
  44.6 16.9 %collective-permute-start.1 = (bf16[2,2,32,2048]{3,2,1,0:T(8,128)(2,1)}, bf16[2,2,32,2048]{3,2,1,0:T(8,128)(2,1)S(1)}, u32[]{:S(2)}, u32[]{:S(2)}) collective-permute-start(bf16[2,2,32,2048]{3,2,1,0:T(8,128)(2,1)} %get-tuple-element.209), channel_id=1, source_target_pairs={{1,0},{2,1},{3,2},{4,3},{5,4},{6,5},{7,6},{8,7},{9,8},{10,9},{11,1... | collective-permute-start | bytes 1572872 | tf_op jit(solution)/shard_map/ppermute | solution.py:423
  210.0 20.0 %collective-permute-start.7 = (bf16[128,2048]{1,0:T(8,128)(2,1)}, bf16[128,2048]{1,0:T(8,128)(2,1)S(1)}, u32[]{:S(2)}, u32[]{:S(2)}) collective-permute-start(bf16[128,2048]{1,0:T(8,128)(2,1)} %get-tuple-element.112), channel_id=1, source_target_pairs={{0,32},{1,33},{2,34},{3,35},{4,36},{5,37},{6,38},{7,39},{8,40},{9,... | collective-permute-start | bytes 1572872 | tf_op jit(solution)/shard_map/ppermute | solution.py:412
  249.8 17.0 %collective-permute-start.10 = (bf16[128,2048]{1,0:T(8,128)(2,1)}, bf16[128,2048]{1,0:T(8,128)(2,1)S(1)}, u32[]{:S(2)}, u32[]{:S(2)}) collective-permute-start(bf16[128,2048]{1,0:T(8,128)(2,1)} %get-tuple-element.120), channel_id=1, source_target_pairs={{32,64},{33,65},{34,66},{35,67},{36,68},{37,69},{38,70},{39,71},{4... | collective-permute-start | bytes 1572872 | tf_op jit(solution)/shard_map/ppermute | solution.py:412
  279.6 30.0 %collective-permute-start.13 = (bf16[128,2048]{1,0:T(8,128)(2,1)}, bf16[128,2048]{1,0:T(8,128)(2,1)S(1)}, u32[]{:S(2)}, u32[]{:S(2)}) collective-permute-start(bf16[128,2048]{1,0:T(8,128)(2,1)} %get-tuple-element.128), channel_id=1, source_target_pairs={{64,96},{65,97},{66,98},{67,99},{68,100},{69,101},{70,102},{71,103... | collective-permute-start | bytes 1572872 | tf_op jit(solution)/shard_map/ppermute | solution.py:412
  322.4 30.0 %collective-permute-start.16 = (bf16[128,2048]{1,0:T(8,128)(2,1)}, bf16[128,2048]{1,0:T(8,128)(2,1)S(1)}, u32[]{:S(2)}, u32[]{:S(2)}) collective-permute-start(bf16[128,2048]{1,0:T(8,128)(2,1)} %get-tuple-element.136), channel_id=1, source_target_pairs={{96,128},{97,129},{98,130},{99,131},{100,132},{101,133},{102,134},... | collective-permute-start | bytes 1572872 | tf_op jit(solution)/shard_map/ppermute | solution.py:412
  372.4 26.3 %collective-permute-start.19 = (bf16[128,2048]{1,0:T(8,128)(2,1)}, bf16[128,2048]{1,0:T(8,128)(2,1)S(1)}, u32[]{:S(2)}, u32[]{:S(2)}) collective-permute-start(bf16[128,2048]{1,0:T(8,128)(2,1)} %get-tuple-element.144), channel_id=1, source_target_pairs={{128,160},{129,161},{130,162},{131,163},{132,164},{133,165},{134,1... | collective-permute-start | bytes 1572872 | tf_op jit(solution)/shard_map/ppermute | solution.py:412
  411.5 31.3 %collective-permute-start.22 = (bf16[128,2048]{1,0:T(8,128)(2,1)}, bf16[128,2048]{1,0:T(8,128)(2,1)S(1)}, u32[]{:S(2)}, u32[]{:S(2)}) collective-permute-start(bf16[128,2048]{1,0:T(8,128)(2,1)} %get-tuple-element.152), channel_id=1, source_target_pairs={{160,192},{161,193},{162,194},{163,195},{164,196},{165,197},{166,1... | collective-permute-start | bytes 1572872 | tf_op jit(solution)/shard_map/ppermute | solution.py:412
  478.7 10.9 %collective-permute-start.28 = (bf16[2,32,2176]{2,1,0:T(8,128)(2,1)}, bf16[2,32,2176]{2,1,0:T(8,128)(2,1)S(1)}, u32[]{:S(2)}, u32[]{:S(2)}) collective-permute-start(bf16[2,32,2176]{2,1,0:T(8,128)(2,1)} %get-tuple-element.211), channel_id=1, source_target_pairs={{0,1},{1,2},{2,3},{3,4},{4,5},{5,6},{6,7},{7,8},{8,9},{9,10},{10,1... | collective-permute-start | bytes 835592 | tf_op jit(solution)/shard_map/ppermute | solution.py:422
  482.0 11.7 %collective-permute-start.29 = (bf16[2,32,2176]{2,1,0:T(8,128)(2,1)}, bf16[2,32,2176]{2,1,0:T(8,128)(2,1)S(1)}, u32[]{:S(2)}, u32[]{:S(2)}) collective-permute-start(bf16[2,32,2176]{2,1,0:T(8,128)(2,1)} %get-tuple-element.210), channel_id=1, source_target_pairs={{1,0},{2,1},{3,2},{4,3},{5,4},{6,5},{7,6},{8,7},{9,8},{10,9},{11,1... | collective-permute-start | bytes 835592 | tf_op jit(solution)/shard_map/ppermute | solution.py:423
  541.5 84.6 %collective-permute-start.33 = (bf16[128,2048]{1,0:T(8,128)(2,1)}, bf16[128,2048]{1,0:T(8,128)(2,1)S(1)}, u32[]{:S(2)}, u32[]{:S(2)}) collective-permute-start(bf16[128,2048]{1,0:T(8,128)(2,1)} %copy-done.181), channel_id=1, source_target_pairs={{192,160},{193,161},{194,162},{195,163},{196,164},{197,165},{198,1... | collective-permute-start | bytes 1572872 | tf_op jit(solution)/shard_map/ppermute | solution.py:412
  598.9 25.9 %collective-permute-start.34 = (bf16[32,2048]{1,0:T(8,128)(2,1)}, bf16[32,2048]{1,0:T(8,128)(2,1)S(1)}, u32[]{:S(2)}, u32[]{:S(2)}) collective-permute-start(bf16[32,2048]{1,0:T(8,128)(2,1)} %copy-done.195), channel_id=1, source_target_pairs={{192,161},{193,162},{194,163},{195,164},{196,165},{197,166},{198,1... | collective-permute-start | bytes 393224 | tf_op jit(solution)/shard_map/ppermute | solution.py:413
  611.8 13.7 %collective-permute-start.35 = (bf16[32,2048]{1,0:T(8,128)(2,1)}, bf16[32,2048]{1,0:T(8,128)(2,1)S(1)}, u32[]{:S(2)}, u32[]{:S(2)}) collective-permute-start(bf16[32,2048]{1,0:T(8,128)(2,1)} %copy-done.188), channel_id=1, source_target_pairs={{193,160},{194,161},{195,162},{196,163},{197,164},{198,165},{199,1... | collective-permute-start | bytes 393224 | tf_op jit(solution)/shard_map/ppermute | solution.py:414
  644.1 31.6 %collective-permute-start.36 = (bf16[128,2048]{1,0:T(8,128)(2,1)}, bf16[128,2048]{1,0:T(8,128)(2,1)S(1)}, u32[]{:S(2)}, u32[]{:S(2)}) collective-permute-start(bf16[128,2048]{1,0:T(8,128)(2,1)} %copy-done.177), channel_id=1, source_target_pairs={{160,128},{161,129},{162,130},{163,131},{164,132},{165,133},{166,1... | collective-permute-start | bytes 1572872 | tf_op jit(solution)/shard_map/ppermute | solution.py:412
  699.7 31.2 %collective-permute-start.39 = (bf16[128,2048]{1,0:T(8,128)(2,1)}, bf16[128,2048]{1,0:T(8,128)(2,1)S(1)}, u32[]{:S(2)}, u32[]{:S(2)}) collective-permute-start(bf16[128,2048]{1,0:T(8,128)(2,1)} %copy-done.178), channel_id=1, source_target_pairs={{128,96},{129,97},{130,98},{131,99},{132,100},{133,101},{134,102},... | collective-permute-start | bytes 1572872 | tf_op jit(solution)/shard_map/ppermute | solution.py:412
  749.0 35.9 %collective-permute-start.42 = (bf16[128,2048]{1,0:T(8,128)(2,1)}, bf16[128,2048]{1,0:T(8,128)(2,1)S(1)}, u32[]{:S(2)}, u32[]{:S(2)}) collective-permute-start(bf16[128,2048]{1,0:T(8,128)(2,1)} %copy-done.179), channel_id=1, source_target_pairs={{96,64},{97,65},{98,66},{99,67},{100,68},{101,69},{102,70},{103,71... | collective-permute-start | bytes 1572872 | tf_op jit(solution)/shard_map/ppermute | solution.py:412
  809.0 29.7 %collective-permute-start.45 = (bf16[128,2048]{1,0:T(8,128)(2,1)}, bf16[128,2048]{1,0:T(8,128)(2,1)S(1)}, u32[]{:S(2)}, u32[]{:S(2)}) collective-permute-start(bf16[128,2048]{1,0:T(8,128)(2,1)} %copy-done.180), channel_id=1, source_target_pairs={{64,32},{65,33},{66,34},{67,35},{68,36},{69,37},{70,38},{71,39},{7... | collective-permute-start | bytes 1572872 | tf_op jit(solution)/shard_map/ppermute | solution.py:412
  856.8 42.1 %collective-permute-start.48 = (bf16[128,2048]{1,0:T(8,128)(2,1)}, bf16[128,2048]{1,0:T(8,128)(2,1)}, u32[]{:S(2)}, u32[]{:S(2)}) collective-permute-start(bf16[128,2048]{1,0:T(8,128)(2,1)} %copy-done.183), channel_id=1, source_target_pairs={{32,0},{33,1},{34,2},{35,3},{36,4},{37,5},{38,6},{39,7},{40,8},{41... | collective-permute-start | bytes 1572872 | tf_op jit(solution)/shard_map/ppermute | solution.py:412
  889.6 9.3 collective-permute-start.50
  920.7 14.2 %collective-permute-start.51 = (bf16[128,2048]{1,0:T(8,128)(2,1)}, bf16[128,2048]{1,0:T(8,128)(2,1)}, u32[]{:S(2)}, u32[]{:S(2)}) collective-permute-start(bf16[128,2048]{1,0:T(8,128)(2,1)} %get-tuple-element.201), channel_id=1, source_target_pairs={{32,0},{33,1},{34,2},{35,3},{36,4},{37,5},{38,6},{39,7},{40,8},{41... | collective-permute-start | bytes 1572872 | tf_op jit(solution)/shard_map/ppermute | solution.py:412
  923.3 11.6 %collective-permute-start.53 = (bf16[32,2048]{1,0:T(8,128)(2,1)}, bf16[32,2048]{1,0:T(8,128)(2,1)}, u32[]{:S(2)}, u32[]{:S(2)}) collective-permute-start(bf16[32,2048]{1,0:T(8,128)(2,1)} %get-tuple-element.203), channel_id=1, source_target_pairs={{33,0},{34,1},{35,2},{36,3},{37,4},{38,5},{39,6},{40,7},{41,8},{42... | collective-permute-start | bytes 393224 | tf_op jit(solution)/shard_map/ppermute | solution.py:414
  (233 other events, 828.9 us)
Sparse Core Ops, SparseCore 0:
  12.7 143.6 all-gather.2

commit v2 on v1

v2 whole, which is shorter than its diff:
```python
import functools

import jax
import jax.numpy as jnp
from jax import lax
from jax.experimental import pallas as pl
from jax.experimental.pallas import tpu as pltpu
from jax.sharding import PartitionSpec as P

D = 2048
HEADS = 8
HDIM = 128
BLOCKS_DEV = 4
BLK = 32
MICRO = 2
ROWS = BLK * BLOCKS_DEV
EXT = ROWS + 2 * BLK
WIDTH = HEADS * HDIM
PACK = 2 * WIDTH + 128
EPS = 1e-06
VMEM_LIMIT = 16 << 20
SCALE = HDIM ** (-0.5)
F32 = jnp.float32
BF16 = jnp.bfloat16

NT = (((1,), (1,)), ((), ()))
NN = (((1,), (0,)), ((), ()))
TN = (((0,), (0,)), ((), ()))


def dot(a, b, dims=NN):
    return lax.dot_general(a, b, dims, preferred_element_type=F32)


def wtile(w_ref, row, count, col, width):
    tile = w_ref[:, row : row + count, col : col + width]
    return tile.reshape(tile.shape[0] * count, width)


def schedule(step, position):
    micro_id = step - position
    active = (micro_id >= 0) & (micro_id < MICRO)
    return active, jnp.clip(micro_id, 0, MICRO - 1), position == 0


def forward_body(
    step,
    section_ref,
    x0_ref,
    x_ref,
    xl_ref,
    xr_ref,
    mask_ref,
    w_ref,
    xs_in,
    out_in,
    qa_in,
    kv_in,
    rr_in,
    next_ref,
    xs_ref,
    out_ref,
    qa_ref,
    kv_ref,
    rr_ref,
    xe,
    normed,
    qa,
    kv,
    rr,
    result,
    inverse,
    mask,
    sem_in,
    sem_out,
):
    active, slot, first = schedule(step, section_ref[0])

    @pl.when(active)
    def _():
        mask_copy = pltpu.make_async_copy(mask_ref.at[slot], mask, sem_in.at[3])
        mask_copy.start()

        @pl.when(first)
        def _():
            copy = pltpu.make_async_copy(x0_ref.at[slot], xe, sem_in.at[0])
            copy.start()
            copy.wait()

        @pl.when(jnp.logical_not(first))
        def _():
            copies = [
                pltpu.make_async_copy(xl_ref, xe.at[:BLK], sem_in.at[0]),
                pltpu.make_async_copy(x_ref, xe.at[BLK : BLK + ROWS], sem_in.at[1]),
                pltpu.make_async_copy(xr_ref, xe.at[BLK + ROWS :], sem_in.at[2]),
            ]
            for copy in copies:
                copy.start()
            for copy in copies:
                copy.wait()

        saves = [pltpu.make_async_copy(xe.at[BLK : BLK + ROWS], xs_ref.at[slot], sem_out.at[0])]
        saves[0].start()

        @pl.loop(0, EXT // BLK)
        def _(block):
            at = pl.ds(pl.multiple_of(block * BLK, BLK), BLK)
            rows = xe[at].astype(F32)
            scale = lax.rsqrt(jnp.mean(rows * rows, axis=-1, keepdims=True) + EPS)
            normed[at] = (rows * scale).astype(BF16)

        rr[...] = jnp.zeros((ROWS, 128), F32)
        inverse[...] = jnp.zeros((ROWS, 128), F32)
        mask_copy.wait()

        @pl.loop(0, 4)
        def _(pair):
            lane = lax.broadcasted_iota(jnp.int32, (ROWS, 128), 1)
            tile = pl.ds(pl.multiple_of(pair * 256, 256), 256)
            queries = dot(normed[BLK : BLK + ROWS], w_ref[:, 0:64, tile].reshape(D, 256))
            keys = dot(normed[...], w_ref[:, 64:128, tile].reshape(D, 256))
            values = dot(normed[...], w_ref[:, 128:192, tile].reshape(D, 256))
            for half in range(2):
                head = pair * 2 + half
                cols = slice(half * HDIM, (half + 1) * HDIM)
                at = pl.ds(pl.multiple_of(head * HDIM, HDIM), HDIM)
                beyond = pl.ds(pl.multiple_of(WIDTH + head * HDIM, HDIM), HDIM)
                query, key, value = queries[:, cols], keys[:, cols], values[:, cols]
                rq = lax.rsqrt(jnp.mean(query * query, axis=-1, keepdims=True) + EPS)
                rk = lax.rsqrt(jnp.mean(key * key, axis=-1, keepdims=True) + EPS)
                query = (query * rq).astype(BF16)
                key = (key * rk).astype(BF16)
                value = value.astype(BF16)
                probs = jnp.exp(dot(query, key, NT) * SCALE) * mask[...]
                inv = 1.0 / jnp.sum(probs, axis=-1, keepdims=True)
                attended = dot(probs.astype(BF16), value) * inv
                qa[:, at] = query
                qa[:, beyond] = attended.astype(BF16)
                kv[:, at] = key
                kv[:, beyond] = value
                high = inv.astype(BF16).astype(F32)
                stored = jnp.where(lane == head, rq, rr[...])
                rr[...] = jnp.where(lane == HEADS + head, rk[BLK : BLK + ROWS], stored)
                stored = jnp.where(lane == head, high, inverse[...])
                inverse[...] = jnp.where(lane == HEADS + head, inv - high, stored)

        qa[:, 2 * WIDTH :] = inverse[...].astype(BF16)
        for index, (source, target) in enumerate(((qa, qa_ref), (kv, kv_ref), (rr, rr_ref))):
            copy = pltpu.make_async_copy(source, target.at[slot], sem_out.at[1 + index])
            copy.start()
            saves.append(copy)

        for half in range(2):
            @pl.loop(0, 4)
            def _(tile):
                source = pl.ds(pl.multiple_of(tile * 256, 256), 256)
                cols = pl.ds(pl.multiple_of(half * 1024 + tile * 256, 256), 256)
                low = 192 + 32 * half
                weight = w_ref[:, low : low + 32, source].reshape(WIDTH, 256)
                update = dot(qa[:, WIDTH : 2 * WIDTH], weight)
                result[:, cols] = (xe[BLK : BLK + ROWS, cols].astype(F32) + update).astype(BF16)

        for index, (source, target) in enumerate(
            (
                (result, next_ref),
                (result, out_ref.at[slot]),
            )
        ):
            copy = pltpu.make_async_copy(source, target, sem_out.at[4 + index])
            copy.start()
            saves.append(copy)
        for copy in saves:
            copy.wait()


def spaces(*names):
    table = dict(s=pltpu.SMEM, v=pltpu.VMEM, a=pltpu.HBM)
    return [pl.BlockSpec(memory_space=table[n]) for n in names]


def shape_of(a):
    return jax.ShapeDtypeStruct(a.shape, a.dtype)


def forward_call(step, position, x0, x, xl, xr, mask, w, saved):
    rows = jax.ShapeDtypeStruct((ROWS, D), BF16)
    outs = pl.pallas_call(
        functools.partial(forward_body, step),
        name="forward_layer",
        out_shape=(rows,) + tuple(shape_of(a) for a in saved),
        in_specs=spaces(*"saaaaavaaaaa"),
        out_specs=spaces(*"aaaaaa"),
        scratch_shapes=[
            pltpu.VMEM((EXT, D), BF16),
            pltpu.VMEM((EXT, D), BF16),
            pltpu.VMEM((ROWS, PACK), BF16),
            pltpu.VMEM((EXT, 2 * WIDTH), BF16),
            pltpu.VMEM((ROWS, 128), F32),
            pltpu.VMEM((ROWS, D), BF16),
            pltpu.VMEM((ROWS, 128), F32),
            pltpu.VMEM((ROWS, EXT), F32),
            pltpu.SemaphoreType.DMA((4,)),
            pltpu.SemaphoreType.DMA((6,)),
        ],
        input_output_aliases={7: 1, 8: 2, 9: 3, 10: 4, 11: 5},
        compiler_params=pltpu.CompilerParams(vmem_limit_bytes=VMEM_LIMIT),
    )(position, x0, x, xl, xr, mask, w, *saved)
    return outs[0], outs[1:]

def load_body(g_ref, w_ref, sem):
    copy = pltpu.make_async_copy(g_ref, w_ref, sem)
    copy.start()
    copy.wait()


def load_call(g):
    return pl.pallas_call(
        load_body,
        name="load_weights",
        out_shape=pltpu.VMEM(g.shape, g.dtype),
        in_specs=spaces("a"),
        out_specs=pl.BlockSpec(memory_space=pltpu.VMEM),
        scratch_shapes=[pltpu.SemaphoreType.DMA],
        compiler_params=pltpu.CompilerParams(vmem_limit_bytes=20 << 20),
    )(g)


def backward_body(
    step,
    section_ref,
    c0_ref,
    g_ref,
    gl_ref,
    gr_ref,
    mask_ref,
    w_ref,
    xs_ref,
    qa_ref,
    qal_ref,
    qar_ref,
    kv_ref,
    rr_ref,
    grad_in,
    next_ref,
    grad_ref,
    ge,
    xs,
    qa,
    kv,
    rr,
    dz,
    dn,
    result,
    mask,
    inner_ref,
    sem_in,
    sem_save,
    sem_out,
):
    active, slot, last = schedule(step, section_ref[0])
    own = slice(BLK, BLK + ROWS)

    @pl.when(active)
    def _():
        loads = [
            pltpu.make_async_copy(source.at[slot], target, sem_save.at[index])
            for index, (source, target) in enumerate(
                (
                    (qal_ref, qa.at[:BLK]),
                    (qa_ref, qa.at[own]),
                    (qar_ref, qa.at[BLK + ROWS :]),
                    (kv_ref, kv),
                    (rr_ref, rr),
                    (xs_ref, xs),
                    (mask_ref, mask),
                )
            )
        ]

        @pl.when(last)
        def _():
            copy = pltpu.make_async_copy(c0_ref.at[slot], ge, sem_in.at[0])
            copy.start()
            for load in loads:
                load.start()
            copy.wait()

        @pl.when(jnp.logical_not(last))
        def _():
            copies = [
                pltpu.make_async_copy(gl_ref, ge.at[:BLK], sem_in.at[0]),
                pltpu.make_async_copy(g_ref, ge.at[own], sem_in.at[1]),
                pltpu.make_async_copy(gr_ref, ge.at[BLK + ROWS :], sem_in.at[2]),
            ]
            for copy in copies:
                copy.start()
            for load in loads:
                load.start()
            for copy in copies:
                copy.wait()

        for load in loads:
            load.wait()

        @pl.loop(0, 4)
        def _(pair):
            lane = lax.broadcasted_iota(jnp.int32, (EXT, 128), 1)
            rows = pl.ds(pl.multiple_of(8 * pair, 8), 8)
            low = w_ref[rows, 192:224, :].reshape(256, 1024)
            high = w_ref[rows, 224:256, :].reshape(256, 1024)
            spread = dot(ge[:, :1024], low, NT) + dot(ge[:, 1024:], high, NT)
            for half in range(2):
                head = pair * 2 + half
                at = pl.ds(pl.multiple_of(head * HDIM, HDIM), HDIM)
                beyond = pl.ds(pl.multiple_of(WIDTH + head * HDIM, HDIM), HDIM)
                third = pl.ds(pl.multiple_of(2 * WIDTH + head * HDIM, HDIM), HDIM)
                d_att = spread[:, half * HDIM : (half + 1) * HDIM].astype(BF16).astype(F32)
                query, key, value = qa[:, at], kv[:, at], kv[:, beyond]
                picked = (lane == head) | (lane == HEADS + head)
                inv = jnp.sum(
                    jnp.where(picked, qa[:, 2 * WIDTH :].astype(F32), 0.0),
                    axis=-1,
                    keepdims=True,
                )
                d_sum = (d_att * inv).astype(BF16)
                d_total = -inv * jnp.sum(
                    d_att * qa[:, beyond].astype(F32), axis=-1, keepdims=True
                )
                probs = jnp.exp(dot(query, key, NT) * SCALE) * mask[...]
                d_probs = dot(d_sum, value, NT)
                d_scores = (probs * (d_probs + d_total) * SCALE).astype(BF16)
                d_value = dot(probs.astype(BF16), d_sum, TN)[own]
                d_key = dot(d_scores, query, TN)[own]
                d_query = dot(d_scores[own], key)

                def unnorm(grad, unit, which):
                    grad = grad.astype(BF16).astype(F32)
                    unit = unit.astype(F32)
                    r = jnp.sum(
                        jnp.where(lane[:ROWS] == which, rr[...], 0.0), axis=-1, keepdims=True
                    )
                    return r * (grad - unit * jnp.mean(grad * unit, axis=-1, keepdims=True))

                dz[:, at] = unnorm(d_query, query[own], head).astype(BF16)
                dz[:, beyond] = unnorm(d_key, key[own], HEADS + head).astype(BF16)
                dz[:, third] = d_value.astype(BF16)

        inner_ref[...] = jnp.zeros((ROWS, 128), F32)

        @pl.loop(0, 8)
        def _(tile):
            rows = pl.ds(pl.multiple_of(4 * tile, 4), 4)
            cols = pl.ds(pl.multiple_of(tile * 256, 256), 256)
            grad = jnp.zeros((ROWS, 256), F32)
            for part in range(3):
                weight = w_ref[rows, 64 * part : 64 * part + 64, :].reshape(256, WIDTH)
                grad += dot(dz[:, part * WIDTH : (part + 1) * WIDTH], weight, NT)
            grad = grad.astype(BF16).astype(F32)
            dn[:, cols] = grad
            product = grad * xs[:, cols].astype(F32)
            inner_ref[...] += product[:, :128] + product[:, 128:]

        @pl.loop(0, ROWS // BLK)
        def _(block):
            at = pl.ds(pl.multiple_of(block * BLK, BLK), BLK)
            x = xs[at].astype(F32)
            scale = lax.rsqrt(jnp.mean(x * x, axis=-1, keepdims=True) + EPS)
            inner = jnp.sum(inner_ref[at], axis=-1, keepdims=True) * scale * scale * (1.0 / D)
            through = ge[pl.ds(pl.multiple_of(block * BLK + BLK, BLK), BLK)].astype(F32)
            result[at] = (through + scale * (dn[at] - x * inner)).astype(BF16)

        saves = [
            pltpu.make_async_copy(source, target, sem_out.at[index])
            for index, (source, target) in enumerate(
                (
                    (result, next_ref),
                    (result, grad_ref.at[slot]),
                )
            )
        ]
        for copy in saves:
            copy.start()
        for copy in saves:
            copy.wait()


def backward_call(step, position, c0, g, gl, gr, mask, w, xs, qa, qal, qar, kv, rr, grads):
    rows = jax.ShapeDtypeStruct((ROWS, D), BF16)
    outs = pl.pallas_call(
        functools.partial(backward_body, step),
        name="backward_layer",
        out_shape=(rows, shape_of(grads)),
        in_specs=spaces(*"saaaaavaaaaaaa"),
        out_specs=spaces(*"aa"),
        scratch_shapes=[
            pltpu.VMEM((EXT, D), BF16),
            pltpu.VMEM((ROWS, D), BF16),
            pltpu.VMEM((EXT, PACK), BF16),
            pltpu.VMEM((EXT, 2 * WIDTH), BF16),
            pltpu.VMEM((ROWS, 128), F32),
            pltpu.VMEM((ROWS, 3 * WIDTH), BF16),
            pltpu.VMEM((ROWS, D), F32),
            pltpu.VMEM((ROWS, D), BF16),
            pltpu.VMEM((EXT, EXT), F32),
            pltpu.VMEM((ROWS, 128), F32),
            pltpu.SemaphoreType.DMA((3,)),
            pltpu.SemaphoreType.DMA((7,)),
            pltpu.SemaphoreType.DMA((2,)),
        ],
        input_output_aliases={13: 1},
        compiler_params=pltpu.CompilerParams(vmem_limit_bytes=VMEM_LIMIT),
    )(position, c0, g, gl, gr, mask, w, xs, qa, qal, qar, kv, rr, grads)
    return outs

BOTH = ("section", "ctx")


def neighbours(n_ctx, distance):
    return [(c, c + distance) for c in range(n_ctx) if 0 <= c + distance < n_ctx]


def hop(sections, step, n_ctx):
    return [(s * n_ctx + c, (s + step) * n_ctx + c) for s in sections for c in range(n_ctx)]


def relay(rows, sections, step, n_ctx):
    rows = lax.ppermute(rows, BOTH, hop(sections, step, n_ctx))
    return (rows, *edges(rows, 0, BLK, n_ctx))


def edges(block, dim, width, n_ctx):
    size = block.shape[dim]
    tail = lax.slice_in_dim(block, size - width, size, axis=dim)
    head = lax.slice_in_dim(block, 0, width, axis=dim)
    from_left = lax.ppermute(tail, "ctx", neighbours(n_ctx, 1))
    from_right = lax.ppermute(head, "ctx", neighbours(n_ctx, -1))
    return from_left, from_right


def allowed_keys(block_mask, place, n_ctx):
    block_ids = place * BLOCKS_DEV + jnp.arange(BLOCKS_DEV)
    mask = block_mask.astype(F32)
    left = mask[:, :, 0] * (block_ids > 0).astype(F32)
    right = mask[:, :, 1] * (block_ids < BLOCKS_DEV * n_ctx - 1).astype(F32)
    return jnp.stack([left, jnp.ones_like(left), right], axis=2)


def key_weights(before, allow, after):
    allow = jnp.concatenate([before, allow, after], axis=1)
    allow = jnp.repeat(allow, BLK, axis=1)
    block = jnp.arange(EXT) // BLK
    offset = block[None, :] - block[:, None] + 1
    return sum(
        jnp.where(offset == side, allow[:, :, side : side + 1], 0.0) for side in range(3)
    )


def per_device(section_input, cotangent, w_query, w_key, w_value, w_out, block_mask):
    n_section = lax.axis_size("section")
    n_ctx = lax.axis_size("ctx")
    section = lax.axis_index("section")
    place = lax.axis_index("ctx")
    micro = section_input.shape[0]
    steps = n_section + micro - 1

    shard = jnp.concatenate(
        [w_query[0], w_key[0], w_value[0], w_out[0][:, :WIDTH], w_out[0][:, WIDTH:]], axis=0
    )
    gathered = lax.all_gather(shard, "ctx", axis=0, tiled=False)
    position = jnp.full((1,), section, jnp.int32)
    reverse = n_section - 1 - position
    allow = allowed_keys(block_mask, place, n_ctx)
    fields = jnp.stack([section_input, cotangent])

    def packed(part, block):
        lanes = jnp.pad(part.reshape(1, -1), ((0, 15), (0, D - part.size)))
        return jnp.concatenate([block.reshape(-1, D), lanes.astype(BF16)], axis=0)

    pieces = jnp.concatenate(
        [packed(allow[:, :1], fields[:, :, :BLK]), packed(allow[:, -1:], fields[:, :, -BLK:])]
    )
    size = pieces.shape[0] // 2
    before, after = edges(pieces, 0, size, n_ctx)

    def unpacked(piece):
        block = piece[: size - 16].reshape(2, micro, BLK, D)
        return block, piece[size - 16, : 3 * micro].astype(F32).reshape(micro, 1, 3)

    before, before_allow = unpacked(before)
    after, after_allow = unpacked(after)
    extended = jnp.concatenate([before, fields, after], axis=2)
    mask = key_weights(before_allow, allow, after_allow)
    forward_mask = mask[:, BLK : BLK + ROWS]
    weights = load_call(gathered)

    saved = (
        jnp.zeros((micro, ROWS, D), BF16),
        jnp.zeros((micro, ROWS, D), BF16),
        jnp.zeros((micro, ROWS, PACK), BF16),
        jnp.zeros((micro, EXT, 2 * WIDTH), BF16),
        jnp.zeros((micro, ROWS, 128), F32),
    )
    zero_rows = jnp.zeros((ROWS, D), BF16)
    zero_edge = jnp.zeros((BLK, D), BF16)
    incoming = (zero_rows, zero_edge, zero_edge)
    for step in range(steps):
        rows, saved = forward_call(
            step, position, extended[0], *incoming, forward_mask, weights, saved
        )
        senders = [s for s in range(step - micro + 1, step + 1) if 0 <= s < n_section - 1]
        if senders:
            incoming = relay(rows, senders, 1, n_ctx)
    xs, outputs, qa, kv, rr = saved
    qa_left, qa_right = edges(qa, 1, BLK, n_ctx)
    grads = jnp.zeros((micro, ROWS, D), BF16)
    incoming = (zero_rows, zero_edge, zero_edge)
    for step in range(steps):
        rows, grads = backward_call(
            step,
            reverse,
            extended[1],
            *incoming,
            mask,
            weights,
            xs,
            qa,
            qa_left,
            qa_right,
            kv,
            rr,
            grads,
        )
        top = n_section - 1 - step
        senders = [s for s in range(top, top + micro) if 0 < s < n_section]
        if senders:
            incoming = relay(rows, senders, -1, n_ctx)
    return (outputs[None], grads[None])


def solution(mesh):
    return jax.shard_map(
        per_device,
        mesh=mesh,
        in_specs=(
            P(None, "ctx", None),
            P(None, "ctx", None),
            P("section", "ctx", None),
            P("section", "ctx", None),
            P("section", "ctx", None),
            P("section", "ctx", None),
            P(None, "ctx", None),
        ),
        out_specs=(P("section", None, "ctx", None), P("section", None, "ctx", None)),
        check_vma=False,
    )
```

time: 976 us -> 705 us (0.72)
  the two profiles are of different devices: /device:TPU:100 before, /device:TPU:128 now
where the time goes in v2:
time: 705 us; the launch traced here: 694 us
  waiting for transfers between devices  482 us (68%)
  starting transfers between devices  123 us (17%)
  Pallas kernels  49.9 us (7%)
  local copies, waits for them, and re-layouts  19.3 us (3%)
  between operations  15.2 us (2%)
    ppermute x16, waiting for transfers between devices, relay(): rows = lax.ppermute(rows, BOTH, hop(sections, step, n_ctx))  244 us
    ppermute x18, waiting for transfers between devices, edges(): from_left = lax.ppermute(tail, 'ctx', neighbours(n_ctx, 1))  106 us
    all_gather x1, waiting for transfers between devices, per_device(): gathered = lax.all_gather(shard, 'ctx', axis=0, tiled=False)  104 us
    ppermute x18, starting transfers between devices, edges(): from_left = lax.ppermute(tail, 'ctx', neighbours(n_ctx, 1))  68.2 us
    ppermute x18, starting transfers between devices, edges(): from_right = lax.ppermute(head, 'ctx', neighbours(n_ctx, -1))  41.3 us
    pallas_call x9, Pallas kernels, backward_call(): pl.pallas_call(functools.partial(backward_body, step), name='backward_lay...  30 us
    ppermute x18, waiting for transfers between devices, edges(): from_right = lax.ppermute(head, 'ctx', neighbours(n_ctx, -1))  28.3 us
    pallas_call x9, Pallas kernels, forward_call(): pl.pallas_call(functools.partial(forward_body, step), name='forward_layer...  18.7 us
  transfers between devices with their start and end apart: 53, of which 41 were waited for; matrix products, arithmetic and copies ran while one was open for 1% of the time, Pallas kernels for 0%

profile of v2, /device:TPU:128, one launch (start us, length us, event | category | flops | bytes accessed | tf_op | source)
XLA Modules:
  0.0 694.4 jit_solution(15871305443092772218)
XLA Ops:
  17.6 5.8 collective-permute-start.1
  23.6 14.4 %collective-permute-done = bf16[144,2048]{1,0:T(8,128)(2,1)} collective-permute-done((bf16[144,2048]{1,0:T(8,128)(2,1)S(1)}, bf16[144,2048]{1,0:T(8,128)(2,1)}, u32[]{:S(2)}, u32[]{:S(2)}) %collective-permute-start) | collective-permute-done | bytes 589856 | tf_op jit(solution)/shard_map/ppermute | solution.py:435
  38.7 5.9 collective-permute-done.1
  51.1 103.7 %all-gather.3.cloned.1.call-done = bf16[8192,1024]{1,0:T(8,128)(2,1)} async-done(((bf16[256,1024]{1,0:T(8,128)(2,1)}), bf16[8192,1024]{1,0:T(8,128)(2,1)}) %all-gather.3.cloned.1.call-update) | async-done | bytes 16777232 | tf_op jit(solution)/shard_map/all_gather | solution.py:469
  154.8 5.8 copy-done.1
  164.0 8.9 %forward_layer.9 = (bf16[128,2048]{1,0:T(8,128)(2,1)S(1)}, bf16[2,128,2048]{2,1,0:T(8,128)(2,1)S(1)}, bf16[2,128,2048]{2,1,0:T(8,128)(2,1)}, bf16[2,128,2176]{2,...) custom-call(s32[1]{0:T(128)} %bitcast.section_ref, ...), custom_call_target="tpu_custom_call", output_to_operand_aliasing={{1}: (7, {}), {2}: (8, {}), {3}: (9, {}), {4}: (10, {}), {5... | custom-call | tf_op jit(solution)/shard_map/forward_layer/pallas_call | solution.py:187
  183.8 7.4 %collective-permute-done.3.xl_ref = bf16[32,2048]{1,0:T(8,128)(2,1)S(1)} collective-permute-done((bf16[32,2048]{1,0:T(8,128)(2,1)S(1)}, bf16[32,2048]{1,0:T(8,128)(2,1)S(1)}, u32[]{:S(2)}, u32[]{:S(2)}) %collective-permute-start.3) | collective-permute-done | bytes 131104 | tf_op jit(solution)/shard_map/ppermute | solution.py:435
  191.2 8.9 %forward_layer.10 = (bf16[128,2048]{1,0:T(8,128)(2,1)S(1)}, bf16[2,128,2048]{2,1,0:T(8,128)(2,1)S(1)}, bf16[2,128,2048]{2,1,0:T(8,128)(2,1)}, bf16[2,128,2176]{2...) custom-call(s32[1]{0:T(128)} %bitcast.section_ref, ...), custom_call_target="tpu_custom_call", output_to_operand_aliasing={{1}: (7, {}), {2}: (8, {}), {3}: (9, {}), {4}: (10, {}), {5... | custom-call | tf_op jit(solution)/shard_map/forward_layer/pallas_call | solution.py:187
  210.0 5.2 collective-permute-done.6.xl_ref
  222.9 5.2 collective-permute-done.9.xl_ref
  235.9 5.2 collective-permute-done.12.xl_ref
  248.8 5.2 collective-permute-done.15.xl_ref
  262.1 5.2 collective-permute-done.18.xl_ref
  301.8 5.2 collective-permute-done.26.qal_ref
  317.3 5.2 collective-permute-done.29.gl_ref
  330.3 5.2 collective-permute-done.32.gl_ref
  344.3 5.5 collective-permute-done.35.gl_ref
  358.1 5.4 collective-permute-done.38.gl_ref
  371.2 5.2 collective-permute-done.41.gl_ref
  390.9 233.6 %collective-permute-done.46.g_ref = bf16[128,2048]{1,0:T(8,128)(2,1)S(1)} collective-permute-done((bf16[128,2048]{1,0:T(8,128)(2,1)S(1)}, bf16[128,2048]{1,0:T(8,128)(2,1)S(1)}, u32[]{:S(2)}, u32[]{:S(2)}) %collective-permute-start.46) | collective-permute-done | bytes 524320 | tf_op jit(solution)/shard_map/ppermute | solution.py:427
  631.4 5.2 collective-permute-done.47.gl_ref
  636.7 14.6 %backward_layer.16 = (bf16[128,2048]{1,0:T(8,128)(2,1)S(1)}, bf16[2,128,2048]{2,1,0:T(8,128)(2,1)}) custom-call(s32[1]{0:T(128)S(6)} %sub.42.section_ref, bf16[2,192,2048]{2,1,0:T(8,128)(2,1)S(1)} %get-tuple-element.144.c0_ref, bf16[128,2048]{1,0:T(8,128)(2,1)S(1)} %collective-permute-done.46.g_ref, ...), custom_call_target="tpu_custom_call", output_to_operand_aliasing={{1}: (13, {})} | custom-call | tf_op jit(solution)/shard_map/backward_layer/pallas_call | solution.py:389
  652.5 7.4 %collective-permute-done.49.g_ref = bf16[128,2048]{1,0:T(8,128)(2,1)S(1)} collective-permute-done((bf16[128,2048]{1,0:T(8,128)(2,1)S(1)}, bf16[128,2048]{1,0:T(8,128)(2,1)S(1)}, u32[]{:S(2)}, u32[]{:S(2)}) %collective-permute-start.49) | collective-permute-done | bytes 524320 | tf_op jit(solution)/shard_map/ppermute | solution.py:427
  672.7 14.7 %backward_layer.17 = (bf16[128,2048]{1,0:T(8,128)(2,1)}, bf16[2,128,2048]{2,1,0:T(8,128)(2,1)}) custom-call(s32[1]{0:T(128)S(6)} %sub.42.section_ref, bf16[2,192,2048]{2,1,0:T(8,128)(2,1)S(1)} %get-tuple-element.144.c0_ref, bf16[128,2048]{1,0:T(8,128)(2,1)S(1)} %collective-permute-done.49.g_ref, ...), custom_call_target="tpu_custom_call", output_to_operand_aliasing={{1}: (13, {})} | custom-call | tf_op jit(solution)/shard_map/backward_layer/pallas_call | solution.py:389
  (172 shorter events, 184.7 us)
Async XLA Ops:
  7.2 147.6 %all-gather.3.cloned.1.call-start = ((), (), s32[]{:S(2)}) async-start(), calls=%async_computation | async-start | bytes 17301504 | tf_op jit(solution)/shard_map/all_gather | solution.py:469
  14.1 23.9 %collective-permute-start = (bf16[144,2048]{1,0:T(8,128)(2,1)S(1)}, bf16[144,2048]{1,0:T(8,128)(2,1)}, u32[]{:S(2)}, u32[]{:S(2)}) collective-permute-start(bf16[144,2048]{1,0:T(8,128)(2,1)S(1)} %fusion.2), channel_id=1, source_target_pairs={{0,1},{1,2},{2,3},{3,4},{4,5},{5,6},{6,7},{7,8},{8,9},{9,10},{10,1... | collective-permute-start | bytes 1769480 | tf_op jit(solution)/shard_map/ppermute | solution.py:435
  17.6 27.0 %collective-permute-start.1 = (bf16[144,2048]{1,0:T(8,128)(2,1)S(1)}, bf16[144,2048]{1,0:T(8,128)(2,1)}, u32[]{:S(2)}, u32[]{:S(2)}) collective-permute-start(bf16[144,2048]{1,0:T(8,128)(2,1)S(1)} %fusion.3), channel_id=1, source_target_pairs={{1,0},{2,1},{3,2},{4,3},{5,4},{6,5},{7,6},{8,7},{9,8},{10,9},{11,1... | collective-permute-start | bytes 1769480 | tf_op jit(solution)/shard_map/ppermute | solution.py:436
  180.5 10.7 %collective-permute-start.3 = (bf16[32,2048]{1,0:T(8,128)(2,1)S(1)}, bf16[32,2048]{1,0:T(8,128)(2,1)S(1)}, u32[]{:S(2)}, u32[]{:S(2)}) collective-permute-start(bf16[32,2048]{1,0:T(8,128)(2,1)S(1)} %get-tuple-element.181), channel_id=1, source_target_pairs={{0,1},{1,2},{2,3},{3,4},{4,5},{5,6},{6,7},{7,8},{8,9},{9,10},{10,1... | collective-permute-start | bytes 393224 | tf_op jit(solution)/shard_map/ppermute | solution.py:435
  205.1 10.2 %collective-permute-start.6 = (bf16[32,2048]{1,0:T(8,128)(2,1)S(1)}, bf16[32,2048]{1,0:T(8,128)(2,1)S(1)}, u32[]{:S(2)}, u32[]{:S(2)}) collective-permute-start(bf16[32,2048]{1,0:T(8,128)(2,1)S(1)} %get-tuple-element.179), channel_id=1, source_target_pairs={{0,1},{1,2},{2,3},{3,4},{4,5},{5,6},{6,7},{7,8},{8,9},{9,10},{10,1... | collective-permute-start | bytes 393224 | tf_op jit(solution)/shard_map/ppermute | solution.py:435
  218.0 10.2 %collective-permute-start.9 = (bf16[32,2048]{1,0:T(8,128)(2,1)S(1)}, bf16[32,2048]{1,0:T(8,128)(2,1)S(1)}, u32[]{:S(2)}, u32[]{:S(2)}) collective-permute-start(bf16[32,2048]{1,0:T(8,128)(2,1)S(1)} %get-tuple-element.177), channel_id=1, source_target_pairs={{0,1},{1,2},{2,3},{3,4},{4,5},{5,6},{6,7},{7,8},{8,9},{9,10},{10,1... | collective-permute-start | bytes 393224 | tf_op jit(solution)/shard_map/ppermute | solution.py:435
  230.9 10.2 %collective-permute-start.12 = (bf16[32,2048]{1,0:T(8,128)(2,1)S(1)}, bf16[32,2048]{1,0:T(8,128)(2,1)S(1)}, u32[]{:S(2)}, u32[]{:S(2)}) collective-permute-start(bf16[32,2048]{1,0:T(8,128)(2,1)S(1)} %get-tuple-element.175), channel_id=1, source_target_pairs={{0,1},{1,2},{2,3},{3,4},{4,5},{5,6},{6,7},{7,8},{8,9},{9,10},{10,1... | collective-permute-start | bytes 393224 | tf_op jit(solution)/shard_map/ppermute | solution.py:435
  243.9 10.2 %collective-permute-start.15 = (bf16[32,2048]{1,0:T(8,128)(2,1)S(1)}, bf16[32,2048]{1,0:T(8,128)(2,1)S(1)}, u32[]{:S(2)}, u32[]{:S(2)}) collective-permute-start(bf16[32,2048]{1,0:T(8,128)(2,1)S(1)} %get-tuple-element.173), channel_id=1, source_target_pairs={{0,1},{1,2},{2,3},{3,4},{4,5},{5,6},{6,7},{7,8},{8,9},{9,10},{10,1... | collective-permute-start | bytes 393224 | tf_op jit(solution)/shard_map/ppermute | solution.py:435
  257.2 10.2 %collective-permute-start.18 = (bf16[32,2048]{1,0:T(8,128)(2,1)S(1)}, bf16[32,2048]{1,0:T(8,128)(2,1)S(1)}, u32[]{:S(2)}, u32[]{:S(2)}) collective-permute-start(bf16[32,2048]{1,0:T(8,128)(2,1)S(1)} %get-tuple-element.171), channel_id=1, source_target_pairs={{0,1},{1,2},{2,3},{3,4},{4,5},{5,6},{6,7},{7,8},{8,9},{9,10},{10,1... | collective-permute-start | bytes 393224 | tf_op jit(solution)/shard_map/ppermute | solution.py:435
  270.1 10.2 %collective-permute-start.21 = (bf16[32,2048]{1,0:T(8,128)(2,1)S(1)}, bf16[32,2048]{1,0:T(8,128)(2,1)S(1)}, u32[]{:S(2)}, u32[]{:S(2)}) collective-permute-start(bf16[32,2048]{1,0:T(8,128)(2,1)S(1)} %get-tuple-element.169), channel_id=1, source_target_pairs={{0,1},{1,2},{2,3},{3,4},{4,5},{5,6},{6,7},{7,8},{8,9},{9,10},{10,1... | collective-permute-start | bytes 393224 | tf_op jit(solution)/shard_map/ppermute | solution.py:435
  283.1 10.2 %collective-permute-start.24 = (bf16[32,2048]{1,0:T(8,128)(2,1)S(1)}, bf16[32,2048]{1,0:T(8,128)(2,1)S(1)}, u32[]{:S(2)}, u32[]{:S(2)}) collective-permute-start(bf16[32,2048]{1,0:T(8,128)(2,1)S(1)} %get-tuple-element.167), channel_id=1, source_target_pairs={{0,1},{1,2},{2,3},{3,4},{4,5},{5,6},{6,7},{7,8},{8,9},{9,10},{10,1... | collective-permute-start | bytes 393224 | tf_op jit(solution)/shard_map/ppermute | solution.py:435
  293.4 8.4 %collective-permute-start.27 = (bf16[2,32,2176]{2,1,0:T(8,128)(2,1)S(1)}, bf16[2,32,2176]{2,1,0:T(8,128)(2,1)S(1)}, u32[]{:S(2)}, u32[]{:S(2)}) collective-permute-start(bf16[2,32,2176]{2,1,0:T(8,128)(2,1)S(1)} %get-tuple-element.148), channel_id=1, source_target_pairs={{1,0},{2,1},{3,2},{4,3},{5,4},{6,5},{7,6},{8,7},{9,8},{10,9},{11,1... | collective-permute-start | bytes 835592 | tf_op jit(solution)/shard_map/ppermute | solution.py:436
  295.3 11.8 %collective-permute-start.26 = (bf16[2,32,2176]{2,1,0:T(8,128)(2,1)S(1)}, bf16[2,32,2176]{2,1,0:T(8,128)(2,1)S(1)}, u32[]{:S(2)}, u32[]{:S(2)}) collective-permute-start(bf16[2,32,2176]{2,1,0:T(8,128)(2,1)S(1)} %get-tuple-element.149), channel_id=1, source_target_pairs={{0,1},{1,2},{2,3},{3,4},{4,5},{5,6},{6,7},{7,8},{8,9},{9,10},{10,1... | collective-permute-start | bytes 835592 | tf_op jit(solution)/shard_map/ppermute | solution.py:435
  309.0 8.3 %collective-permute-start.30 = (bf16[32,2048]{1,0:T(8,128)(2,1)S(1)}, bf16[32,2048]{1,0:T(8,128)(2,1)S(1)}, u32[]{:S(2)}, u32[]{:S(2)}) collective-permute-start(bf16[32,2048]{1,0:T(8,128)(2,1)S(1)} %get-tuple-element.164), channel_id=1, source_target_pairs={{1,0},{2,1},{3,2},{4,3},{5,4},{6,5},{7,6},{8,7},{9,8},{10,9},{11,1... | collective-permute-start | bytes 393224 | tf_op jit(solution)/shard_map/ppermute | solution.py:436
  311.0 11.6 %collective-permute-start.29 = (bf16[32,2048]{1,0:T(8,128)(2,1)S(1)}, bf16[32,2048]{1,0:T(8,128)(2,1)S(1)}, u32[]{:S(2)}, u32[]{:S(2)}) collective-permute-start(bf16[32,2048]{1,0:T(8,128)(2,1)S(1)} %get-tuple-element.165), channel_id=1, source_target_pairs={{0,1},{1,2},{2,3},{3,4},{4,5},{5,6},{6,7},{7,8},{8,9},{9,10},{10,1... | collective-permute-start | bytes 393224 | tf_op jit(solution)/shard_map/ppermute | solution.py:435
  325.3 10.2 %collective-permute-start.32 = (bf16[32,2048]{1,0:T(8,128)(2,1)S(1)}, bf16[32,2048]{1,0:T(8,128)(2,1)S(1)}, u32[]{:S(2)}, u32[]{:S(2)}) collective-permute-start(bf16[32,2048]{1,0:T(8,128)(2,1)S(1)} %get-tuple-element.163), channel_id=1, source_target_pairs={{0,1},{1,2},{2,3},{3,4},{4,5},{5,6},{6,7},{7,8},{8,9},{9,10},{10,1... | collective-permute-start | bytes 393224 | tf_op jit(solution)/shard_map/ppermute | solution.py:435
  338.3 11.6 %collective-permute-start.35 = (bf16[32,2048]{1,0:T(8,128)(2,1)S(1)}, bf16[32,2048]{1,0:T(8,128)(2,1)S(1)}, u32[]{:S(2)}, u32[]{:S(2)}) collective-permute-start(bf16[32,2048]{1,0:T(8,128)(2,1)S(1)} %get-tuple-element.161), channel_id=1, source_target_pairs={{0,1},{1,2},{2,3},{3,4},{4,5},{5,6},{6,7},{7,8},{8,9},{9,10},{10,1... | collective-permute-start | bytes 393224 | tf_op jit(solution)/shard_map/ppermute | solution.py:435
  352.6 10.9 %collective-permute-start.38 = (bf16[32,2048]{1,0:T(8,128)(2,1)S(1)}, bf16[32,2048]{1,0:T(8,128)(2,1)S(1)}, u32[]{:S(2)}, u32[]{:S(2)}) collective-permute-start(bf16[32,2048]{1,0:T(8,128)(2,1)S(1)} %get-tuple-element.159), channel_id=1, source_target_pairs={{0,1},{1,2},{2,3},{3,4},{4,5},{5,6},{6,7},{7,8},{8,9},{9,10},{10,1... | collective-permute-start | bytes 393224 | tf_op jit(solution)/shard_map/ppermute | solution.py:435
  366.3 10.2 %collective-permute-start.41 = (bf16[32,2048]{1,0:T(8,128)(2,1)S(1)}, bf16[32,2048]{1,0:T(8,128)(2,1)S(1)}, u32[]{:S(2)}, u32[]{:S(2)}) collective-permute-start(bf16[32,2048]{1,0:T(8,128)(2,1)S(1)} %get-tuple-element.157), channel_id=1, source_target_pairs={{0,1},{1,2},{2,3},{3,4},{4,5},{5,6},{6,7},{7,8},{8,9},{9,10},{10,1... | collective-permute-start | bytes 393224 | tf_op jit(solution)/shard_map/ppermute | solution.py:435
  379.3 10.2 %collective-permute-start.44 = (bf16[32,2048]{1,0:T(8,128)(2,1)S(1)}, bf16[32,2048]{1,0:T(8,128)(2,1)S(1)}, u32[]{:S(2)}, u32[]{:S(2)}) collective-permute-start(bf16[32,2048]{1,0:T(8,128)(2,1)S(1)} %get-tuple-element.155), channel_id=1, source_target_pairs={{0,1},{1,2},{2,3},{3,4},{4,5},{5,6},{6,7},{7,8},{8,9},{9,10},{10,1... | collective-permute-start | bytes 393224 | tf_op jit(solution)/shard_map/ppermute | solution.py:435
  389.6 234.9 %collective-permute-start.46 = (bf16[128,2048]{1,0:T(8,128)(2,1)S(1)}, bf16[128,2048]{1,0:T(8,128)(2,1)S(1)}, u32[]{:S(2)}, u32[]{:S(2)}) collective-permute-start(bf16[128,2048]{1,0:T(8,128)(2,1)S(1)} %get-tuple-element.137), channel_id=1, source_target_pairs={{32,0},{33,1},{34,2},{35,3},{36,4},{37,5},{38,6},{39,7},{40,8},{41... | collective-permute-start | bytes 1572872 | tf_op jit(solution)/shard_map/ppermute | solution.py:427
  626.5 10.2 %collective-permute-start.47 = (bf16[32,2048]{1,0:T(8,128)(2,1)S(1)}, bf16[32,2048]{1,0:T(8,128)(2,1)S(1)}, u32[]{:S(2)}, u32[]{:S(2)}) collective-permute-start(bf16[32,2048]{1,0:T(8,128)(2,1)S(1)} %get-tuple-element.153), channel_id=1, source_target_pairs={{0,1},{1,2},{2,3},{3,4},{4,5},{5,6},{6,7},{7,8},{8,9},{9,10},{10,1... | collective-permute-start | bytes 393224 | tf_op jit(solution)/shard_map/ppermute | solution.py:435
  651.2 8.7 %collective-permute-start.49 = (bf16[128,2048]{1,0:T(8,128)(2,1)S(1)}, bf16[128,2048]{1,0:T(8,128)(2,1)S(1)}, u32[]{:S(2)}, u32[]{:S(2)}) collective-permute-start(bf16[128,2048]{1,0:T(8,128)(2,1)S(1)} %get-tuple-element.139), channel_id=1, source_target_pairs={{32,0},{33,1},{34,2},{35,3},{36,4},{37,5},{38,6},{39,7},{40,8},{41... | collective-permute-start | bytes 1572872 | tf_op jit(solution)/shard_map/ppermute | solution.py:427
  661.9 10.8 %collective-permute-start.50 = (bf16[32,2048]{1,0:T(8,128)(2,1)S(1)}, bf16[32,2048]{1,0:T(8,128)(2,1)S(1)}, u32[]{:S(2)}, u32[]{:S(2)}) collective-permute-start(bf16[32,2048]{1,0:T(8,128)(2,1)S(1)} %get-tuple-element.151), channel_id=1, source_target_pairs={{0,1},{1,2},{2,3},{3,4},{4,5},{5,6},{6,7},{7,8},{8,9},{9,10},{10,1... | collective-permute-start | bytes 393224 | tf_op jit(solution)/shard_map/ppermute | solution.py:435
  (35 other events, 143.2 us)
Sparse Core Ops, SparseCore 0:
  12.7 142.0 all-gather.2

commit v3 on v2

--- a/solution.py
+++ b/solution.py
@@ -58,6 +58,8 @@
     kv_in,
     rr_in,
     next_ref,
+    left_ref,
+    right_ref,
     xs_ref,
     out_ref,
     qa_ref,
@@ -113,15 +115,15 @@
         inverse[...] = jnp.zeros((ROWS, 128), F32)
         mask_copy.wait()
 
-        @pl.loop(0, 4)
+        @pl.loop(0, 2)
         def _(pair):
             lane = lax.broadcasted_iota(jnp.int32, (ROWS, 128), 1)
-            tile = pl.ds(pl.multiple_of(pair * 256, 256), 256)
-            queries = dot(normed[BLK : BLK + ROWS], w_ref[:, 0:64, tile].reshape(D, 256))
-            keys = dot(normed[...], w_ref[:, 64:128, tile].reshape(D, 256))
-            values = dot(normed[...], w_ref[:, 128:192, tile].reshape(D, 256))
-            for half in range(2):
-                head = pair * 2 + half
+            tile = pl.ds(pl.multiple_of(pair * 512, 512), 512)
+            queries = dot(normed[BLK : BLK + ROWS], w_ref[:, 0:64, tile].reshape(D, 512))
+            keys = dot(normed[...], w_ref[:, 64:128, tile].reshape(D, 512))
+            values = dot(normed[...], w_ref[:, 128:192, tile].reshape(D, 512))
+            for half in range(4):
+                head = pair * 4 + half
                 cols = slice(half * HDIM, (half + 1) * HDIM)
                 at = pl.ds(pl.multiple_of(head * HDIM, HDIM), HDIM)
                 beyond = pl.ds(pl.multiple_of(WIDTH + head * HDIM, HDIM), HDIM)
@@ -151,18 +153,20 @@
             saves.append(copy)
 
         for half in range(2):
-            @pl.loop(0, 4)
+            @pl.loop(0, 2)
             def _(tile):
-                source = pl.ds(pl.multiple_of(tile * 256, 256), 256)
-                cols = pl.ds(pl.multiple_of(half * 1024 + tile * 256, 256), 256)
+                source = pl.ds(pl.multiple_of(tile * 512, 512), 512)
+                cols = pl.ds(pl.multiple_of(half * 1024 + tile * 512, 512), 512)
                 low = 192 + 32 * half
-                weight = w_ref[:, low : low + 32, source].reshape(WIDTH, 256)
+                weight = w_ref[:, low : low + 32, source].reshape(WIDTH, 512)
                 update = dot(qa[:, WIDTH : 2 * WIDTH], weight)
                 result[:, cols] = (xe[BLK : BLK + ROWS, cols].astype(F32) + update).astype(BF16)
 
         for index, (source, target) in enumerate(
             (
                 (result, next_ref),
+                (result.at[:BLK], left_ref),
+                (result.at[ROWS - BLK :], right_ref),
                 (result, out_ref.at[slot]),
             )
         ):
@@ -184,12 +188,13 @@
 
 def forward_call(step, position, x0, x, xl, xr, mask, w, saved):
     rows = jax.ShapeDtypeStruct((ROWS, D), BF16)
+    edge = jax.ShapeDtypeStruct((BLK, D), BF16)
     outs = pl.pallas_call(
         functools.partial(forward_body, step),
         name="forward_layer",
-        out_shape=(rows,) + tuple(shape_of(a) for a in saved),
+        out_shape=(rows, edge, edge) + tuple(shape_of(a) for a in saved),
         in_specs=spaces(*"saaaaavaaaaa"),
-        out_specs=spaces(*"aaaaaa"),
+        out_specs=spaces(*"aaaaaaaa"),
         scratch_shapes=[
             pltpu.VMEM((EXT, D), BF16),
             pltpu.VMEM((EXT, D), BF16),
@@ -200,12 +205,12 @@
             pltpu.VMEM((ROWS, 128), F32),
             pltpu.VMEM((ROWS, EXT), F32),
             pltpu.SemaphoreType.DMA((4,)),
-            pltpu.SemaphoreType.DMA((6,)),
+            pltpu.SemaphoreType.DMA((8,)),
         ],
-        input_output_aliases={7: 1, 8: 2, 9: 3, 10: 4, 11: 5},
+        input_output_aliases={7: 3, 8: 4, 9: 5, 10: 6, 11: 7},
         compiler_params=pltpu.CompilerParams(vmem_limit_bytes=VMEM_LIMIT),
     )(position, x0, x, xl, xr, mask, w, *saved)
-    return outs[0], outs[1:]
+    return outs[:3], outs[3:]
 
 def load_body(g_ref, w_ref, sem):
     copy = pltpu.make_async_copy(g_ref, w_ref, sem)
@@ -242,6 +247,8 @@
     rr_ref,
     grad_in,
     next_ref,
+    left_ref,
+    right_ref,
     grad_ref,
     ge,
     xs,
@@ -302,15 +309,15 @@
         for load in loads:
             load.wait()
 
-        @pl.loop(0, 4)
+        @pl.loop(0, 2)
         def _(pair):
             lane = lax.broadcasted_iota(jnp.int32, (EXT, 128), 1)
-            rows = pl.ds(pl.multiple_of(8 * pair, 8), 8)
-            low = w_ref[rows, 192:224, :].reshape(256, 1024)
-            high = w_ref[rows, 224:256, :].reshape(256, 1024)
+            rows = pl.ds(pl.multiple_of(16 * pair, 16), 16)
+            low = w_ref[rows, 192:224, :].reshape(512, 1024)
+            high = w_ref[rows, 224:256, :].reshape(512, 1024)
             spread = dot(ge[:, :1024], low, NT) + dot(ge[:, 1024:], high, NT)
-            for half in range(2):
-                head = pair * 2 + half
+            for half in range(4):
+                head = pair * 4 + half
                 at = pl.ds(pl.multiple_of(head * HDIM, HDIM), HDIM)
                 beyond = pl.ds(pl.multiple_of(WIDTH + head * HDIM, HDIM), HDIM)
                 third = pl.ds(pl.multiple_of(2 * WIDTH + head * HDIM, HDIM), HDIM)
@@ -347,18 +354,18 @@
 
         inner_ref[...] = jnp.zeros((ROWS, 128), F32)
 
-        @pl.loop(0, 8)
+        @pl.loop(0, 4)
         def _(tile):
-            rows = pl.ds(pl.multiple_of(4 * tile, 4), 4)
-            cols = pl.ds(pl.multiple_of(tile * 256, 256), 256)
-            grad = jnp.zeros((ROWS, 256), F32)
+            rows = pl.ds(pl.multiple_of(8 * tile, 8), 8)
+            cols = pl.ds(pl.multiple_of(tile * 512, 512), 512)
+            grad = jnp.zeros((ROWS, 512), F32)
             for part in range(3):
-                weight = w_ref[rows, 64 * part : 64 * part + 64, :].reshape(256, WIDTH)
+                weight = w_ref[rows, 64 * part : 64 * part + 64, :].reshape(512, WIDTH)
                 grad += dot(dz[:, part * WIDTH : (part + 1) * WIDTH], weight, NT)
             grad = grad.astype(BF16).astype(F32)
             dn[:, cols] = grad
             product = grad * xs[:, cols].astype(F32)
-            inner_ref[...] += product[:, :128] + product[:, 128:]
+            inner_ref[...] += (product[:, :128] + product[:, 128:256]) + (product[:, 256:384] + product[:, 384:])
 
         @pl.loop(0, ROWS // BLK)
         def _(block):
@@ -374,6 +381,8 @@
             for index, (source, target) in enumerate(
                 (
                     (result, next_ref),
+                (result.at[:BLK], left_ref),
+                (result.at[ROWS - BLK :], right_ref),
                     (result, grad_ref.at[slot]),
                 )
             )
@@ -386,12 +395,13 @@
 
 def backward_call(step, position, c0, g, gl, gr, mask, w, xs, qa, qal, qar, kv, rr, grads):
     rows = jax.ShapeDtypeStruct((ROWS, D), BF16)
+    edge = jax.ShapeDtypeStruct((BLK, D), BF16)
     outs = pl.pallas_call(
         functools.partial(backward_body, step),
         name="backward_layer",
-        out_shape=(rows, shape_of(grads)),
+        out_shape=(rows, edge, edge, shape_of(grads)),
         in_specs=spaces(*"saaaaavaaaaaaa"),
-        out_specs=spaces(*"aa"),
+        out_specs=spaces(*"aaaa"),
         scratch_shapes=[
             pltpu.VMEM((EXT, D), BF16),
             pltpu.VMEM((ROWS, D), BF16),
@@ -405,12 +415,12 @@
             pltpu.VMEM((ROWS, 128), F32),
             pltpu.SemaphoreType.DMA((3,)),
             pltpu.SemaphoreType.DMA((7,)),
-            pltpu.SemaphoreType.DMA((2,)),
+            pltpu.SemaphoreType.DMA((4,)),
         ],
-        input_output_aliases={13: 1},
+        input_output_aliases={13: 3},
         compiler_params=pltpu.CompilerParams(vmem_limit_bytes=VMEM_LIMIT),
     )(position, c0, g, gl, gr, mask, w, xs, qa, qal, qar, kv, rr, grads)
-    return outs
+    return outs[:3], outs[3]
 
 BOTH = ("section", "ctx")
 
@@ -423,9 +433,21 @@
     return [(s * n_ctx + c, (s + step) * n_ctx + c) for s in sections for c in range(n_ctx)]
 
 
-def relay(rows, sections, step, n_ctx):
+def diagonal(n_section, step, n_ctx, distance):
+    return [
+        (s * n_ctx + source, (s + step) * n_ctx + target)
+        for s in range(n_section)
+        if 0 <= s + step < n_section
+        for source, target in neighbours(n_ctx, distance)
+    ]
+
+
+def relay(parts, sections, step, n_section, n_ctx):
+    rows, left, right = parts
     rows = lax.ppermute(rows, BOTH, hop(sections, step, n_ctx))
-    return (rows, *edges(rows, 0, BLK, n_ctx))
+    from_left = lax.ppermute(right, BOTH, diagonal(n_section, step, n_ctx, 1))
+    from_right = lax.ppermute(left, BOTH, diagonal(n_section, step, n_ctx, -1))
+    return rows, from_left, from_right
 
 
 def edges(block, dim, width, n_ctx):
@@ -504,18 +526,18 @@
     zero_edge = jnp.zeros((BLK, D), BF16)
     incoming = (zero_rows, zero_edge, zero_edge)
     for step in range(steps):
-        rows, saved = forward_call(
+        parts, saved = forward_call(
             step, position, extended[0], *incoming, forward_mask, weights, saved
         )
         senders = [s for s in range(step - micro + 1, step + 1) if 0 <= s < n_section - 1]
         if senders:
-            incoming = relay(rows, senders, 1, n_ctx)
+            incoming = relay(parts, senders, 1, n_section, n_ctx)
     xs, outputs, qa, kv, rr = saved
     qa_left, qa_right = edges(qa, 1, BLK, n_ctx)
     grads = jnp.zeros((micro, ROWS, D), BF16)
     incoming = (zero_rows, zero_edge, zero_edge)
     for step in range(steps):
-        rows, grads = backward_call(
+        parts, grads = backward_call(
             step,
             reverse,
             extended[1],
@@ -533,7 +555,7 @@
         top = n_section - 1 - step
         senders = [s for s in range(top, top + micro) if 0 < s < n_section]
         if senders:
-            incoming = relay(rows, senders, -1, n_ctx)
+            incoming = relay(parts, senders, -1, n_section, n_ctx)
     return (outputs[None], grads[None])
 
 

time: 705 us -> 564 us (0.80)
  the two profiles are of different devices: /device:TPU:128 before, /device:TPU:100 now
where the time goes in v3:
time: 564 us; the launch traced here: 554 us
  waiting for transfers between devices  325 us (58%)
  starting transfers between devices  141 us (25%)
  Pallas kernels  51.9 us (9%)
  local copies, waits for them, and re-layouts  18.2 us (3%)
  between operations  15.5 us (3%)
    ppermute x16, waiting for transfers between devices, relay(): from_left = lax.ppermute(right, BOTH, diagonal(n_section, step, n_ctx, 1))  127 us
    all_gather x1, waiting for transfers between devices, per_device(): gathered = lax.all_gather(shard, 'ctx', axis=0, tiled=False)  110 us
    ppermute x16, starting transfers between devices, relay(): from_left = lax.ppermute(right, BOTH, diagonal(n_section, step, n_ctx, 1))  75.2 us
    ppermute x16, waiting for transfers between devices, relay(): from_right = lax.ppermute(left, BOTH, diagonal(n_section, step, n_ctx, -1))  62.4 us
    ppermute x16, starting transfers between devices, relay(): from_right = lax.ppermute(left, BOTH, diagonal(n_section, step, n_ctx, -1))  38 us
    pallas_call x9, Pallas kernels, backward_call(): pl.pallas_call(functools.partial(backward_body, step), name='backward_lay...  33.9 us
    pallas_call x9, Pallas kernels, forward_call(): pl.pallas_call(functools.partial(forward_body, step), name='forward_layer...  16.8 us
    ppermute x2, waiting for transfers between devices, edges(): from_left = lax.ppermute(tail, 'ctx', neighbours(n_ctx, 1))  16.5 us
  transfers between devices with their start and end apart: 53, of which 34 were waited for; matrix products, arithmetic and copies ran while one was open for 1% of the time, Pallas kernels for 0%

profile of v3, /device:TPU:100, one launch (start us, length us, event | category | flops | bytes accessed | tf_op | source)
XLA Modules:
  0.0 554.2 jit_solution(15319398474313375993)
XLA Ops:
  20.3 14.0 %collective-permute-done = bf16[144,2048]{1,0:T(8,128)(2,1)} collective-permute-done((bf16[144,2048]{1,0:T(8,128)(2,1)S(1)}, bf16[144,2048]{1,0:T(8,128)(2,1)}, u32[]{:S(2)}, u32[]{:S(2)}) %collective-permute-start) | collective-permute-done | bytes 589856 | tf_op jit(solution)/shard_map/ppermute | solution.py:457
  35.0 6.0 %collective-permute-done.1 = bf16[144,2048]{1,0:T(8,128)(2,1)} collective-permute-done((bf16[144,2048]{1,0:T(8,128)(2,1)S(1)}, bf16[144,2048]{1,0:T(8,128)(2,1)}, u32[]{:S(2)}, u32[]{:S(2)}) %collective-permute-start.1) | collective-permute-done | bytes 589856 | tf_op jit(solution)/shard_map/ppermute | solution.py:458
  45.7 110.0 %all-gather.3.cloned.1.call-done = bf16[8192,1024]{1,0:T(8,128)(2,1)} async-done(((bf16[256,1024]{1,0:T(8,128)(2,1)}), bf16[8192,1024]{1,0:T(8,128)(2,1)}) %all-gather.3.cloned.1.call-update) | async-done | bytes 16777232 | tf_op jit(solution)/shard_map/all_gather | solution.py:491
  155.7 5.8 %copy-done.1 = bf16[8192,1024]{1,0:T(8,128)(2,1)S(1)} copy-done((bf16[8192,1024]{1,0:T(8,128)(2,1)S(1)}, bf16[8192,1024]{1,0:T(8,128)(2,1)}, u32[]{:S(2)}) %copy-start.1) | copy-done | bytes 16777240
  164.9 7.7 %forward_layer.9 = (bf16[128,2048]{1,0:T(8,128)(2,1)S(1)}, bf16[32,2048]{1,0:T(8,128)(2,1)S(1)}, bf16[32,2048]{1,0:T(8,128)(2,1)S(1)}, bf16[2,128,2048]{2,1,0:T(...) custom-call(s32[1]{0:T(128)} %bitcast.section_ref, ...), custom_call_target="tpu_custom_call", output_to_operand_aliasing={{3}: (7, {}), {4}: (8, {}), {5}: (9, {}), {6}: (10, {}), {7... | custom-call | tf_op jit(solution)/shard_map/forward_layer/pallas_call | solution.py:192
  179.1 7.7 %forward_layer.10 = (bf16[128,2048]{1,0:T(8,128)(2,1)S(1)}, bf16[32,2048]{1,0:T(8,128)(2,1)S(1)}, bf16[32,2048]{1,0:T(8,128)(2,1)S(1)}, bf16[2,128,2048]{2,1,0:T...) custom-call(s32[1]{0:T(128)} %bitcast.section_ref, ...), custom_call_target="tpu_custom_call", output_to_operand_aliasing={{3}: (7, {}), {4}: (8, {}), {5}: (9, {}), {6}: (10, {}), {7... | custom-call | tf_op jit(solution)/shard_map/forward_layer/pallas_call | solution.py:192
  198.8 16.8 %collective-permute-start.9 = (bf16[32,2048]{1,0:T(8,128)(2,1)S(1)}, bf16[32,2048]{1,0:T(8,128)(2,1)S(1)}, u32[]{:S(2)}, u32[]{:S(2)}) collective-permute-start(bf16[32,2048]{1,0:T(8,128)(2,1)S(1)} %get-tuple-element.121), channel_id=1, source_target_pairs={{0,33},{1,34},{2,35},{3,36},{4,37},{5,38},{6,39},{7,40},{8,41},{9,... | collective-permute-start | bytes 393224 | tf_op jit(solution)/shard_map/ppermute | solution.py:448
  221.8 7.6 %collective-permute-start.12 = (bf16[32,2048]{1,0:T(8,128)(2,1)S(1)}, bf16[32,2048]{1,0:T(8,128)(2,1)S(1)}, u32[]{:S(2)}, u32[]{:S(2)}) collective-permute-start(bf16[32,2048]{1,0:T(8,128)(2,1)S(1)} %get-tuple-element.129), channel_id=1, source_target_pairs={{0,33},{1,34},{2,35},{3,36},{4,37},{5,38},{6,39},{7,40},{8,41},{9,... | collective-permute-start | bytes 393224 | tf_op jit(solution)/shard_map/ppermute | solution.py:448
  229.4 8.8 %collective-permute-start.13 = (bf16[32,2048]{1,0:T(8,128)(2,1)S(1)}, bf16[32,2048]{1,0:T(8,128)(2,1)S(1)}, u32[]{:S(2)}, u32[]{:S(2)}) collective-permute-start(bf16[32,2048]{1,0:T(8,128)(2,1)S(1)} %get-tuple-element.130), channel_id=1, source_target_pairs={{1,32},{2,33},{3,34},{4,35},{5,36},{6,37},{7,38},{8,39},{9,40},{10... | collective-permute-start | bytes 393224 | tf_op jit(solution)/shard_map/ppermute | solution.py:449
  242.2 8.6 %collective-permute-start.15 = (bf16[32,2048]{1,0:T(8,128)(2,1)S(1)}, bf16[32,2048]{1,0:T(8,128)(2,1)S(1)}, u32[]{:S(2)}, u32[]{:S(2)}) collective-permute-start(bf16[32,2048]{1,0:T(8,128)(2,1)S(1)} %get-tuple-element.137), channel_id=1, source_target_pairs={{0,33},{1,34},{2,35},{3,36},{4,37},{5,38},{6,39},{7,40},{8,41},{9,... | collective-permute-start | bytes 393224 | tf_op jit(solution)/shard_map/ppermute | solution.py:448
  255.4 7.9 %collective-permute-start.18 = (bf16[32,2048]{1,0:T(8,128)(2,1)S(1)}, bf16[32,2048]{1,0:T(8,128)(2,1)S(1)}, u32[]{:S(2)}, u32[]{:S(2)}) collective-permute-start(bf16[32,2048]{1,0:T(8,128)(2,1)S(1)} %get-tuple-element.145), channel_id=1, source_target_pairs={{0,33},{1,34},{2,35},{3,36},{4,37},{5,38},{6,39},{7,40},{8,41},{9,... | collective-permute-start | bytes 393224 | tf_op jit(solution)/shard_map/ppermute | solution.py:448
  263.3 5.3 collective-permute-start.19
  271.9 9.1 %collective-permute-start.21 = (bf16[32,2048]{1,0:T(8,128)(2,1)S(1)}, bf16[32,2048]{1,0:T(8,128)(2,1)S(1)}, u32[]{:S(2)}, u32[]{:S(2)}) collective-permute-start(bf16[32,2048]{1,0:T(8,128)(2,1)S(1)} %get-tuple-element.153), channel_id=1, source_target_pairs={{0,33},{1,34},{2,35},{3,36},{4,37},{5,38},{6,39},{7,40},{8,41},{9,... | collective-permute-start | bytes 393224 | tf_op jit(solution)/shard_map/ppermute | solution.py:448
  281.0 7.0 %collective-permute-start.22 = (bf16[32,2048]{1,0:T(8,128)(2,1)S(1)}, bf16[32,2048]{1,0:T(8,128)(2,1)S(1)}, u32[]{:S(2)}, u32[]{:S(2)}) collective-permute-start(bf16[32,2048]{1,0:T(8,128)(2,1)S(1)} %get-tuple-element.154), channel_id=1, source_target_pairs={{1,32},{2,33},{3,34},{4,35},{5,36},{6,37},{7,38},{8,39},{9,40},{10... | collective-permute-start | bytes 393224 | tf_op jit(solution)/shard_map/ppermute | solution.py:449
  292.2 9.7 %collective-permute-start.24 = (bf16[32,2048]{1,0:T(8,128)(2,1)S(1)}, bf16[32,2048]{1,0:T(8,128)(2,1)S(1)}, u32[]{:S(2)}, u32[]{:S(2)}) collective-permute-start(bf16[32,2048]{1,0:T(8,128)(2,1)S(1)} %get-tuple-element.161), channel_id=1, source_target_pairs={{0,33},{1,34},{2,35},{3,36},{4,37},{5,38},{6,39},{7,40},{8,41},{9,... | collective-permute-start | bytes 393224 | tf_op jit(solution)/shard_map/ppermute | solution.py:448
  327.1 9.1 %collective-permute-done.30.gr_ref = bf16[32,2048]{1,0:T(8,128)(2,1)S(1)} collective-permute-done((bf16[32,2048]{1,0:T(8,128)(2,1)S(1)}, bf16[32,2048]{1,0:T(8,128)(2,1)S(1)}, u32[]{:S(2)}, u32[]{:S(2)}) %collective-permute-start.30) | collective-permute-done | bytes 131104 | tf_op jit(solution)/shard_map/ppermute | solution.py:449
  339.6 5.4 collective-permute-done.32.gl_ref
  345.0 9.8 %collective-permute-done.33.gr_ref = bf16[32,2048]{1,0:T(8,128)(2,1)S(1)} collective-permute-done((bf16[32,2048]{1,0:T(8,128)(2,1)S(1)}, bf16[32,2048]{1,0:T(8,128)(2,1)S(1)}, u32[]{:S(2)}, u32[]{:S(2)}) %collective-permute-start.33) | collective-permute-done | bytes 131104 | tf_op jit(solution)/shard_map/ppermute | solution.py:449
  368.0 7.5 %backward_layer.12 = (bf16[128,2048]{1,0:T(8,128)(2,1)S(1)}, bf16[32,2048]{1,0:T(8,128)(2,1)S(1)}, bf16[32,2048]{1,0:T(8,128)(2,1)S(1)}, bf16[2,128,2048]{2,1,0:T(8,128)(2,1)}) custom-call(s32[1]{0:T(128)S(6)} %sub.42.section_ref, bf16[2,192,2048]{2,1,0:T(8,128)(2,1)S(1)} %get-tuple-element.208.c0_ref, ...), custom_call_target="tpu_custom_call", output_to_operand_aliasing={{3}: (13, {})} | custom-call | tf_op jit(solution)/shard_map/backward_layer/pallas_call | solution.py:399
  405.4 5.4 collective-permute-done.44.gl_ref
  419.9 83.6 %collective-permute-done.47.gl_ref = bf16[32,2048]{1,0:T(8,128)(2,1)S(1)} collective-permute-done((bf16[32,2048]{1,0:T(8,128)(2,1)S(1)}, bf16[32,2048]{1,0:T(8,128)(2,1)S(1)}, u32[]{:S(2)}, u32[]{:S(2)}) %collective-permute-start.47) | collective-permute-done | bytes 131104 | tf_op jit(solution)/shard_map/ppermute | solution.py:448
  507.1 13.2 %backward_layer.16 = (bf16[128,2048]{1,0:T(8,128)(2,1)S(1)}, bf16[32,2048]{1,0:T(8,128)(2,1)S(1)}, bf16[32,2048]{1,0:T(8,128)(2,1)S(1)}, bf16[2,128,2048]{2,1,0:T(8,128)(2,1)}) custom-call(s32[1]{0:T(128)S(6)} %sub.42.section_ref, bf16[2,192,2048]{2,1,0:T(8,128)(2,1)S(1)} %get-tuple-element.208.c0_ref, ...), custom_call_target="tpu_custom_call", output_to_operand_aliasing={{3}: (13, {})} | custom-call | tf_op jit(solution)/shard_map/backward_layer/pallas_call | solution.py:399
  524.2 6.0 %collective-permute-done.50.gl_ref = bf16[32,2048]{1,0:T(8,128)(2,1)S(1)} collective-permute-done((bf16[32,2048]{1,0:T(8,128)(2,1)S(1)}, bf16[32,2048]{1,0:T(8,128)(2,1)S(1)}, u32[]{:S(2)}, u32[]{:S(2)}) %collective-permute-start.50) | collective-permute-done | bytes 131104 | tf_op jit(solution)/shard_map/ppermute | solution.py:448
  534.3 12.5 %backward_layer.17 = (bf16[128,2048]{1,0:T(8,128)(2,1)}, bf16[32,2048]{1,0:T(8,128)(2,1)}, bf16[32,2048]{1,0:T(8,128)(2,1)}, bf16[2,128,2048]{2,1,0:T(8,128)(2,1)}) custom-call(s32[1]{0:T(128)S(6)} %sub.42.section_ref, bf16[2,192,2048]{2,1,0:T(8,128)(2,1)S(1)} %get-tuple-element.208.c0_ref, ...), custom_call_target="tpu_custom_call", output_to_operand_aliasing={{3}: (13, {})} | custom-call | tf_op jit(solution)/shard_map/backward_layer/pallas_call | solution.py:399
  (156 shorter events, 154.4 us)
Async XLA Ops:
  7.2 148.5 %all-gather.3.cloned.1.call-start = ((), (), s32[]{:S(2)}) async-start(), calls=%async_computation | async-start | bytes 17301504 | tf_op jit(solution)/shard_map/all_gather | solution.py:491
  14.1 20.2 %collective-permute-start = (bf16[144,2048]{1,0:T(8,128)(2,1)S(1)}, bf16[144,2048]{1,0:T(8,128)(2,1)}, u32[]{:S(2)}, u32[]{:S(2)}) collective-permute-start(bf16[144,2048]{1,0:T(8,128)(2,1)S(1)} %fusion.2), channel_id=1, source_target_pairs={{0,1},{1,2},{2,3},{3,4},{4,5},{5,6},{6,7},{7,8},{8,9},{9,10},{10,1... | collective-permute-start | bytes 1769480 | tf_op jit(solution)/shard_map/ppermute | solution.py:457
  17.3 23.7 %collective-permute-start.1 = (bf16[144,2048]{1,0:T(8,128)(2,1)S(1)}, bf16[144,2048]{1,0:T(8,128)(2,1)}, u32[]{:S(2)}, u32[]{:S(2)}) collective-permute-start(bf16[144,2048]{1,0:T(8,128)(2,1)S(1)} %fusion.3), channel_id=1, source_target_pairs={{1,0},{2,1},{3,2},{4,3},{5,4},{6,5},{7,6},{8,7},{9,8},{10,9},{11,1... | collective-permute-start | bytes 1769480 | tf_op jit(solution)/shard_map/ppermute | solution.py:458
  198.1 22.4 %collective-permute-start.8 = (bf16[128,2048]{1,0:T(8,128)(2,1)S(1)}, bf16[128,2048]{1,0:T(8,128)(2,1)S(1)}, u32[]{:S(2)}, u32[]{:S(2)}) collective-permute-start(bf16[128,2048]{1,0:T(8,128)(2,1)S(1)} %get-tuple-element.120), channel_id=1, source_target_pairs={{32,64},{33,65},{34,66},{35,67},{36,68},{37,69},{38,70},{39,71},{4... | collective-permute-start | bytes 1572872 | tf_op jit(solution)/shard_map/ppermute | solution.py:447
  198.8 19.8 %collective-permute-start.9 = (bf16[32,2048]{1,0:T(8,128)(2,1)S(1)}, bf16[32,2048]{1,0:T(8,128)(2,1)S(1)}, u32[]{:S(2)}, u32[]{:S(2)}) collective-permute-start(bf16[32,2048]{1,0:T(8,128)(2,1)S(1)} %get-tuple-element.121), channel_id=1, source_target_pairs={{0,33},{1,34},{2,35},{3,36},{4,37},{5,38},{6,39},{7,40},{8,41},{9,... | collective-permute-start | bytes 393224 | tf_op jit(solution)/shard_map/ppermute | solution.py:448
  221.1 20.3 %collective-permute-start.11 = (bf16[128,2048]{1,0:T(8,128)(2,1)S(1)}, bf16[128,2048]{1,0:T(8,128)(2,1)S(1)}, u32[]{:S(2)}, u32[]{:S(2)}) collective-permute-start(bf16[128,2048]{1,0:T(8,128)(2,1)S(1)} %get-tuple-element.128), channel_id=1, source_target_pairs={{64,96},{65,97},{66,98},{67,99},{68,100},{69,101},{70,102},{71,103... | collective-permute-start | bytes 1572872 | tf_op jit(solution)/shard_map/ppermute | solution.py:447
  221.8 16.4 %collective-permute-start.12 = (bf16[32,2048]{1,0:T(8,128)(2,1)S(1)}, bf16[32,2048]{1,0:T(8,128)(2,1)S(1)}, u32[]{:S(2)}, u32[]{:S(2)}) collective-permute-start(bf16[32,2048]{1,0:T(8,128)(2,1)S(1)} %get-tuple-element.129), channel_id=1, source_target_pairs={{0,33},{1,34},{2,35},{3,36},{4,37},{5,38},{6,39},{7,40},{8,41},{9,... | collective-permute-start | bytes 393224 | tf_op jit(solution)/shard_map/ppermute | solution.py:448
  254.7 16.3 %collective-permute-start.17 = (bf16[128,2048]{1,0:T(8,128)(2,1)S(1)}, bf16[128,2048]{1,0:T(8,128)(2,1)S(1)}, u32[]{:S(2)}, u32[]{:S(2)}) collective-permute-start(bf16[128,2048]{1,0:T(8,128)(2,1)S(1)} %get-tuple-element.144), channel_id=1, source_target_pairs={{128,160},{129,161},{130,162},{131,163},{132,164},{133,165},{134,1... | collective-permute-start | bytes 1572872 | tf_op jit(solution)/shard_map/ppermute | solution.py:447
  255.4 13.1 %collective-permute-start.18 = (bf16[32,2048]{1,0:T(8,128)(2,1)S(1)}, bf16[32,2048]{1,0:T(8,128)(2,1)S(1)}, u32[]{:S(2)}, u32[]{:S(2)}) collective-permute-start(bf16[32,2048]{1,0:T(8,128)(2,1)S(1)} %get-tuple-element.145), channel_id=1, source_target_pairs={{0,33},{1,34},{2,35},{3,36},{4,37},{5,38},{6,39},{7,40},{8,41},{9,... | collective-permute-start | bytes 393224 | tf_op jit(solution)/shard_map/ppermute | solution.py:448
  271.2 20.2 %collective-permute-start.20 = (bf16[128,2048]{1,0:T(8,128)(2,1)S(1)}, bf16[128,2048]{1,0:T(8,128)(2,1)S(1)}, u32[]{:S(2)}, u32[]{:S(2)}) collective-permute-start(bf16[128,2048]{1,0:T(8,128)(2,1)S(1)} %get-tuple-element.152), channel_id=1, source_target_pairs={{160,192},{161,193},{162,194},{163,195},{164,196},{165,197},{166,1... | collective-permute-start | bytes 1572872 | tf_op jit(solution)/shard_map/ppermute | solution.py:447
  271.9 16.2 %collective-permute-start.21 = (bf16[32,2048]{1,0:T(8,128)(2,1)S(1)}, bf16[32,2048]{1,0:T(8,128)(2,1)S(1)}, u32[]{:S(2)}, u32[]{:S(2)}) collective-permute-start(bf16[32,2048]{1,0:T(8,128)(2,1)S(1)} %get-tuple-element.153), channel_id=1, source_target_pairs={{0,33},{1,34},{2,35},{3,36},{4,37},{5,38},{6,39},{7,40},{8,41},{9,... | collective-permute-start | bytes 393224 | tf_op jit(solution)/shard_map/ppermute | solution.py:448
  291.5 14.7 %collective-permute-start.23 = (bf16[128,2048]{1,0:T(8,128)(2,1)S(1)}, bf16[128,2048]{1,0:T(8,128)(2,1)S(1)}, u32[]{:S(2)}, u32[]{:S(2)}) collective-permute-start(bf16[128,2048]{1,0:T(8,128)(2,1)S(1)} %get-tuple-element.160), channel_id=1, source_target_pairs={{192,224},{193,225},{194,226},{195,227},{196,228},{197,229},{198,2... | collective-permute-start | bytes 1572872 | tf_op jit(solution)/shard_map/ppermute | solution.py:447
  318.8 17.4 %collective-permute-start.28 = (bf16[128,2048]{1,0:T(8,128)(2,1)S(1)}, bf16[128,2048]{1,0:T(8,128)(2,1)S(1)}, u32[]{:S(2)}, u32[]{:S(2)}) collective-permute-start(bf16[128,2048]{1,0:T(8,128)(2,1)S(1)} %get-tuple-element.173), channel_id=1, source_target_pairs={{224,192},{225,193},{226,194},{227,195},{228,196},{229,197},{230,1... | collective-permute-start | bytes 1572872 | tf_op jit(solution)/shard_map/ppermute | solution.py:447
  320.8 15.4 %collective-permute-start.30 = (bf16[32,2048]{1,0:T(8,128)(2,1)S(1)}, bf16[32,2048]{1,0:T(8,128)(2,1)S(1)}, u32[]{:S(2)}, u32[]{:S(2)}) collective-permute-start(bf16[32,2048]{1,0:T(8,128)(2,1)S(1)} %get-tuple-element.175), channel_id=1, source_target_pairs={{33,0},{34,1},{35,2},{36,3},{37,4},{38,5},{39,6},{40,7},{41,8},{42... | collective-permute-start | bytes 393224 | tf_op jit(solution)/shard_map/ppermute | solution.py:449
  336.3 18.5 %collective-permute-start.31 = (bf16[128,2048]{1,0:T(8,128)(2,1)S(1)}, bf16[128,2048]{1,0:T(8,128)(2,1)S(1)}, u32[]{:S(2)}, u32[]{:S(2)}) collective-permute-start(bf16[128,2048]{1,0:T(8,128)(2,1)S(1)} %get-tuple-element.177), channel_id=1, source_target_pairs={{192,160},{193,161},{194,162},{195,163},{196,164},{197,165},{198,1... | collective-permute-start | bytes 1572872 | tf_op jit(solution)/shard_map/ppermute | solution.py:447
  338.3 16.5 %collective-permute-start.33 = (bf16[32,2048]{1,0:T(8,128)(2,1)S(1)}, bf16[32,2048]{1,0:T(8,128)(2,1)S(1)}, u32[]{:S(2)}, u32[]{:S(2)}) collective-permute-start(bf16[32,2048]{1,0:T(8,128)(2,1)S(1)} %get-tuple-element.179), channel_id=1, source_target_pairs={{33,0},{34,1},{35,2},{36,3},{37,4},{38,5},{39,6},{40,7},{41,8},{42... | collective-permute-start | bytes 393224 | tf_op jit(solution)/shard_map/ppermute | solution.py:449
  354.9 13.1 %collective-permute-start.34 = (bf16[128,2048]{1,0:T(8,128)(2,1)S(1)}, bf16[128,2048]{1,0:T(8,128)(2,1)S(1)}, u32[]{:S(2)}, u32[]{:S(2)}) collective-permute-start(bf16[128,2048]{1,0:T(8,128)(2,1)S(1)} %get-tuple-element.181), channel_id=1, source_target_pairs={{160,128},{161,129},{162,130},{163,131},{164,132},{165,133},{166,1... | collective-permute-start | bytes 1572872 | tf_op jit(solution)/shard_map/ppermute | solution.py:447
  375.6 13.1 %collective-permute-start.37 = (bf16[128,2048]{1,0:T(8,128)(2,1)S(1)}, bf16[128,2048]{1,0:T(8,128)(2,1)S(1)}, u32[]{:S(2)}, u32[]{:S(2)}) collective-permute-start(bf16[128,2048]{1,0:T(8,128)(2,1)S(1)} %get-tuple-element.185), channel_id=1, source_target_pairs={{128,96},{129,97},{130,98},{131,99},{132,100},{133,101},{134,102},... | collective-permute-start | bytes 1572872 | tf_op jit(solution)/shard_map/ppermute | solution.py:447
  388.8 13.1 %collective-permute-start.40 = (bf16[128,2048]{1,0:T(8,128)(2,1)S(1)}, bf16[128,2048]{1,0:T(8,128)(2,1)S(1)}, u32[]{:S(2)}, u32[]{:S(2)}) collective-permute-start(bf16[128,2048]{1,0:T(8,128)(2,1)S(1)} %get-tuple-element.189), channel_id=1, source_target_pairs={{96,64},{97,65},{98,66},{99,67},{100,68},{101,69},{102,70},{103,71... | collective-permute-start | bytes 1572872 | tf_op jit(solution)/shard_map/ppermute | solution.py:447
  402.1 13.7 %collective-permute-start.43 = (bf16[128,2048]{1,0:T(8,128)(2,1)S(1)}, bf16[128,2048]{1,0:T(8,128)(2,1)S(1)}, u32[]{:S(2)}, u32[]{:S(2)}) collective-permute-start(bf16[128,2048]{1,0:T(8,128)(2,1)S(1)} %get-tuple-element.193), channel_id=1, source_target_pairs={{64,32},{65,33},{66,34},{67,35},{68,36},{69,37},{70,38},{71,39},{7... | collective-permute-start | bytes 1572872 | tf_op jit(solution)/shard_map/ppermute | solution.py:447
  416.0 91.2 %collective-permute-start.46 = (bf16[128,2048]{1,0:T(8,128)(2,1)S(1)}, bf16[128,2048]{1,0:T(8,128)(2,1)S(1)}, u32[]{:S(2)}, u32[]{:S(2)}) collective-permute-start(bf16[128,2048]{1,0:T(8,128)(2,1)S(1)} %get-tuple-element.197), channel_id=1, source_target_pairs={{32,0},{33,1},{34,2},{35,3},{36,4},{37,5},{38,6},{39,7},{40,8},{41... | collective-permute-start | bytes 1572872 | tf_op jit(solution)/shard_map/ppermute | solution.py:447
  417.3 86.2 %collective-permute-start.47 = (bf16[32,2048]{1,0:T(8,128)(2,1)S(1)}, bf16[32,2048]{1,0:T(8,128)(2,1)S(1)}, u32[]{:S(2)}, u32[]{:S(2)}) collective-permute-start(bf16[32,2048]{1,0:T(8,128)(2,1)S(1)} %get-tuple-element.198), channel_id=1, source_target_pairs={{32,1},{33,2},{34,3},{35,4},{36,5},{37,6},{38,7},{39,8},{40,9},{41... | collective-permute-start | bytes 393224 | tf_op jit(solution)/shard_map/ppermute | solution.py:448
  418.6 88.5 %collective-permute-start.48 = (bf16[32,2048]{1,0:T(8,128)(2,1)S(1)}, bf16[32,2048]{1,0:T(8,128)(2,1)S(1)}, u32[]{:S(2)}, u32[]{:S(2)}) collective-permute-start(bf16[32,2048]{1,0:T(8,128)(2,1)S(1)} %get-tuple-element.199), channel_id=1, source_target_pairs={{33,0},{34,1},{35,2},{36,3},{37,4},{38,5},{39,6},{40,7},{41,8},{42... | collective-permute-start | bytes 393224 | tf_op jit(solution)/shard_map/ppermute | solution.py:449
  520.3 14.0 %collective-permute-start.49 = (bf16[128,2048]{1,0:T(8,128)(2,1)S(1)}, bf16[128,2048]{1,0:T(8,128)(2,1)S(1)}, u32[]{:S(2)}, u32[]{:S(2)}) collective-permute-start(bf16[128,2048]{1,0:T(8,128)(2,1)S(1)} %get-tuple-element.201), channel_id=1, source_target_pairs={{32,0},{33,1},{34,2},{35,3},{36,4},{37,5},{38,6},{39,7},{40,8},{41... | collective-permute-start | bytes 1572872 | tf_op jit(solution)/shard_map/ppermute | solution.py:447
  (35 other events, 266.2 us)
Sparse Core Ops, SparseCore 0:
  12.7 142.9 all-gather.2

commit v4 on v3

--- a/solution.py
+++ b/solution.py
@@ -186,14 +186,24 @@
     return jax.ShapeDtypeStruct(a.shape, a.dtype)
 
 
-def forward_call(step, position, x0, x, xl, xr, mask, w, saved):
+def fresh(body, position, count):
+    def wrapped(*refs):
+        return body(*refs[:position], *([None] * count), *refs[position:])
+
+    return wrapped
+
+
+def forward_call(step, position, x0, x, xl, xr, mask, w, saved, kinds):
     rows = jax.ShapeDtypeStruct((ROWS, D), BF16)
     edge = jax.ShapeDtypeStruct((BLK, D), BF16)
+    body = functools.partial(forward_body, step)
+    if not saved:
+        body = fresh(body, 7, len(kinds))
     outs = pl.pallas_call(
-        functools.partial(forward_body, step),
+        body,
         name="forward_layer",
-        out_shape=(rows, edge, edge) + tuple(shape_of(a) for a in saved),
-        in_specs=spaces(*"saaaaavaaaaa"),
+        out_shape=(rows, edge, edge) + kinds,
+        in_specs=spaces(*("saaaaav" + "a" * len(saved))),
         out_specs=spaces(*"aaaaaaaa"),
         scratch_shapes=[
             pltpu.VMEM((EXT, D), BF16),
@@ -207,7 +217,7 @@
             pltpu.SemaphoreType.DMA((4,)),
             pltpu.SemaphoreType.DMA((8,)),
         ],
-        input_output_aliases={7: 3, 8: 4, 9: 5, 10: 6, 11: 7},
+        input_output_aliases={7 + i: 3 + i for i in range(len(saved))},
         compiler_params=pltpu.CompilerParams(vmem_limit_bytes=VMEM_LIMIT),
     )(position, x0, x, xl, xr, mask, w, *saved)
     return outs[:3], outs[3:]
@@ -226,7 +236,7 @@
         in_specs=spaces("a"),
         out_specs=pl.BlockSpec(memory_space=pltpu.VMEM),
         scratch_shapes=[pltpu.SemaphoreType.DMA],
-        compiler_params=pltpu.CompilerParams(vmem_limit_bytes=20 << 20),
+        compiler_params=pltpu.CompilerParams(vmem_limit_bytes=40 << 20),
     )(g)
 
 
@@ -241,8 +251,10 @@
     w_ref,
     xs_ref,
     qa_ref,
-    qal_ref,
-    qar_ref,
+    qal0_ref,
+    qar0_ref,
+    qal1_ref,
+    qar1_ref,
     kv_ref,
     rr_ref,
     grad_in,
@@ -273,9 +285,7 @@
             pltpu.make_async_copy(source.at[slot], target, sem_save.at[index])
             for index, (source, target) in enumerate(
                 (
-                    (qal_ref, qa.at[:BLK]),
                     (qa_ref, qa.at[own]),
-                    (qar_ref, qa.at[BLK + ROWS :]),
                     (kv_ref, kv),
                     (rr_ref, rr),
                     (xs_ref, xs),
@@ -283,6 +293,22 @@
                 )
             )
         ]
+
+        def ends(left, right):
+            return [
+                pltpu.make_async_copy(left, qa.at[:BLK], sem_save.at[5]),
+                pltpu.make_async_copy(right, qa.at[BLK + ROWS :], sem_save.at[6]),
+            ]
+
+        @pl.when(slot == 0)
+        def _():
+            for copy in ends(qal0_ref, qar0_ref):
+                copy.start()
+
+        @pl.when(slot == 1)
+        def _():
+            for copy in ends(qal1_ref, qar1_ref):
+                copy.start()
 
         @pl.when(last)
         def _():
@@ -306,7 +332,7 @@
             for copy in copies:
                 copy.wait()
 
-        for load in loads:
+        for load in loads + ends(qal0_ref, qar0_ref):
             load.wait()
 
         @pl.loop(0, 2)
@@ -393,14 +419,18 @@
             copy.wait()
 
 
-def backward_call(step, position, c0, g, gl, gr, mask, w, xs, qa, qal, qar, kv, rr, grads):
+def backward_call(step, position, c0, g, gl, gr, mask, w, xs, qa, ends, kv, rr, grads, kind):
     rows = jax.ShapeDtypeStruct((ROWS, D), BF16)
     edge = jax.ShapeDtypeStruct((BLK, D), BF16)
+    body = functools.partial(backward_body, step)
+    carried = () if grads is None else (grads,)
+    if not carried:
+        body = fresh(body, 15, 1)
     outs = pl.pallas_call(
-        functools.partial(backward_body, step),
+        body,
         name="backward_layer",
-        out_shape=(rows, edge, edge, shape_of(grads)),
-        in_specs=spaces(*"saaaaavaaaaaaa"),
+        out_shape=(rows, edge, edge, kind),
+        in_specs=spaces(*("saaaaav" + "a" * (8 + len(carried)))),
         out_specs=spaces(*"aaaa"),
         scratch_shapes=[
             pltpu.VMEM((EXT, D), BF16),
@@ -417,10 +447,40 @@
             pltpu.SemaphoreType.DMA((7,)),
             pltpu.SemaphoreType.DMA((4,)),
         ],
-        input_output_aliases={13: 3},
+        input_output_aliases={15: 3} if carried else {},
         compiler_params=pltpu.CompilerParams(vmem_limit_bytes=VMEM_LIMIT),
-    )(position, c0, g, gl, gr, mask, w, xs, qa, qal, qar, kv, rr, grads)
+    )(position, c0, g, gl, gr, mask, w, xs, qa, *ends, kv, rr, *carried)
     return outs[:3], outs[3]
+
+
+def pack_body(wq_ref, wk_ref, wv_ref, wo_ref, out_ref, sem):
+    copies = [
+        pltpu.make_async_copy(source, target, sem.at[index])
+        for index, (source, target) in enumerate(
+            (
+                (wq_ref.at[0], out_ref.at[0:64]),
+                (wk_ref.at[0], out_ref.at[64:128]),
+                (wv_ref.at[0], out_ref.at[128:192]),
+                (wo_ref.at[0, :, :WIDTH], out_ref.at[192:224]),
+                (wo_ref.at[0, :, WIDTH:], out_ref.at[224:256]),
+            )
+        )
+    ]
+    for copy in copies:
+        copy.start()
+    for copy in copies:
+        copy.wait()
+
+
+def pack_call(*weights):
+    return pl.pallas_call(
+        pack_body,
+        name="pack_weights",
+        out_shape=jax.ShapeDtypeStruct((256, WIDTH), BF16),
+        in_specs=spaces(*"aaaa"),
+        out_specs=pl.BlockSpec(memory_space=pltpu.HBM),
+        scratch_shapes=[pltpu.SemaphoreType.DMA((5,))],
+    )(*weights)
 
 BOTH = ("section", "ctx")
 
@@ -485,9 +545,7 @@
     micro = section_input.shape[0]
     steps = n_section + micro - 1
 
-    shard = jnp.concatenate(
-        [w_query[0], w_key[0], w_value[0], w_out[0][:, :WIDTH], w_out[0][:, WIDTH:]], axis=0
-    )
+    shard = pack_call(w_query, w_key, w_value, w_out)
     gathered = lax.all_gather(shard, "ctx", axis=0, tiled=False)
     position = jnp.full((1,), section, jnp.int32)
     reverse = n_section - 1 - position
@@ -515,47 +573,49 @@
     forward_mask = mask[:, BLK : BLK + ROWS]
     weights = load_call(gathered)
 
-    saved = (
-        jnp.zeros((micro, ROWS, D), BF16),
-        jnp.zeros((micro, ROWS, D), BF16),
-        jnp.zeros((micro, ROWS, PACK), BF16),
-        jnp.zeros((micro, EXT, 2 * WIDTH), BF16),
-        jnp.zeros((micro, ROWS, 128), F32),
+    kinds = (
+        jax.ShapeDtypeStruct((micro, ROWS, D), BF16),
+        jax.ShapeDtypeStruct((micro, ROWS, D), BF16),
+        jax.ShapeDtypeStruct((micro, ROWS, PACK), BF16),
+        jax.ShapeDtypeStruct((micro, EXT, 2 * WIDTH), BF16),
+        jax.ShapeDtypeStruct((micro, ROWS, 128), F32),
     )
     zero_rows = jnp.zeros((ROWS, D), BF16)
     zero_edge = jnp.zeros((BLK, D), BF16)
     incoming = (zero_rows, zero_edge, zero_edge)
-    for step in range(steps):
+
+    def forward(step, incoming, saved):
         parts, saved = forward_call(
-            step, position, extended[0], *incoming, forward_mask, weights, saved
+            step, position, extended[0], *incoming, forward_mask, weights, saved, kinds
         )
         senders = [s for s in range(step - micro + 1, step + 1) if 0 <= s < n_section - 1]
         if senders:
             incoming = relay(parts, senders, 1, n_section, n_ctx)
-    xs, outputs, qa, kv, rr = saved
-    qa_left, qa_right = edges(qa, 1, BLK, n_ctx)
-    grads = jnp.zeros((micro, ROWS, D), BF16)
-    incoming = (zero_rows, zero_edge, zero_edge)
-    for step in range(steps):
+        return incoming, saved
+
+    def backward(step, incoming, saved, ends, grads):
+        xs, _, qa, kv, rr = saved
         parts, grads = backward_call(
-            step,
-            reverse,
-            extended[1],
-            *incoming,
-            mask,
-            weights,
-            xs,
-            qa,
-            qa_left,
-            qa_right,
-            kv,
-            rr,
-            grads,
+            step, reverse, extended[1], *incoming, mask, weights, xs, qa, ends, kv, rr, grads, kinds[0]
         )
         top = n_section - 1 - step
         senders = [s for s in range(top, top + micro) if 0 < s < n_section]
         if senders:
             incoming = relay(parts, senders, -1, n_section, n_ctx)
+        return incoming, grads
+
+    saved = ()
+    for step in range(n_section):
+        incoming, saved = forward(step, incoming, saved)
+    ends = edges(saved[2][0], 0, BLK, n_ctx)
+    pulled, grads = backward(0, (zero_rows, zero_edge, zero_edge), saved, ends * 2, None)
+    saved, grads = lax.optimization_barrier((saved, grads))
+    for step in range(n_section, steps):
+        incoming, saved = forward(step, incoming, saved)
+    ends = ends + edges(saved[2][1], 0, BLK, n_ctx)
+    for step in range(1, steps):
+        pulled, grads = backward(step, pulled, saved, ends, grads)
+    outputs = saved[1]
     return (outputs[None], grads[None])
 
 

time: 564 us -> 563 us (level)
  Pallas kernels: 51.9 us -> 65.8 us
  local copies, waits for them, and re-layouts: 18.2 us -> 4.69 us
  waiting for transfers between devices: 325 us -> 314 us
  starting transfers between devices: 141 us -> 150 us
    ppermute x16, waiting for transfers between devices: 62.4 us -> 48.7 us  [relay(): from_right = lax.ppermute(left, BOTH, diagonal(n_section, step, n_ctx, -1))]
    unnamed x16 -> x8, local copies, waits for them, and re-layouts: 10.9 us -> 0.02 us
    ppermute x16, waiting for transfers between devices: 127 us -> 137 us  [relay(): from_left = lax.ppermute(right, BOTH, diagonal(n_section, step, n_ctx, 1))]
    pallas_call x18 -> x19, Pallas kernels: 50.7 us -> 60 us  [the longest x9 26.4 us: backward_call(): pl.pallas_call(body, name='backward_layer', out_shape=(rows, edge, edge,...]
    ppermute x2 -> x3, starting transfers between devices: 7.08 us -> 11.3 us  [edges(): from_left = lax.ppermute(tail, 'ctx', neighbours(n_ctx, 1))]
    ppermute x2 -> x3, waiting for transfers between devices: 16.5 us -> 14 us  [edges(): from_left = lax.ppermute(tail, 'ctx', neighbours(n_ctx, 1))]
  transfers between devices with their start and end apart: 53 -> 55, of which waited for: 34 -> 32; matrix products, arithmetic and copies ran while one was open for 1% -> 2% of each run, Pallas kernels for 0% -> 0%
where the time goes in v4:
time: 563 us; the launch traced here: 554 us
  waiting for transfers between devices  314 us (56%)
  starting transfers between devices  150 us (27%)
  Pallas kernels  65.8 us (12%)
  between operations  15.3 us (3%)
    ppermute x16, waiting for transfers between devices, relay(): from_left = lax.ppermute(right, BOTH, diagonal(n_section, step, n_ctx, 1))  137 us
    all_gather x1, waiting for transfers between devices, per_device(): gathered = lax.all_gather(shard, 'ctx', axis=0, tiled=False)  108 us
    ppermute x16, starting transfers between devices, relay(): from_left = lax.ppermute(right, BOTH, diagonal(n_section, step, n_ctx, 1))  78.1 us
    ppermute x16, waiting for transfers between devices, relay(): from_right = lax.ppermute(left, BOTH, diagonal(n_section, step, n_ctx, -1))  48.7 us
    ppermute x16, starting transfers between devices, relay(): from_right = lax.ppermute(left, BOTH, diagonal(n_section, step, n_ctx, -1))  37.9 us
    pallas_call x9, Pallas kernels, backward_call(): pl.pallas_call(body, name='backward_layer', out_shape=(rows, edge, edge,...  26.4 us
    pallas_call x1, Pallas kernels, pack_call(): pl.pallas_call(pack_body, name='pack_weights', out_shape=jax.ShapeDtypeSt...  17 us
    pallas_call x9, Pallas kernels, forward_call(): pl.pallas_call(body, name='forward_layer', out_shape=(rows, edge, edge) +...  16.5 us
  transfers between devices with their start and end apart: 55, of which 32 were waited for; matrix products, arithmetic and copies ran while one was open for 2% of the time, Pallas kernels for 0%

profile of v4, /device:TPU:100, one launch (start us, length us, event | category | flops | bytes accessed | tf_op | source)
XLA Modules:
  0.0 553.6 jit_solution(9117105139222385659)
XLA Ops:
  7.2 17.0 %pack_weights.1 = bf16[256,1024]{1,0:T(8,128)(2,1)} custom-call(bf16[1,64,1024]{2,1,0:T(8,128)(2,1)} %wq_ref.1, bf16[1,64,1024]{2,1,0:T(8,128)(2,1)} %wk_ref.1, bf16[1,64,1024]{2,1,0:T(8,128)(2,1)} %wv_ref.1, bf16[1,32,2048]{2,1,0:T(8,128)(2,1)} %wo_ref.1), custom_call_target="tpu_custom_call" | custom-call | tf_op jit(solution)/shard_map/pack_weights/pallas_call | solution.py:476
  32.0 14.0 %collective-permute-done = bf16[144,2048]{1,0:T(8,128)(2,1)} collective-permute-done((bf16[144,2048]{1,0:T(8,128)(2,1)S(1)}, bf16[144,2048]{1,0:T(8,128)(2,1)}, u32[]{:S(2)}, u32[]{:S(2)}) %collective-permute-start) | collective-permute-done | bytes 589856 | tf_op jit(solution)/shard_map/ppermute | solution.py:517
  46.8 6.0 %collective-permute-done.1 = bf16[144,2048]{1,0:T(8,128)(2,1)} collective-permute-done((bf16[144,2048]{1,0:T(8,128)(2,1)S(1)}, bf16[144,2048]{1,0:T(8,128)(2,1)}, u32[]{:S(2)}, u32[]{:S(2)}) %collective-permute-start.1) | collective-permute-done | bytes 589856 | tf_op jit(solution)/shard_map/ppermute | solution.py:518
  59.2 108.3 %all-gather.3.cloned.1.call-done = bf16[8192,1024]{1,0:T(8,128)(2,1)} async-done(((bf16[256,1024]{1,0:T(8,128)(2,1)}), bf16[8192,1024]{1,0:T(8,128)(2,1)}) %all-gather.3.cloned.1.call-update) | async-done | bytes 16777232 | tf_op jit(solution)/shard_map/all_gather | solution.py:549
  167.4 5.8 %load_weights.1.refs_6_.w_ref = bf16[32,256,1024]{2,1,0:T(8,128)(2,1)S(1)} custom-call(bf16[32,256,1024]{2,1,0:T(8,128)(2,1)} %bitcast.32), custom_call_target="tpu_custom_call" | custom-call | tf_op jit(solution)/shard_map/load_weights/pallas_call | solution.py:232
  173.3 7.7 %forward_layer.9 = (bf16[128,2048]{1,0:T(8,128)(2,1)S(1)}, bf16[32,2048]{1,0:T(8,128)(2,1)S(1)}, bf16[32,2048]{1,0:T(8,128)(2,1)S(1)}, bf16[2,128,2048]{2,1,0:T(...) custom-call(s32[1]{0:T(128)} %bitcast.refs_0_.section_ref, ...), custom_call_target="tpu_custom_call" | custom-call | tf_op jit(solution)/shard_map/forward_layer/pallas_call | solution.py:202
  187.5 7.7 %forward_layer.10 = (bf16[128,2048]{1,0:T(8,128)(2,1)S(1)}, bf16[32,2048]{1,0:T(8,128)(2,1)S(1)}, bf16[32,2048]{1,0:T(8,128)(2,1)S(1)}, bf16[2,128,2048]{2,1,0:T...) custom-call(s32[1]{0:T(128)} %bitcast.refs_0_.section_ref, ...), custom_call_target="tpu_custom_call", output_to_operand_aliasing={{3}: (7, {}), {4}: (8, {}), {5}: (9, {}), {6}: (10, {}), {7... | custom-call | tf_op jit(solution)/shard_map/forward_layer/pallas_call | solution.py:202
  207.3 16.8 %collective-permute-start.9 = (bf16[32,2048]{1,0:T(8,128)(2,1)S(1)}, bf16[32,2048]{1,0:T(8,128)(2,1)S(1)}, u32[]{:S(2)}, u32[]{:S(2)}) collective-permute-start(bf16[32,2048]{1,0:T(8,128)(2,1)S(1)} %get-tuple-element.127), channel_id=1, source_target_pairs={{0,33},{1,34},{2,35},{3,36},{4,37},{5,38},{6,39},{7,40},{8,41},{9,... | collective-permute-start | bytes 393224 | tf_op jit(solution)/shard_map/ppermute | solution.py:508
  229.8 7.6 %collective-permute-start.12 = (bf16[32,2048]{1,0:T(8,128)(2,1)S(1)}, bf16[32,2048]{1,0:T(8,128)(2,1)S(1)}, u32[]{:S(2)}, u32[]{:S(2)}) collective-permute-start(bf16[32,2048]{1,0:T(8,128)(2,1)S(1)} %get-tuple-element.135), channel_id=1, source_target_pairs={{0,33},{1,34},{2,35},{3,36},{4,37},{5,38},{6,39},{7,40},{8,41},{9,... | collective-permute-start | bytes 393224 | tf_op jit(solution)/shard_map/ppermute | solution.py:508
  237.4 8.8 %collective-permute-start.13 = (bf16[32,2048]{1,0:T(8,128)(2,1)S(1)}, bf16[32,2048]{1,0:T(8,128)(2,1)S(1)}, u32[]{:S(2)}, u32[]{:S(2)}) collective-permute-start(bf16[32,2048]{1,0:T(8,128)(2,1)S(1)} %get-tuple-element.136), channel_id=1, source_target_pairs={{1,32},{2,33},{3,34},{4,35},{5,36},{6,37},{7,38},{8,39},{9,40},{10... | collective-permute-start | bytes 393224 | tf_op jit(solution)/shard_map/ppermute | solution.py:509
  250.5 8.7 %collective-permute-start.15 = (bf16[32,2048]{1,0:T(8,128)(2,1)S(1)}, bf16[32,2048]{1,0:T(8,128)(2,1)S(1)}, u32[]{:S(2)}, u32[]{:S(2)}) collective-permute-start(bf16[32,2048]{1,0:T(8,128)(2,1)S(1)} %get-tuple-element.143), channel_id=1, source_target_pairs={{0,33},{1,34},{2,35},{3,36},{4,37},{5,38},{6,39},{7,40},{8,41},{9,... | collective-permute-start | bytes 393224 | tf_op jit(solution)/shard_map/ppermute | solution.py:508
  263.8 7.9 %collective-permute-start.18 = (bf16[32,2048]{1,0:T(8,128)(2,1)S(1)}, bf16[32,2048]{1,0:T(8,128)(2,1)S(1)}, u32[]{:S(2)}, u32[]{:S(2)}) collective-permute-start(bf16[32,2048]{1,0:T(8,128)(2,1)S(1)} %get-tuple-element.151), channel_id=1, source_target_pairs={{0,33},{1,34},{2,35},{3,36},{4,37},{5,38},{6,39},{7,40},{8,41},{9,... | collective-permute-start | bytes 393224 | tf_op jit(solution)/shard_map/ppermute | solution.py:508
  280.2 9.2 %collective-permute-start.21 = (bf16[32,2048]{1,0:T(8,128)(2,1)S(1)}, bf16[32,2048]{1,0:T(8,128)(2,1)S(1)}, u32[]{:S(2)}, u32[]{:S(2)}) collective-permute-start(bf16[32,2048]{1,0:T(8,128)(2,1)S(1)} %get-tuple-element.159), channel_id=1, source_target_pairs={{0,33},{1,34},{2,35},{3,36},{4,37},{5,38},{6,39},{7,40},{8,41},{9,... | collective-permute-start | bytes 393224 | tf_op jit(solution)/shard_map/ppermute | solution.py:508
  289.4 7.0 %collective-permute-start.22 = (bf16[32,2048]{1,0:T(8,128)(2,1)S(1)}, bf16[32,2048]{1,0:T(8,128)(2,1)S(1)}, u32[]{:S(2)}, u32[]{:S(2)}) collective-permute-start(bf16[32,2048]{1,0:T(8,128)(2,1)S(1)} %get-tuple-element.160), channel_id=1, source_target_pairs={{1,32},{2,33},{3,34},{4,35},{5,36},{6,37},{7,38},{8,39},{9,40},{10... | collective-permute-start | bytes 393224 | tf_op jit(solution)/shard_map/ppermute | solution.py:509
  306.5 12.4 %collective-permute-start.24 = (bf16[32,2048]{1,0:T(8,128)(2,1)S(1)}, bf16[32,2048]{1,0:T(8,128)(2,1)S(1)}, u32[]{:S(2)}, u32[]{:S(2)}) collective-permute-start(bf16[32,2048]{1,0:T(8,128)(2,1)S(1)} %get-tuple-element.167), channel_id=1, source_target_pairs={{0,33},{1,34},{2,35},{3,36},{4,37},{5,38},{6,39},{7,40},{8,41},{9,... | collective-permute-start | bytes 393224 | tf_op jit(solution)/shard_map/ppermute | solution.py:508
  336.6 7.2 %collective-permute-done.30.gr_ref = bf16[32,2048]{1,0:T(8,128)(2,1)S(1)} collective-permute-done((bf16[32,2048]{1,0:T(8,128)(2,1)S(1)}, bf16[32,2048]{1,0:T(8,128)(2,1)S(1)}, u32[]{:S(2)}, u32[]{:S(2)}) %collective-permute-start.30) | collective-permute-done | bytes 131104 | tf_op jit(solution)/shard_map/ppermute | solution.py:509
  360.5 6.3 %collective-permute-done.37.gl_ref = bf16[32,2048]{1,0:T(8,128)(2,1)S(1)} collective-permute-done((bf16[32,2048]{1,0:T(8,128)(2,1)S(1)}, bf16[32,2048]{1,0:T(8,128)(2,1)S(1)}, u32[]{:S(2)}, u32[]{:S(2)}) %collective-permute-start.37) | collective-permute-done | bytes 131104 | tf_op jit(solution)/shard_map/ppermute | solution.py:508
  374.0 6.3 %collective-permute-done.40.gl_ref = bf16[32,2048]{1,0:T(8,128)(2,1)S(1)} collective-permute-done((bf16[32,2048]{1,0:T(8,128)(2,1)S(1)}, bf16[32,2048]{1,0:T(8,128)(2,1)S(1)}, u32[]{:S(2)}, u32[]{:S(2)}) %collective-permute-start.40) | collective-permute-done | bytes 131104 | tf_op jit(solution)/shard_map/ppermute | solution.py:508
  387.3 7.3 %collective-permute-done.43.gl_ref = bf16[32,2048]{1,0:T(8,128)(2,1)S(1)} collective-permute-done((bf16[32,2048]{1,0:T(8,128)(2,1)S(1)}, bf16[32,2048]{1,0:T(8,128)(2,1)S(1)}, u32[]{:S(2)}, u32[]{:S(2)}) %collective-permute-start.43) | collective-permute-done | bytes 131104 | tf_op jit(solution)/shard_map/ppermute | solution.py:508
  401.4 8.3 %collective-permute-done.46.gl_ref = bf16[32,2048]{1,0:T(8,128)(2,1)S(1)} collective-permute-done((bf16[32,2048]{1,0:T(8,128)(2,1)S(1)}, bf16[32,2048]{1,0:T(8,128)(2,1)S(1)}, u32[]{:S(2)}, u32[]{:S(2)}) %collective-permute-start.46) | collective-permute-done | bytes 131104 | tf_op jit(solution)/shard_map/ppermute | solution.py:508
  417.0 86.6 %collective-permute-done.49.gl_ref = bf16[32,2048]{1,0:T(8,128)(2,1)S(1)} collective-permute-done((bf16[32,2048]{1,0:T(8,128)(2,1)S(1)}, bf16[32,2048]{1,0:T(8,128)(2,1)S(1)}, u32[]{:S(2)}, u32[]{:S(2)}) %collective-permute-start.49) | collective-permute-done | bytes 131104 | tf_op jit(solution)/shard_map/ppermute | solution.py:508
  506.9 12.8 %backward_layer.16 = (bf16[128,2048]{1,0:T(8,128)(2,1)S(1)}, bf16[32,2048]{1,0:T(8,128)(2,1)S(1)}, bf16[32,2048]{1,0:T(8,128)(2,1)S(1)}, bf16[2,128,2048]{2,1,0:T(8,128)(2,1)}) custom-call(s32[1]{0:T(128)S(6)} %sub.42.refs_0_.section_ref, bf16[2,192,2048]{2,1,0:T(8,128)(2,1)S(1)} %get-tuple-element.220.refs_1_.c0_ref, ...), custom_call_target="tpu_custom_call", output_to_operand_aliasing={{3}: (15, {})} | custom-call | tf_op jit(solution)/shard_map/backward_layer/pallas_call | solution.py:429
  523.7 6.0 %collective-permute-done.52.gl_ref = bf16[32,2048]{1,0:T(8,128)(2,1)S(1)} collective-permute-done((bf16[32,2048]{1,0:T(8,128)(2,1)S(1)}, bf16[32,2048]{1,0:T(8,128)(2,1)S(1)}, u32[]{:S(2)}, u32[]{:S(2)}) %collective-permute-start.52) | collective-permute-done | bytes 131104 | tf_op jit(solution)/shard_map/ppermute | solution.py:508
  533.8 12.5 %backward_layer.17 = (bf16[128,2048]{1,0:T(8,128)(2,1)}, bf16[32,2048]{1,0:T(8,128)(2,1)}, bf16[32,2048]{1,0:T(8,128)(2,1)}, bf16[2,128,2048]{2,1,0:T(8,128)(2,1)}) custom-call(s32[1]{0:T(128)S(6)} %sub.42.refs_0_.section_ref, bf16[2,192,2048]{2,1,0:T(8,128)(2,1)S(1)} %get-tuple-element.220.refs_1_.c0_ref, ...), custom_call_target="tpu_custom_call", output_to_operand_aliasing={{3}: (15, {})} | custom-call | tf_op jit(solution)/shard_map/backward_layer/pallas_call | solution.py:429
  (147 shorter events, 140.0 us)
Async XLA Ops:
  7.2 160.2 %all-gather.3.cloned.1.call-start = ((), (), s32[]{:S(2)}) async-start(), calls=%async_computation | async-start | bytes 17301504 | tf_op jit(solution)/shard_map/all_gather | solution.py:549
  25.8 20.2 %collective-permute-start = (bf16[144,2048]{1,0:T(8,128)(2,1)S(1)}, bf16[144,2048]{1,0:T(8,128)(2,1)}, u32[]{:S(2)}, u32[]{:S(2)}) collective-permute-start(bf16[144,2048]{1,0:T(8,128)(2,1)S(1)} %fusion.2), channel_id=1, source_target_pairs={{0,1},{1,2},{2,3},{3,4},{4,5},{5,6},{6,7},{7,8},{8,9},{9,10},{10,1... | collective-permute-start | bytes 1769480 | tf_op jit(solution)/shard_map/ppermute | solution.py:517
  29.1 23.7 %collective-permute-start.1 = (bf16[144,2048]{1,0:T(8,128)(2,1)S(1)}, bf16[144,2048]{1,0:T(8,128)(2,1)}, u32[]{:S(2)}, u32[]{:S(2)}) collective-permute-start(bf16[144,2048]{1,0:T(8,128)(2,1)S(1)} %fusion.3), channel_id=1, source_target_pairs={{1,0},{2,1},{3,2},{4,3},{5,4},{6,5},{7,6},{8,7},{9,8},{10,9},{11,1... | collective-permute-start | bytes 1769480 | tf_op jit(solution)/shard_map/ppermute | solution.py:518
  206.6 22.4 %collective-permute-start.8 = (bf16[128,2048]{1,0:T(8,128)(2,1)S(1)}, bf16[128,2048]{1,0:T(8,128)(2,1)S(1)}, u32[]{:S(2)}, u32[]{:S(2)}) collective-permute-start(bf16[128,2048]{1,0:T(8,128)(2,1)S(1)} %get-tuple-element.126), channel_id=1, source_target_pairs={{32,64},{33,65},{34,66},{35,67},{36,68},{37,69},{38,70},{39,71},{4... | collective-permute-start | bytes 1572872 | tf_op jit(solution)/shard_map/ppermute | solution.py:507
  207.3 19.8 %collective-permute-start.9 = (bf16[32,2048]{1,0:T(8,128)(2,1)S(1)}, bf16[32,2048]{1,0:T(8,128)(2,1)S(1)}, u32[]{:S(2)}, u32[]{:S(2)}) collective-permute-start(bf16[32,2048]{1,0:T(8,128)(2,1)S(1)} %get-tuple-element.127), channel_id=1, source_target_pairs={{0,33},{1,34},{2,35},{3,36},{4,37},{5,38},{6,39},{7,40},{8,41},{9,... | collective-permute-start | bytes 393224 | tf_op jit(solution)/shard_map/ppermute | solution.py:508
  229.1 20.2 %collective-permute-start.11 = (bf16[128,2048]{1,0:T(8,128)(2,1)S(1)}, bf16[128,2048]{1,0:T(8,128)(2,1)S(1)}, u32[]{:S(2)}, u32[]{:S(2)}) collective-permute-start(bf16[128,2048]{1,0:T(8,128)(2,1)S(1)} %get-tuple-element.134), channel_id=1, source_target_pairs={{64,96},{65,97},{66,98},{67,99},{68,100},{69,101},{70,102},{71,103... | collective-permute-start | bytes 1572872 | tf_op jit(solution)/shard_map/ppermute | solution.py:507
  229.8 16.4 %collective-permute-start.12 = (bf16[32,2048]{1,0:T(8,128)(2,1)S(1)}, bf16[32,2048]{1,0:T(8,128)(2,1)S(1)}, u32[]{:S(2)}, u32[]{:S(2)}) collective-permute-start(bf16[32,2048]{1,0:T(8,128)(2,1)S(1)} %get-tuple-element.135), channel_id=1, source_target_pairs={{0,33},{1,34},{2,35},{3,36},{4,37},{5,38},{6,39},{7,40},{8,41},{9,... | collective-permute-start | bytes 393224 | tf_op jit(solution)/shard_map/ppermute | solution.py:508
  263.1 16.3 %collective-permute-start.17 = (bf16[128,2048]{1,0:T(8,128)(2,1)S(1)}, bf16[128,2048]{1,0:T(8,128)(2,1)S(1)}, u32[]{:S(2)}, u32[]{:S(2)}) collective-permute-start(bf16[128,2048]{1,0:T(8,128)(2,1)S(1)} %get-tuple-element.150), channel_id=1, source_target_pairs={{128,160},{129,161},{130,162},{131,163},{132,164},{133,165},{134,1... | collective-permute-start | bytes 1572872 | tf_op jit(solution)/shard_map/ppermute | solution.py:507
  279.5 20.3 %collective-permute-start.20 = (bf16[128,2048]{1,0:T(8,128)(2,1)S(1)}, bf16[128,2048]{1,0:T(8,128)(2,1)S(1)}, u32[]{:S(2)}, u32[]{:S(2)}) collective-permute-start(bf16[128,2048]{1,0:T(8,128)(2,1)S(1)} %get-tuple-element.158), channel_id=1, source_target_pairs={{160,192},{161,193},{162,194},{163,195},{164,196},{165,197},{166,1... | collective-permute-start | bytes 1572872 | tf_op jit(solution)/shard_map/ppermute | solution.py:507
  280.2 16.2 %collective-permute-start.21 = (bf16[32,2048]{1,0:T(8,128)(2,1)S(1)}, bf16[32,2048]{1,0:T(8,128)(2,1)S(1)}, u32[]{:S(2)}, u32[]{:S(2)}) collective-permute-start(bf16[32,2048]{1,0:T(8,128)(2,1)S(1)} %get-tuple-element.159), channel_id=1, source_target_pairs={{0,33},{1,34},{2,35},{3,36},{4,37},{5,38},{6,39},{7,40},{8,41},{9,... | collective-permute-start | bytes 393224 | tf_op jit(solution)/shard_map/ppermute | solution.py:508
  299.9 24.0 %collective-permute-start.23 = (bf16[128,2048]{1,0:T(8,128)(2,1)S(1)}, bf16[128,2048]{1,0:T(8,128)(2,1)S(1)}, u32[]{:S(2)}, u32[]{:S(2)}) collective-permute-start(bf16[128,2048]{1,0:T(8,128)(2,1)S(1)} %get-tuple-element.166), channel_id=1, source_target_pairs={{192,224},{193,225},{194,226},{195,227},{196,228},{197,229},{198,2... | collective-permute-start | bytes 1572872 | tf_op jit(solution)/shard_map/ppermute | solution.py:507
  300.7 19.6 %collective-permute-start.27 = (bf16[32,2176]{1,0:T(8,128)(2,1)S(1)}, bf16[32,2176]{1,0:T(8,128)(2,1)S(1)}, u32[]{:S(2)}, u32[]{:S(2)}) collective-permute-start(bf16[32,2176]{1,0:T(8,128)(2,1)S(1)} %get-tuple-element.226), channel_id=1, source_target_pairs={{1,0},{2,1},{3,2},{4,3},{5,4},{6,5},{7,6},{8,7},{9,8},{10,9},{11,1... | collective-permute-start | bytes 417800 | tf_op jit(solution)/shard_map/ppermute | solution.py:518
  302.6 17.6 %collective-permute-start.26 = (bf16[32,2176]{1,0:T(8,128)(2,1)S(1)}, bf16[32,2176]{1,0:T(8,128)(2,1)S(1)}, u32[]{:S(2)}, u32[]{:S(2)}) collective-permute-start(bf16[32,2176]{1,0:T(8,128)(2,1)S(1)} %get-tuple-element.227), channel_id=1, source_target_pairs={{0,1},{1,2},{2,3},{3,4},{4,5},{5,6},{6,7},{7,8},{8,9},{9,10},{10,1... | collective-permute-start | bytes 417800 | tf_op jit(solution)/shard_map/ppermute | solution.py:517
  306.5 15.8 %collective-permute-start.24 = (bf16[32,2048]{1,0:T(8,128)(2,1)S(1)}, bf16[32,2048]{1,0:T(8,128)(2,1)S(1)}, u32[]{:S(2)}, u32[]{:S(2)}) collective-permute-start(bf16[32,2048]{1,0:T(8,128)(2,1)S(1)} %get-tuple-element.167), channel_id=1, source_target_pairs={{0,33},{1,34},{2,35},{3,36},{4,37},{5,38},{6,39},{7,40},{8,41},{9,... | collective-permute-start | bytes 393224 | tf_op jit(solution)/shard_map/ppermute | solution.py:508
  320.6 23.3 %collective-permute-start.28 = (bf16[128,2048]{1,0:T(8,128)(2,1)S(1)}, bf16[128,2048]{1,0:T(8,128)(2,1)S(1)}, u32[]{:S(2)}, u32[]{:S(2)}) collective-permute-start(bf16[128,2048]{1,0:T(8,128)(2,1)S(1)} %get-tuple-element.181), channel_id=1, source_target_pairs={{224,192},{225,193},{226,194},{227,195},{228,196},{229,197},{230,1... | collective-permute-start | bytes 1572872 | tf_op jit(solution)/shard_map/ppermute | solution.py:507
  324.1 19.7 %collective-permute-start.32 = (bf16[32,2176]{1,0:T(8,128)(2,1)S(1)}, bf16[32,2176]{1,0:T(8,128)(2,1)S(1)}, u32[]{:S(2)}, u32[]{:S(2)}) collective-permute-start(bf16[32,2176]{1,0:T(8,128)(2,1)S(1)} %get-tuple-element.224), channel_id=1, source_target_pairs={{1,0},{2,1},{3,2},{4,3},{5,4},{6,5},{7,6},{8,7},{9,8},{10,9},{11,1... | collective-permute-start | bytes 417800 | tf_op jit(solution)/shard_map/ppermute | solution.py:518
  326.0 17.8 %collective-permute-start.31 = (bf16[32,2176]{1,0:T(8,128)(2,1)S(1)}, bf16[32,2176]{1,0:T(8,128)(2,1)S(1)}, u32[]{:S(2)}, u32[]{:S(2)}) collective-permute-start(bf16[32,2176]{1,0:T(8,128)(2,1)S(1)} %get-tuple-element.225), channel_id=1, source_target_pairs={{0,1},{1,2},{2,3},{3,4},{4,5},{5,6},{6,7},{7,8},{8,9},{9,10},{10,1... | collective-permute-start | bytes 417800 | tf_op jit(solution)/shard_map/ppermute | solution.py:517
  370.5 13.4 %collective-permute-start.39 = (bf16[128,2048]{1,0:T(8,128)(2,1)S(1)}, bf16[128,2048]{1,0:T(8,128)(2,1)S(1)}, u32[]{:S(2)}, u32[]{:S(2)}) collective-permute-start(bf16[128,2048]{1,0:T(8,128)(2,1)S(1)} %get-tuple-element.197), channel_id=1, source_target_pairs={{128,96},{129,97},{130,98},{131,99},{132,100},{133,101},{134,102},... | collective-permute-start | bytes 1572872 | tf_op jit(solution)/shard_map/ppermute | solution.py:507
  384.0 13.9 %collective-permute-start.42 = (bf16[128,2048]{1,0:T(8,128)(2,1)S(1)}, bf16[128,2048]{1,0:T(8,128)(2,1)S(1)}, u32[]{:S(2)}, u32[]{:S(2)}) collective-permute-start(bf16[128,2048]{1,0:T(8,128)(2,1)S(1)} %get-tuple-element.201), channel_id=1, source_target_pairs={{96,64},{97,65},{98,66},{99,67},{100,68},{101,69},{102,70},{103,71... | collective-permute-start | bytes 1572872 | tf_op jit(solution)/shard_map/ppermute | solution.py:507
  398.1 14.9 %collective-permute-start.45 = (bf16[128,2048]{1,0:T(8,128)(2,1)S(1)}, bf16[128,2048]{1,0:T(8,128)(2,1)S(1)}, u32[]{:S(2)}, u32[]{:S(2)}) collective-permute-start(bf16[128,2048]{1,0:T(8,128)(2,1)S(1)} %get-tuple-element.205), channel_id=1, source_target_pairs={{64,32},{65,33},{66,34},{67,35},{68,36},{69,37},{70,38},{71,39},{7... | collective-permute-start | bytes 1572872 | tf_op jit(solution)/shard_map/ppermute | solution.py:507
  413.1 93.8 %collective-permute-start.48 = (bf16[128,2048]{1,0:T(8,128)(2,1)S(1)}, bf16[128,2048]{1,0:T(8,128)(2,1)S(1)}, u32[]{:S(2)}, u32[]{:S(2)}) collective-permute-start(bf16[128,2048]{1,0:T(8,128)(2,1)S(1)} %get-tuple-element.209), channel_id=1, source_target_pairs={{32,0},{33,1},{34,2},{35,3},{36,4},{37,5},{38,6},{39,7},{40,8},{41... | collective-permute-start | bytes 1572872 | tf_op jit(solution)/shard_map/ppermute | solution.py:507
  414.4 89.2 %collective-permute-start.49 = (bf16[32,2048]{1,0:T(8,128)(2,1)S(1)}, bf16[32,2048]{1,0:T(8,128)(2,1)S(1)}, u32[]{:S(2)}, u32[]{:S(2)}) collective-permute-start(bf16[32,2048]{1,0:T(8,128)(2,1)S(1)} %get-tuple-element.210), channel_id=1, source_target_pairs={{32,1},{33,2},{34,3},{35,4},{36,5},{37,6},{38,7},{39,8},{40,9},{41... | collective-permute-start | bytes 393224 | tf_op jit(solution)/shard_map/ppermute | solution.py:508
  415.7 91.2 %collective-permute-start.50 = (bf16[32,2048]{1,0:T(8,128)(2,1)S(1)}, bf16[32,2048]{1,0:T(8,128)(2,1)S(1)}, u32[]{:S(2)}, u32[]{:S(2)}) collective-permute-start(bf16[32,2048]{1,0:T(8,128)(2,1)S(1)} %get-tuple-element.211), channel_id=1, source_target_pairs={{33,0},{34,1},{35,2},{36,3},{37,4},{38,5},{39,6},{40,7},{41,8},{42... | collective-permute-start | bytes 393224 | tf_op jit(solution)/shard_map/ppermute | solution.py:509
  519.8 14.0 %collective-permute-start.51 = (bf16[128,2048]{1,0:T(8,128)(2,1)S(1)}, bf16[128,2048]{1,0:T(8,128)(2,1)S(1)}, u32[]{:S(2)}, u32[]{:S(2)}) collective-permute-start(bf16[128,2048]{1,0:T(8,128)(2,1)S(1)} %get-tuple-element.213), channel_id=1, source_target_pairs={{32,0},{33,1},{34,2},{35,3},{36,4},{37,5},{38,6},{39,7},{40,8},{41... | collective-permute-start | bytes 1572872 | tf_op jit(solution)/shard_map/ppermute | solution.py:507
  (35 other events, 331.3 us)
Sparse Core Ops, SparseCore 0:
  24.4 142.9 all-gather.2

commit v5 on v4

--- a/solution.py
+++ b/solution.py
@@ -453,23 +453,12 @@
     return outs[:3], outs[3]
 
 
-def pack_body(wq_ref, wk_ref, wv_ref, wo_ref, out_ref, sem):
-    copies = [
-        pltpu.make_async_copy(source, target, sem.at[index])
-        for index, (source, target) in enumerate(
-            (
-                (wq_ref.at[0], out_ref.at[0:64]),
-                (wk_ref.at[0], out_ref.at[64:128]),
-                (wv_ref.at[0], out_ref.at[128:192]),
-                (wo_ref.at[0, :, :WIDTH], out_ref.at[192:224]),
-                (wo_ref.at[0, :, WIDTH:], out_ref.at[224:256]),
-            )
-        )
-    ]
-    for copy in copies:
-        copy.start()
-    for copy in copies:
-        copy.wait()
+def pack_body(wq_ref, wk_ref, wv_ref, wo_ref, out_ref):
+    out_ref[0:64] = wq_ref[0]
+    out_ref[64:128] = wk_ref[0]
+    out_ref[128:192] = wv_ref[0]
+    out_ref[192:224] = wo_ref[0, :, :WIDTH]
+    out_ref[224:256] = wo_ref[0, :, WIDTH:]
 
 
 def pack_call(*weights):
@@ -477,9 +466,8 @@
         pack_body,
         name="pack_weights",
         out_shape=jax.ShapeDtypeStruct((256, WIDTH), BF16),
-        in_specs=spaces(*"aaaa"),
-        out_specs=pl.BlockSpec(memory_space=pltpu.HBM),
-        scratch_shapes=[pltpu.SemaphoreType.DMA((5,))],
+        in_specs=spaces(*"vvvv"),
+        out_specs=pl.BlockSpec(memory_space=pltpu.VMEM),
     )(*weights)
 
 BOTH = ("section", "ctx")

time: 563 us -> 549 us (0.975)
  Pallas kernels: 65.8 us -> 50.5 us
    pallas_call x1, Pallas kernels: 17 us -> 2 us  [pack_call(): pl.pallas_call(pack_body, name='pack_weights', out_shape=jax.ShapeDtypeSt...]
where the time goes in v5:
time: 549 us; the launch traced here: 540 us
  waiting for transfers between devices  315 us (57%)
  starting transfers between devices  150 us (27%)
  Pallas kernels  50.5 us (9%)
  between operations  15.3 us (3%)
    ppermute x16, waiting for transfers between devices, relay(): from_left = lax.ppermute(right, BOTH, diagonal(n_section, step, n_ctx, 1))  137 us
    all_gather x1, waiting for transfers between devices, per_device(): gathered = lax.all_gather(shard, 'ctx', axis=0, tiled=False)  112 us
    ppermute x16, starting transfers between devices, relay(): from_left = lax.ppermute(right, BOTH, diagonal(n_section, step, n_ctx, 1))  78.1 us
    ppermute x16, waiting for transfers between devices, relay(): from_right = lax.ppermute(left, BOTH, diagonal(n_section, step, n_ctx, -1))  48.3 us
    ppermute x16, starting transfers between devices, relay(): from_right = lax.ppermute(left, BOTH, diagonal(n_section, step, n_ctx, -1))  38.3 us
    pallas_call x9, Pallas kernels, backward_call(): pl.pallas_call(body, name='backward_layer', out_shape=(rows, edge, edge,...  26.4 us
    pallas_call x9, Pallas kernels, forward_call(): pl.pallas_call(body, name='forward_layer', out_shape=(rows, edge, edge) +...  16.2 us
    ppermute x16, starting transfers between devices, relay(): rows = lax.ppermute(rows, BOTH, hop(sections, step, n_ctx))  15.9 us
  transfers between devices with their start and end apart: 55, of which 32 were waited for; matrix products, arithmetic and copies ran while one was open for 2% of the time, Pallas kernels for 0%

profile of v5, /device:TPU:100, one launch (start us, length us, event | category | flops | bytes accessed | tf_op | source)
XLA Modules:
  0.0 539.5 jit_solution(13198536508658450755)
XLA Ops:
  17.0 11.4 %collective-permute-done = bf16[144,2048]{1,0:T(8,128)(2,1)} collective-permute-done((bf16[144,2048]{1,0:T(8,128)(2,1)S(1)}, bf16[144,2048]{1,0:T(8,128)(2,1)}, u32[]{:S(2)}, u32[]{:S(2)}) %collective-permute-start) | collective-permute-done | bytes 589856 | tf_op jit(solution)/shard_map/ppermute | solution.py:505
  29.1 6.5 %collective-permute-done.1 = bf16[144,2048]{1,0:T(8,128)(2,1)} collective-permute-done((bf16[144,2048]{1,0:T(8,128)(2,1)S(1)}, bf16[144,2048]{1,0:T(8,128)(2,1)}, u32[]{:S(2)}, u32[]{:S(2)}) %collective-permute-start.1) | collective-permute-done | bytes 589856 | tf_op jit(solution)/shard_map/ppermute | solution.py:506
  42.1 111.6 %all-gather.3.cloned.1.call-done = bf16[8192,1024]{1,0:T(8,128)(2,1)} async-done(((bf16[256,1024]{1,0:T(8,128)(2,1)}), bf16[8192,1024]{1,0:T(8,128)(2,1)}) %all-gather.3.cloned.1.call-update) | async-done | bytes 16777232 | tf_op jit(solution)/shard_map/all_gather | solution.py:537
  153.7 5.8 %load_weights.1.refs_6_.w_ref = bf16[32,256,1024]{2,1,0:T(8,128)(2,1)S(1)} custom-call(bf16[32,256,1024]{2,1,0:T(8,128)(2,1)} %bitcast.32), custom_call_target="tpu_custom_call" | custom-call | tf_op jit(solution)/shard_map/load_weights/pallas_call | solution.py:232
  159.6 7.7 %forward_layer.9 = (bf16[128,2048]{1,0:T(8,128)(2,1)S(1)}, bf16[32,2048]{1,0:T(8,128)(2,1)S(1)}, bf16[32,2048]{1,0:T(8,128)(2,1)S(1)}, bf16[2,128,2048]{2,1,0:T(...) custom-call(s32[1]{0:T(128)} %bitcast.refs_0_.section_ref, ...), custom_call_target="tpu_custom_call" | custom-call | tf_op jit(solution)/shard_map/forward_layer/pallas_call | solution.py:202
  173.8 7.7 %forward_layer.10 = (bf16[128,2048]{1,0:T(8,128)(2,1)S(1)}, bf16[32,2048]{1,0:T(8,128)(2,1)S(1)}, bf16[32,2048]{1,0:T(8,128)(2,1)S(1)}, bf16[2,128,2048]{2,1,0:T...) custom-call(s32[1]{0:T(128)} %bitcast.refs_0_.section_ref, ...), custom_call_target="tpu_custom_call", output_to_operand_aliasing={{3}: (7, {}), {4}: (8, {}), {5}: (9, {}), {6}: (10, {}), {7... | custom-call | tf_op jit(solution)/shard_map/forward_layer/pallas_call | solution.py:202
  193.5 16.8 %collective-permute-start.9 = (bf16[32,2048]{1,0:T(8,128)(2,1)S(1)}, bf16[32,2048]{1,0:T(8,128)(2,1)S(1)}, u32[]{:S(2)}, u32[]{:S(2)}) collective-permute-start(bf16[32,2048]{1,0:T(8,128)(2,1)S(1)} %get-tuple-element.127), channel_id=1, source_target_pairs={{0,33},{1,34},{2,35},{3,36},{4,37},{5,38},{6,39},{7,40},{8,41},{9,... | collective-permute-start | bytes 393224 | tf_op jit(solution)/shard_map/ppermute | solution.py:496
  216.1 7.6 %collective-permute-start.12 = (bf16[32,2048]{1,0:T(8,128)(2,1)S(1)}, bf16[32,2048]{1,0:T(8,128)(2,1)S(1)}, u32[]{:S(2)}, u32[]{:S(2)}) collective-permute-start(bf16[32,2048]{1,0:T(8,128)(2,1)S(1)} %get-tuple-element.135), channel_id=1, source_target_pairs={{0,33},{1,34},{2,35},{3,36},{4,37},{5,38},{6,39},{7,40},{8,41},{9,... | collective-permute-start | bytes 393224 | tf_op jit(solution)/shard_map/ppermute | solution.py:496
  223.7 9.1 %collective-permute-start.13 = (bf16[32,2048]{1,0:T(8,128)(2,1)S(1)}, bf16[32,2048]{1,0:T(8,128)(2,1)S(1)}, u32[]{:S(2)}, u32[]{:S(2)}) collective-permute-start(bf16[32,2048]{1,0:T(8,128)(2,1)S(1)} %get-tuple-element.136), channel_id=1, source_target_pairs={{1,32},{2,33},{3,34},{4,35},{5,36},{6,37},{7,38},{8,39},{9,40},{10... | collective-permute-start | bytes 393224 | tf_op jit(solution)/shard_map/ppermute | solution.py:497
  236.4 8.6 %collective-permute-start.15 = (bf16[32,2048]{1,0:T(8,128)(2,1)S(1)}, bf16[32,2048]{1,0:T(8,128)(2,1)S(1)}, u32[]{:S(2)}, u32[]{:S(2)}) collective-permute-start(bf16[32,2048]{1,0:T(8,128)(2,1)S(1)} %get-tuple-element.143), channel_id=1, source_target_pairs={{0,33},{1,34},{2,35},{3,36},{4,37},{5,38},{6,39},{7,40},{8,41},{9,... | collective-permute-start | bytes 393224 | tf_op jit(solution)/shard_map/ppermute | solution.py:496
  249.7 7.8 %collective-permute-start.18 = (bf16[32,2048]{1,0:T(8,128)(2,1)S(1)}, bf16[32,2048]{1,0:T(8,128)(2,1)S(1)}, u32[]{:S(2)}, u32[]{:S(2)}) collective-permute-start(bf16[32,2048]{1,0:T(8,128)(2,1)S(1)} %get-tuple-element.151), channel_id=1, source_target_pairs={{0,33},{1,34},{2,35},{3,36},{4,37},{5,38},{6,39},{7,40},{8,41},{9,... | collective-permute-start | bytes 393224 | tf_op jit(solution)/shard_map/ppermute | solution.py:496
  257.6 5.3 collective-permute-start.19
  266.1 9.1 %collective-permute-start.21 = (bf16[32,2048]{1,0:T(8,128)(2,1)S(1)}, bf16[32,2048]{1,0:T(8,128)(2,1)S(1)}, u32[]{:S(2)}, u32[]{:S(2)}) collective-permute-start(bf16[32,2048]{1,0:T(8,128)(2,1)S(1)} %get-tuple-element.159), channel_id=1, source_target_pairs={{0,33},{1,34},{2,35},{3,36},{4,37},{5,38},{6,39},{7,40},{8,41},{9,... | collective-permute-start | bytes 393224 | tf_op jit(solution)/shard_map/ppermute | solution.py:496
  275.3 7.0 %collective-permute-start.22 = (bf16[32,2048]{1,0:T(8,128)(2,1)S(1)}, bf16[32,2048]{1,0:T(8,128)(2,1)S(1)}, u32[]{:S(2)}, u32[]{:S(2)}) collective-permute-start(bf16[32,2048]{1,0:T(8,128)(2,1)S(1)} %get-tuple-element.160), channel_id=1, source_target_pairs={{1,32},{2,33},{3,34},{4,35},{5,36},{6,37},{7,38},{8,39},{9,40},{10... | collective-permute-start | bytes 393224 | tf_op jit(solution)/shard_map/ppermute | solution.py:497
  292.4 12.5 %collective-permute-start.24 = (bf16[32,2048]{1,0:T(8,128)(2,1)S(1)}, bf16[32,2048]{1,0:T(8,128)(2,1)S(1)}, u32[]{:S(2)}, u32[]{:S(2)}) collective-permute-start(bf16[32,2048]{1,0:T(8,128)(2,1)S(1)} %get-tuple-element.167), channel_id=1, source_target_pairs={{0,33},{1,34},{2,35},{3,36},{4,37},{5,38},{6,39},{7,40},{8,41},{9,... | collective-permute-start | bytes 393224 | tf_op jit(solution)/shard_map/ppermute | solution.py:496
  322.5 7.2 %collective-permute-done.30.gr_ref = bf16[32,2048]{1,0:T(8,128)(2,1)S(1)} collective-permute-done((bf16[32,2048]{1,0:T(8,128)(2,1)S(1)}, bf16[32,2048]{1,0:T(8,128)(2,1)S(1)}, u32[]{:S(2)}, u32[]{:S(2)}) %collective-permute-start.30) | collective-permute-done | bytes 131104 | tf_op jit(solution)/shard_map/ppermute | solution.py:497
  346.4 6.3 %collective-permute-done.37.gl_ref = bf16[32,2048]{1,0:T(8,128)(2,1)S(1)} collective-permute-done((bf16[32,2048]{1,0:T(8,128)(2,1)S(1)}, bf16[32,2048]{1,0:T(8,128)(2,1)S(1)}, u32[]{:S(2)}, u32[]{:S(2)}) %collective-permute-start.37) | collective-permute-done | bytes 131104 | tf_op jit(solution)/shard_map/ppermute | solution.py:496
  359.9 6.3 %collective-permute-done.40.gl_ref = bf16[32,2048]{1,0:T(8,128)(2,1)S(1)} collective-permute-done((bf16[32,2048]{1,0:T(8,128)(2,1)S(1)}, bf16[32,2048]{1,0:T(8,128)(2,1)S(1)}, u32[]{:S(2)}, u32[]{:S(2)}) %collective-permute-start.40) | collective-permute-done | bytes 131104 | tf_op jit(solution)/shard_map/ppermute | solution.py:496
  373.2 7.3 %collective-permute-done.43.gl_ref = bf16[32,2048]{1,0:T(8,128)(2,1)S(1)} collective-permute-done((bf16[32,2048]{1,0:T(8,128)(2,1)S(1)}, bf16[32,2048]{1,0:T(8,128)(2,1)S(1)}, u32[]{:S(2)}, u32[]{:S(2)}) %collective-permute-start.43) | collective-permute-done | bytes 131104 | tf_op jit(solution)/shard_map/ppermute | solution.py:496
  387.3 8.3 %collective-permute-done.46.gl_ref = bf16[32,2048]{1,0:T(8,128)(2,1)S(1)} collective-permute-done((bf16[32,2048]{1,0:T(8,128)(2,1)S(1)}, bf16[32,2048]{1,0:T(8,128)(2,1)S(1)}, u32[]{:S(2)}, u32[]{:S(2)}) %collective-permute-start.46) | collective-permute-done | bytes 131104 | tf_op jit(solution)/shard_map/ppermute | solution.py:496
  402.9 86.6 %collective-permute-done.49.gl_ref = bf16[32,2048]{1,0:T(8,128)(2,1)S(1)} collective-permute-done((bf16[32,2048]{1,0:T(8,128)(2,1)S(1)}, bf16[32,2048]{1,0:T(8,128)(2,1)S(1)}, u32[]{:S(2)}, u32[]{:S(2)}) %collective-permute-start.49) | collective-permute-done | bytes 131104 | tf_op jit(solution)/shard_map/ppermute | solution.py:496
  492.9 12.8 %backward_layer.16 = (bf16[128,2048]{1,0:T(8,128)(2,1)S(1)}, bf16[32,2048]{1,0:T(8,128)(2,1)S(1)}, bf16[32,2048]{1,0:T(8,128)(2,1)S(1)}, bf16[2,128,2048]{2,1,0:T(8,128)(2,1)}) custom-call(s32[1]{0:T(128)S(6)} %sub.42.refs_0_.section_ref, bf16[2,192,2048]{2,1,0:T(8,128)(2,1)S(1)} %get-tuple-element.220.refs_1_.c0_ref, ...), custom_call_target="tpu_custom_call", output_to_operand_aliasing={{3}: (15, {})} | custom-call | tf_op jit(solution)/shard_map/backward_layer/pallas_call | solution.py:429
  509.6 6.0 %collective-permute-done.52.gl_ref = bf16[32,2048]{1,0:T(8,128)(2,1)S(1)} collective-permute-done((bf16[32,2048]{1,0:T(8,128)(2,1)S(1)}, bf16[32,2048]{1,0:T(8,128)(2,1)S(1)}, u32[]{:S(2)}, u32[]{:S(2)}) %collective-permute-start.52) | collective-permute-done | bytes 131104 | tf_op jit(solution)/shard_map/ppermute | solution.py:496
  519.7 12.5 %backward_layer.17 = (bf16[128,2048]{1,0:T(8,128)(2,1)}, bf16[32,2048]{1,0:T(8,128)(2,1)}, bf16[32,2048]{1,0:T(8,128)(2,1)}, bf16[2,128,2048]{2,1,0:T(8,128)(2,1)}) custom-call(s32[1]{0:T(128)S(6)} %sub.42.refs_0_.section_ref, bf16[2,192,2048]{2,1,0:T(8,128)(2,1)S(1)} %get-tuple-element.220.refs_1_.c0_ref, ...), custom_call_target="tpu_custom_call", output_to_operand_aliasing={{3}: (15, {})} | custom-call | tf_op jit(solution)/shard_map/backward_layer/pallas_call | solution.py:429
  (147 shorter events, 136.0 us)
Async XLA Ops:
  7.2 146.5 %all-gather.3.cloned.1.call-start = ((), (), s32[]{:S(2)}) async-start(), calls=%async_computation | async-start | bytes 17301504 | tf_op jit(solution)/shard_map/all_gather | solution.py:537
  10.8 17.5 %collective-permute-start = (bf16[144,2048]{1,0:T(8,128)(2,1)S(1)}, bf16[144,2048]{1,0:T(8,128)(2,1)}, u32[]{:S(2)}, u32[]{:S(2)}) collective-permute-start(bf16[144,2048]{1,0:T(8,128)(2,1)S(1)} %fusion.2), channel_id=1, source_target_pairs={{0,1},{1,2},{2,3},{3,4},{4,5},{5,6},{6,7},{7,8},{8,9},{9,10},{10,1... | collective-permute-start | bytes 1769480 | tf_op jit(solution)/shard_map/ppermute | solution.py:505
  14.0 21.6 %collective-permute-start.1 = (bf16[144,2048]{1,0:T(8,128)(2,1)S(1)}, bf16[144,2048]{1,0:T(8,128)(2,1)}, u32[]{:S(2)}, u32[]{:S(2)}) collective-permute-start(bf16[144,2048]{1,0:T(8,128)(2,1)S(1)} %fusion.3), channel_id=1, source_target_pairs={{1,0},{2,1},{3,2},{4,3},{5,4},{6,5},{7,6},{8,7},{9,8},{10,9},{11,1... | collective-permute-start | bytes 1769480 | tf_op jit(solution)/shard_map/ppermute | solution.py:506
  192.8 22.4 %collective-permute-start.8 = (bf16[128,2048]{1,0:T(8,128)(2,1)S(1)}, bf16[128,2048]{1,0:T(8,128)(2,1)S(1)}, u32[]{:S(2)}, u32[]{:S(2)}) collective-permute-start(bf16[128,2048]{1,0:T(8,128)(2,1)S(1)} %get-tuple-element.126), channel_id=1, source_target_pairs={{32,64},{33,65},{34,66},{35,67},{36,68},{37,69},{38,70},{39,71},{4... | collective-permute-start | bytes 1572872 | tf_op jit(solution)/shard_map/ppermute | solution.py:495
  193.5 19.8 %collective-permute-start.9 = (bf16[32,2048]{1,0:T(8,128)(2,1)S(1)}, bf16[32,2048]{1,0:T(8,128)(2,1)S(1)}, u32[]{:S(2)}, u32[]{:S(2)}) collective-permute-start(bf16[32,2048]{1,0:T(8,128)(2,1)S(1)} %get-tuple-element.127), channel_id=1, source_target_pairs={{0,33},{1,34},{2,35},{3,36},{4,37},{5,38},{6,39},{7,40},{8,41},{9,... | collective-permute-start | bytes 393224 | tf_op jit(solution)/shard_map/ppermute | solution.py:496
  215.4 20.2 %collective-permute-start.11 = (bf16[128,2048]{1,0:T(8,128)(2,1)S(1)}, bf16[128,2048]{1,0:T(8,128)(2,1)S(1)}, u32[]{:S(2)}, u32[]{:S(2)}) collective-permute-start(bf16[128,2048]{1,0:T(8,128)(2,1)S(1)} %get-tuple-element.134), channel_id=1, source_target_pairs={{64,96},{65,97},{66,98},{67,99},{68,100},{69,101},{70,102},{71,103... | collective-permute-start | bytes 1572872 | tf_op jit(solution)/shard_map/ppermute | solution.py:495
  216.1 16.8 %collective-permute-start.12 = (bf16[32,2048]{1,0:T(8,128)(2,1)S(1)}, bf16[32,2048]{1,0:T(8,128)(2,1)S(1)}, u32[]{:S(2)}, u32[]{:S(2)}) collective-permute-start(bf16[32,2048]{1,0:T(8,128)(2,1)S(1)} %get-tuple-element.135), channel_id=1, source_target_pairs={{0,33},{1,34},{2,35},{3,36},{4,37},{5,38},{6,39},{7,40},{8,41},{9,... | collective-permute-start | bytes 393224 | tf_op jit(solution)/shard_map/ppermute | solution.py:496
  249.0 16.3 %collective-permute-start.17 = (bf16[128,2048]{1,0:T(8,128)(2,1)S(1)}, bf16[128,2048]{1,0:T(8,128)(2,1)S(1)}, u32[]{:S(2)}, u32[]{:S(2)}) collective-permute-start(bf16[128,2048]{1,0:T(8,128)(2,1)S(1)} %get-tuple-element.150), channel_id=1, source_target_pairs={{128,160},{129,161},{130,162},{131,163},{132,164},{133,165},{134,1... | collective-permute-start | bytes 1572872 | tf_op jit(solution)/shard_map/ppermute | solution.py:495
  265.4 20.2 %collective-permute-start.20 = (bf16[128,2048]{1,0:T(8,128)(2,1)S(1)}, bf16[128,2048]{1,0:T(8,128)(2,1)S(1)}, u32[]{:S(2)}, u32[]{:S(2)}) collective-permute-start(bf16[128,2048]{1,0:T(8,128)(2,1)S(1)} %get-tuple-element.158), channel_id=1, source_target_pairs={{160,192},{161,193},{162,194},{163,195},{164,196},{165,197},{166,1... | collective-permute-start | bytes 1572872 | tf_op jit(solution)/shard_map/ppermute | solution.py:495
  266.1 16.2 %collective-permute-start.21 = (bf16[32,2048]{1,0:T(8,128)(2,1)S(1)}, bf16[32,2048]{1,0:T(8,128)(2,1)S(1)}, u32[]{:S(2)}, u32[]{:S(2)}) collective-permute-start(bf16[32,2048]{1,0:T(8,128)(2,1)S(1)} %get-tuple-element.159), channel_id=1, source_target_pairs={{0,33},{1,34},{2,35},{3,36},{4,37},{5,38},{6,39},{7,40},{8,41},{9,... | collective-permute-start | bytes 393224 | tf_op jit(solution)/shard_map/ppermute | solution.py:496
  285.8 24.1 %collective-permute-start.23 = (bf16[128,2048]{1,0:T(8,128)(2,1)S(1)}, bf16[128,2048]{1,0:T(8,128)(2,1)S(1)}, u32[]{:S(2)}, u32[]{:S(2)}) collective-permute-start(bf16[128,2048]{1,0:T(8,128)(2,1)S(1)} %get-tuple-element.166), channel_id=1, source_target_pairs={{192,224},{193,225},{194,226},{195,227},{196,228},{197,229},{198,2... | collective-permute-start | bytes 1572872 | tf_op jit(solution)/shard_map/ppermute | solution.py:495
  286.5 19.6 %collective-permute-start.27 = (bf16[32,2176]{1,0:T(8,128)(2,1)S(1)}, bf16[32,2176]{1,0:T(8,128)(2,1)S(1)}, u32[]{:S(2)}, u32[]{:S(2)}) collective-permute-start(bf16[32,2176]{1,0:T(8,128)(2,1)S(1)} %get-tuple-element.226), channel_id=1, source_target_pairs={{1,0},{2,1},{3,2},{4,3},{5,4},{6,5},{7,6},{8,7},{9,8},{10,9},{11,1... | collective-permute-start | bytes 417800 | tf_op jit(solution)/shard_map/ppermute | solution.py:506
  288.4 17.7 %collective-permute-start.26 = (bf16[32,2176]{1,0:T(8,128)(2,1)S(1)}, bf16[32,2176]{1,0:T(8,128)(2,1)S(1)}, u32[]{:S(2)}, u32[]{:S(2)}) collective-permute-start(bf16[32,2176]{1,0:T(8,128)(2,1)S(1)} %get-tuple-element.227), channel_id=1, source_target_pairs={{0,1},{1,2},{2,3},{3,4},{4,5},{5,6},{6,7},{7,8},{8,9},{9,10},{10,1... | collective-permute-start | bytes 417800 | tf_op jit(solution)/shard_map/ppermute | solution.py:505
  292.4 15.8 %collective-permute-start.24 = (bf16[32,2048]{1,0:T(8,128)(2,1)S(1)}, bf16[32,2048]{1,0:T(8,128)(2,1)S(1)}, u32[]{:S(2)}, u32[]{:S(2)}) collective-permute-start(bf16[32,2048]{1,0:T(8,128)(2,1)S(1)} %get-tuple-element.167), channel_id=1, source_target_pairs={{0,33},{1,34},{2,35},{3,36},{4,37},{5,38},{6,39},{7,40},{8,41},{9,... | collective-permute-start | bytes 393224 | tf_op jit(solution)/shard_map/ppermute | solution.py:496
  306.5 23.2 %collective-permute-start.28 = (bf16[128,2048]{1,0:T(8,128)(2,1)S(1)}, bf16[128,2048]{1,0:T(8,128)(2,1)S(1)}, u32[]{:S(2)}, u32[]{:S(2)}) collective-permute-start(bf16[128,2048]{1,0:T(8,128)(2,1)S(1)} %get-tuple-element.181), channel_id=1, source_target_pairs={{224,192},{225,193},{226,194},{227,195},{228,196},{229,197},{230,1... | collective-permute-start | bytes 1572872 | tf_op jit(solution)/shard_map/ppermute | solution.py:495
  310.0 19.7 %collective-permute-start.32 = (bf16[32,2176]{1,0:T(8,128)(2,1)S(1)}, bf16[32,2176]{1,0:T(8,128)(2,1)S(1)}, u32[]{:S(2)}, u32[]{:S(2)}) collective-permute-start(bf16[32,2176]{1,0:T(8,128)(2,1)S(1)} %get-tuple-element.224), channel_id=1, source_target_pairs={{1,0},{2,1},{3,2},{4,3},{5,4},{6,5},{7,6},{8,7},{9,8},{10,9},{11,1... | collective-permute-start | bytes 417800 | tf_op jit(solution)/shard_map/ppermute | solution.py:506
  311.9 17.8 %collective-permute-start.31 = (bf16[32,2176]{1,0:T(8,128)(2,1)S(1)}, bf16[32,2176]{1,0:T(8,128)(2,1)S(1)}, u32[]{:S(2)}, u32[]{:S(2)}) collective-permute-start(bf16[32,2176]{1,0:T(8,128)(2,1)S(1)} %get-tuple-element.225), channel_id=1, source_target_pairs={{0,1},{1,2},{2,3},{3,4},{4,5},{5,6},{6,7},{7,8},{8,9},{9,10},{10,1... | collective-permute-start | bytes 417800 | tf_op jit(solution)/shard_map/ppermute | solution.py:505
  356.4 13.4 %collective-permute-start.39 = (bf16[128,2048]{1,0:T(8,128)(2,1)S(1)}, bf16[128,2048]{1,0:T(8,128)(2,1)S(1)}, u32[]{:S(2)}, u32[]{:S(2)}) collective-permute-start(bf16[128,2048]{1,0:T(8,128)(2,1)S(1)} %get-tuple-element.197), channel_id=1, source_target_pairs={{128,96},{129,97},{130,98},{131,99},{132,100},{133,101},{134,102},... | collective-permute-start | bytes 1572872 | tf_op jit(solution)/shard_map/ppermute | solution.py:495
  369.9 13.9 %collective-permute-start.42 = (bf16[128,2048]{1,0:T(8,128)(2,1)S(1)}, bf16[128,2048]{1,0:T(8,128)(2,1)S(1)}, u32[]{:S(2)}, u32[]{:S(2)}) collective-permute-start(bf16[128,2048]{1,0:T(8,128)(2,1)S(1)} %get-tuple-element.201), channel_id=1, source_target_pairs={{96,64},{97,65},{98,66},{99,67},{100,68},{101,69},{102,70},{103,71... | collective-permute-start | bytes 1572872 | tf_op jit(solution)/shard_map/ppermute | solution.py:495
  384.0 14.9 %collective-permute-start.45 = (bf16[128,2048]{1,0:T(8,128)(2,1)S(1)}, bf16[128,2048]{1,0:T(8,128)(2,1)S(1)}, u32[]{:S(2)}, u32[]{:S(2)}) collective-permute-start(bf16[128,2048]{1,0:T(8,128)(2,1)S(1)} %get-tuple-element.205), channel_id=1, source_target_pairs={{64,32},{65,33},{66,34},{67,35},{68,36},{69,37},{70,38},{71,39},{7... | collective-permute-start | bytes 1572872 | tf_op jit(solution)/shard_map/ppermute | solution.py:495
  399.0 93.8 %collective-permute-start.48 = (bf16[128,2048]{1,0:T(8,128)(2,1)S(1)}, bf16[128,2048]{1,0:T(8,128)(2,1)S(1)}, u32[]{:S(2)}, u32[]{:S(2)}) collective-permute-start(bf16[128,2048]{1,0:T(8,128)(2,1)S(1)} %get-tuple-element.209), channel_id=1, source_target_pairs={{32,0},{33,1},{34,2},{35,3},{36,4},{37,5},{38,6},{39,7},{40,8},{41... | collective-permute-start | bytes 1572872 | tf_op jit(solution)/shard_map/ppermute | solution.py:495
  400.3 89.2 %collective-permute-start.49 = (bf16[32,2048]{1,0:T(8,128)(2,1)S(1)}, bf16[32,2048]{1,0:T(8,128)(2,1)S(1)}, u32[]{:S(2)}, u32[]{:S(2)}) collective-permute-start(bf16[32,2048]{1,0:T(8,128)(2,1)S(1)} %get-tuple-element.210), channel_id=1, source_target_pairs={{32,1},{33,2},{34,3},{35,4},{36,5},{37,6},{38,7},{39,8},{40,9},{41... | collective-permute-start | bytes 393224 | tf_op jit(solution)/shard_map/ppermute | solution.py:496
  401.6 91.2 %collective-permute-start.50 = (bf16[32,2048]{1,0:T(8,128)(2,1)S(1)}, bf16[32,2048]{1,0:T(8,128)(2,1)S(1)}, u32[]{:S(2)}, u32[]{:S(2)}) collective-permute-start(bf16[32,2048]{1,0:T(8,128)(2,1)S(1)} %get-tuple-element.211), channel_id=1, source_target_pairs={{33,0},{34,1},{35,2},{36,3},{37,4},{38,5},{39,6},{40,7},{41,8},{42... | collective-permute-start | bytes 393224 | tf_op jit(solution)/shard_map/ppermute | solution.py:497
  505.7 14.0 %collective-permute-start.51 = (bf16[128,2048]{1,0:T(8,128)(2,1)S(1)}, bf16[128,2048]{1,0:T(8,128)(2,1)S(1)}, u32[]{:S(2)}, u32[]{:S(2)}) collective-permute-start(bf16[128,2048]{1,0:T(8,128)(2,1)S(1)} %get-tuple-element.213), channel_id=1, source_target_pairs={{32,0},{33,1},{34,2},{35,3},{36,4},{37,5},{38,6},{39,7},{40,8},{41... | collective-permute-start | bytes 1572872 | tf_op jit(solution)/shard_map/ppermute | solution.py:495
  (35 other events, 301.2 us)
Sparse Core Ops, SparseCore 0:
  11.2 142.4 all-gather.2

commit v6 on v5

--- a/solution.py
+++ b/solution.py
@@ -222,22 +222,91 @@
     )(position, x0, x, xl, xr, mask, w, *saved)
     return outs[:3], outs[3:]
 
-def load_body(g_ref, w_ref, sem):
-    copy = pltpu.make_async_copy(g_ref, w_ref, sem)
-    copy.start()
-    copy.wait()
-
-
-def load_call(g):
+ACROSS = 4
+SPLIT = 112
+REST = 256 - SPLIT
+X_ORDER = (0, -1, 1, 2)
+Z_ORDER = (0, -1, -2, -3, 4, 1, 2, 3)
+
+
+def load_body(n_ctx, place_ref, *refs):
+    sources, w_ref, sem = refs[:-2], refs[-2], refs[-1]
+    depth = n_ctx // ACROSS
+    z, x = place_ref[0] // ACROSS, lax.rem(place_ref[0], ACROSS)
+
+    def owner(dx, dz):
+        return lax.rem(z + dz + depth, depth) * ACROSS + lax.rem(x + dx + ACROSS, ACROSS)
+
+    moves = []
+    for ref, dz, blocks in zip(
+        sources[:9],
+        (0, -1, -2, -3, 4, 4, 1, 2, 3),
+        (X_ORDER,) * 4 + (X_ORDER[:2], X_ORDER[2:]) + (X_ORDER,) * 3,
+    ):
+        for index, dx in enumerate(blocks):
+            piece = ref.at[index * SPLIT : (index + 1) * SPLIT]
+            moves.append((piece, w_ref.at[owner(dx, dz), 0:SPLIT]))
+    for ref, dx, blocks in zip(
+        sources[9:], (0, -1, 2, 2, 1), (Z_ORDER, Z_ORDER, Z_ORDER[:4], Z_ORDER[4:], Z_ORDER)
+    ):
+        for index, dz in enumerate(blocks):
+            piece = ref.at[index * REST : (index + 1) * REST]
+            moves.append((piece, w_ref.at[owner(dx, dz), SPLIT:256]))
+    copies = [
+        pltpu.make_async_copy(source, target, sem.at[index])
+        for index, (source, target) in enumerate(moves)
+    ]
+    for copy in copies:
+        copy.start()
+    for copy in copies:
+        copy.wait()
+
+
+def load_call(place, n_ctx, pieces):
     return pl.pallas_call(
-        load_body,
+        functools.partial(load_body, n_ctx),
         name="load_weights",
-        out_shape=pltpu.VMEM(g.shape, g.dtype),
-        in_specs=spaces("a"),
+        out_shape=pltpu.VMEM((n_ctx, 256, WIDTH), BF16),
+        in_specs=spaces("s", *("a" * len(pieces))),
         out_specs=pl.BlockSpec(memory_space=pltpu.VMEM),
-        scratch_shapes=[pltpu.SemaphoreType.DMA],
+        scratch_shapes=[pltpu.SemaphoreType.DMA((2 * n_ctx,))],
         compiler_params=pltpu.CompilerParams(vmem_limit_bytes=40 << 20),
-    )(g)
+    )(place, *pieces)
+
+
+def turn(block, dx, dz, n_ctx):
+    depth = n_ctx // ACROSS
+    pairs = [
+        (z * ACROSS + x, (z + dz) % depth * ACROSS + (x + dx) % ACROSS)
+        for z in range(depth)
+        for x in range(ACROSS)
+    ]
+    return lax.ppermute(block, "ctx", pairs)
+
+
+def ring_x(block, n_ctx):
+    half = block.shape[0] // 2
+    below, above = turn(block, 1, 0, n_ctx), turn(block, -1, 0, n_ctx)
+    return below, turn(below[:half], 1, 0, n_ctx), turn(above[half:], -1, 0, n_ctx), above
+
+
+def ring_z(block, n_ctx):
+    half = block.shape[0] // 2
+    below, above = [block], [block]
+    for _ in range(n_ctx // ACROSS // 2 - 1):
+        below.append(turn(below[-1], 0, 1, n_ctx))
+        above.append(turn(above[-1], 0, -1, n_ctx))
+    low, high = turn(below[-1][:half], 0, 1, n_ctx), turn(above[-1][half:], 0, -1, n_ctx)
+    return (*below[1:], low, high, *above[1:])
+
+
+def gather_weights(first, second, place, n_ctx):
+    below, low, high, above = ring_x(first, n_ctx)
+    wide = jnp.concatenate([first, below, above, low, high])
+    tall = jnp.concatenate([second, *ring_z(second, n_ctx)])
+    wide, tall = lax.optimization_barrier((wide, tall))
+    pieces = (wide, *ring_z(wide, n_ctx), tall, *ring_x(tall, n_ctx))
+    return load_call(place, n_ctx, pieces)
 
 
 def backward_body(
@@ -453,21 +522,25 @@
     return outs[:3], outs[3]
 
 
-def pack_body(wq_ref, wk_ref, wv_ref, wo_ref, out_ref):
-    out_ref[0:64] = wq_ref[0]
-    out_ref[64:128] = wk_ref[0]
-    out_ref[128:192] = wv_ref[0]
-    out_ref[192:224] = wo_ref[0, :, :WIDTH]
-    out_ref[224:256] = wo_ref[0, :, WIDTH:]
+def pack_body(wq_ref, wk_ref, wv_ref, wo_ref, first_ref, second_ref):
+    first_ref[0:64] = wq_ref[0]
+    first_ref[64:SPLIT] = wk_ref[0, : SPLIT - 64]
+    second_ref[: 128 - SPLIT] = wk_ref[0, SPLIT - 64 :]
+    second_ref[128 - SPLIT : 192 - SPLIT] = wv_ref[0]
+    second_ref[192 - SPLIT : 224 - SPLIT] = wo_ref[0, :, :WIDTH]
+    second_ref[224 - SPLIT :] = wo_ref[0, :, WIDTH:]
 
 
 def pack_call(*weights):
     return pl.pallas_call(
         pack_body,
         name="pack_weights",
-        out_shape=jax.ShapeDtypeStruct((256, WIDTH), BF16),
+        out_shape=(
+            jax.ShapeDtypeStruct((SPLIT, WIDTH), BF16),
+            jax.ShapeDtypeStruct((REST, WIDTH), BF16),
+        ),
         in_specs=spaces(*"vvvv"),
-        out_specs=pl.BlockSpec(memory_space=pltpu.VMEM),
+        out_specs=spaces(*"vv"),
     )(*weights)
 
 BOTH = ("section", "ctx")
@@ -533,8 +606,7 @@
     micro = section_input.shape[0]
     steps = n_section + micro - 1
 
-    shard = pack_call(w_query, w_key, w_value, w_out)
-    gathered = lax.all_gather(shard, "ctx", axis=0, tiled=False)
+    first, second = pack_call(w_query, w_key, w_value, w_out)
     position = jnp.full((1,), section, jnp.int32)
     reverse = n_section - 1 - position
     allow = allowed_keys(block_mask, place, n_ctx)
@@ -559,7 +631,7 @@
     extended = jnp.concatenate([before, fields, after], axis=2)
     mask = key_weights(before_allow, allow, after_allow)
     forward_mask = mask[:, BLK : BLK + ROWS]
-    weights = load_call(gathered)
+    weights = gather_weights(first, second, jnp.full((1,), place, jnp.int32), n_ctx)
 
     kinds = (
         jax.ShapeDtypeStruct((micro, ROWS, D), BF16),

time: 549 us -> 549 us (level)
  waiting for transfers between devices: 315 us -> 248 us
  starting transfers between devices: 150 us -> 191 us
  Pallas kernels: 50.5 us -> 72.3 us
  local copies, waits for them, and re-layouts: 4.7 us -> 21.3 us
  between operations: 15.3 us -> 1.92 us
    all_gather x1 -> x0, waiting for transfers between devices: 112 us -> none  [per_device(): gathered = lax.all_gather(shard, 'ctx', axis=0, tiled=False)]
    ppermute x0 -> x24, starting transfers between devices: none -> 39.9 us  [turn(): return lax.ppermute(block, 'ctx', pairs)]
    ppermute x0 -> x24, waiting for transfers between devices: none -> 35.8 us  [turn(): return lax.ppermute(block, 'ctx', pairs)]
    ppermute x16, waiting for transfers between devices: 137 us -> 109 us  [relay(): from_left = lax.ppermute(right, BOTH, diagonal(n_section, step, n_ctx, 1))]
    ppermute x3, waiting for transfers between devices: 11.4 us -> 34.3 us  [edges(): from_left = lax.ppermute(tail, 'ctx', neighbours(n_ctx, 1))]
    ppermute x16, waiting for transfers between devices: 48.3 us -> 62.7 us  [relay(): from_right = lax.ppermute(left, BOTH, diagonal(n_section, step, n_ctx, -1))]
    pallas_call x9, Pallas kernels: 26.4 us -> 38.6 us  [backward_call(): pl.pallas_call(body, name='backward_layer', out_shape=(rows, edge, edge,...]
    unnamed x8 -> x38, local copies, waits for them, and re-layouts: 0.02 us -> 9.15 us
  transfers between devices with their start and end apart: 55 -> 78, of which waited for: 32 -> 41; matrix products, arithmetic and copies ran while one was open for 2% -> 5% of each run, Pallas kernels for 0% -> 0%
where the time goes in v6:
time: 549 us; the launch traced here: 543 us
  waiting for transfers between devices  248 us (45%)
  starting transfers between devices  191 us (35%)
  Pallas kernels  72.3 us (13%)
  local copies, waits for them, and re-layouts  21.3 us (4%)
  other arithmetic  8.67 us (2%)
    ppermute x16, waiting for transfers between devices, relay(): from_left = lax.ppermute(right, BOTH, diagonal(n_section, step, n_ctx, 1))  109 us
    ppermute x16, starting transfers between devices, relay(): from_left = lax.ppermute(right, BOTH, diagonal(n_section, step, n_ctx, 1))  76 us
    ppermute x16, waiting for transfers between devices, relay(): from_right = lax.ppermute(left, BOTH, diagonal(n_section, step, n_ctx, -1))  62.7 us
    ppermute x24, starting transfers between devices, turn(): return lax.ppermute(block, 'ctx', pairs)  39.9 us
    pallas_call x9, Pallas kernels, backward_call(): pl.pallas_call(body, name='backward_layer', out_shape=(rows, edge, edge,...  38.6 us
    ppermute x16, starting transfers between devices, relay(): from_right = lax.ppermute(left, BOTH, diagonal(n_section, step, n_ctx, -1))  38.4 us
    ppermute x24, waiting for transfers between devices, turn(): return lax.ppermute(block, 'ctx', pairs)  35.8 us
    ppermute x3, waiting for transfers between devices, edges(): from_left = lax.ppermute(tail, 'ctx', neighbours(n_ctx, 1))  34.3 us
  transfers between devices with their start and end apart: 78, of which 41 were waited for; matrix products, arithmetic and copies ran while one was open for 5% of the time, Pallas kernels for 0%

profile of v6, /device:TPU:100, one launch (start us, length us, event | category | flops | bytes accessed | tf_op | source)
XLA Modules:
  0.0 543.3 jit_solution(4892994480982716078)
XLA Ops:
  55.5 11.8 %collective-permute-done.14.refs_1_ = bf16[448,1024]{1,0:T(8,128)(2,1)} collective-permute-done((bf16[448,1024]{1,0:T(8,128)(2,1)}, bf16[448,1024]{1,0:T(8,128)(2,1)}, u32[]{:S(2)}, u32[]{:S(2)}) %collective-permute-start.14) | collective-permute-done | bytes 917536 | tf_op jit(solution)/shard_map/ppermute | solution.py:284
  71.4 34.3 %collective-permute-done = bf16[144,2048]{1,0:T(8,128)(2,1)} collective-permute-done((bf16[144,2048]{1,0:T(8,128)(2,1)}, bf16[144,2048]{1,0:T(8,128)(2,1)}, u32[]{:S(2)}, u32[]{:S(2)}) %collective-permute-start) | collective-permute-done | bytes 589856 | tf_op jit(solution)/shard_map/ppermute | solution.py:578
  111.6 6.1 %collective-permute-done.1 = bf16[144,2048]{1,0:T(8,128)(2,1)} collective-permute-done((bf16[144,2048]{1,0:T(8,128)(2,1)}, bf16[144,2048]{1,0:T(8,128)(2,1)}, u32[]{:S(2)}, u32[]{:S(2)}) %collective-permute-start.1) | collective-permute-done | bytes 589856 | tf_op jit(solution)/shard_map/ppermute | solution.py:579
  124.6 11.0 %collective-permute-start.23 = (bf16[576,1024]{1,0:T(8,128)(2,1)S(1)}, bf16[576,1024]{1,0:T(8,128)(2,1)S(1)}, u32[]{:S(2)}, u32[]{:S(2)}) collective-permute-start(bf16[576,1024]{1,0:T(8,128)(2,1)S(1)} %slice.171), channel_id=1, source_target_pairs={{0,1},{1,2},{2,3},{3,0},{4,5},{5,6},{6,7},{7,4},{8,9},{9,10},{10,1... | collective-permute-start | bytes 3538952 | tf_op jit(solution)/shard_map/ppermute | solution.py:284
  154.3 6.5 %load_weights.1.refs_6_.w_ref = bf16[32,256,1024]{2,1,0:T(8,128)(2,1)S(1)} custom-call(s32[1]{0:T(128)} %bitcast.11.place_ref, bf16[448,1024]{1,0:T(8,128)(2,1)} %copy-done.3, bf16[448,1024]{1,0:T(8,128)(2,1)} %collective-permute-done.14.refs_1_, bf16[448,1024]{1,0:T(8,128)(2,1)} %collective-permute-done.15.refs_2_, ...), custom_call_target="tpu_custom_call" | custom-call | tf_op jit(solution)/shard_map/load_weights/pallas_call | solution.py:266
  160.8 7.7 %forward_layer.9 = (bf16[128,2048]{1,0:T(8,128)(2,1)S(1)}, bf16[32,2048]{1,0:T(8,128)(2,1)S(1)}, bf16[32,2048]{1,0:T(8,128)(2,1)S(1)}, bf16[2,128,2048]{2,1,0:T(...) custom-call(s32[1]{0:T(128)} %bitcast.refs_0_.section_ref, ...), custom_call_target="tpu_custom_call" | custom-call | tf_op jit(solution)/shard_map/forward_layer/pallas_call | solution.py:202
  175.0 16.7 %forward_layer.10 = (bf16[128,2048]{1,0:T(8,128)(2,1)S(1)}, bf16[32,2048]{1,0:T(8,128)(2,1)S(1)}, bf16[32,2048]{1,0:T(8,128)(2,1)S(1)}, bf16[2,128,2048]{2,1,0:T...) custom-call(s32[1]{0:T(128)} %bitcast.refs_0_.section_ref, ...), custom_call_target="tpu_custom_call", output_to_operand_aliasing={{3}: (7, {}), {4}: (8, {}), {5}: (9, {}), {6}: (10, {}), {7... | custom-call | tf_op jit(solution)/shard_map/forward_layer/pallas_call | solution.py:202
  204.2 15.8 %collective-permute-start.33 = (bf16[32,2048]{1,0:T(8,128)(2,1)S(1)}, bf16[32,2048]{1,0:T(8,128)(2,1)S(1)}, u32[]{:S(2)}, u32[]{:S(2)}) collective-permute-start(bf16[32,2048]{1,0:T(8,128)(2,1)S(1)} %get-tuple-element.135), channel_id=1, source_target_pairs={{0,33},{1,34},{2,35},{3,36},{4,37},{5,38},{6,39},{7,40},{8,41},{9,... | collective-permute-start | bytes 393224 | tf_op jit(solution)/shard_map/ppermute | solution.py:569
  225.9 9.1 %collective-permute-start.36 = (bf16[32,2048]{1,0:T(8,128)(2,1)S(1)}, bf16[32,2048]{1,0:T(8,128)(2,1)S(1)}, u32[]{:S(2)}, u32[]{:S(2)}) collective-permute-start(bf16[32,2048]{1,0:T(8,128)(2,1)S(1)} %get-tuple-element.143), channel_id=1, source_target_pairs={{0,33},{1,34},{2,35},{3,36},{4,37},{5,38},{6,39},{7,40},{8,41},{9,... | collective-permute-start | bytes 393224 | tf_op jit(solution)/shard_map/ppermute | solution.py:569
  235.1 9.2 %collective-permute-start.37 = (bf16[32,2048]{1,0:T(8,128)(2,1)S(1)}, bf16[32,2048]{1,0:T(8,128)(2,1)S(1)}, u32[]{:S(2)}, u32[]{:S(2)}) collective-permute-start(bf16[32,2048]{1,0:T(8,128)(2,1)S(1)} %get-tuple-element.144), channel_id=1, source_target_pairs={{1,32},{2,33},{3,34},{4,35},{5,36},{6,37},{7,38},{8,39},{9,40},{10... | collective-permute-start | bytes 393224 | tf_op jit(solution)/shard_map/ppermute | solution.py:570
  247.6 8.2 %collective-permute-start.39 = (bf16[32,2048]{1,0:T(8,128)(2,1)S(1)}, bf16[32,2048]{1,0:T(8,128)(2,1)S(1)}, u32[]{:S(2)}, u32[]{:S(2)}) collective-permute-start(bf16[32,2048]{1,0:T(8,128)(2,1)S(1)} %get-tuple-element.151), channel_id=1, source_target_pairs={{0,33},{1,34},{2,35},{3,36},{4,37},{5,38},{6,39},{7,40},{8,41},{9,... | collective-permute-start | bytes 393224 | tf_op jit(solution)/shard_map/ppermute | solution.py:569
  260.5 8.5 %collective-permute-start.42 = (bf16[32,2048]{1,0:T(8,128)(2,1)S(1)}, bf16[32,2048]{1,0:T(8,128)(2,1)S(1)}, u32[]{:S(2)}, u32[]{:S(2)}) collective-permute-start(bf16[32,2048]{1,0:T(8,128)(2,1)S(1)} %get-tuple-element.159), channel_id=1, source_target_pairs={{0,33},{1,34},{2,35},{3,36},{4,37},{5,38},{6,39},{7,40},{8,41},{9,... | collective-permute-start | bytes 393224 | tf_op jit(solution)/shard_map/ppermute | solution.py:569
  268.9 5.3 collective-permute-start.43
  278.0 9.3 %collective-permute-start.45 = (bf16[32,2048]{1,0:T(8,128)(2,1)S(1)}, bf16[32,2048]{1,0:T(8,128)(2,1)S(1)}, u32[]{:S(2)}, u32[]{:S(2)}) collective-permute-start(bf16[32,2048]{1,0:T(8,128)(2,1)S(1)} %get-tuple-element.167), channel_id=1, source_target_pairs={{0,33},{1,34},{2,35},{3,36},{4,37},{5,38},{6,39},{7,40},{8,41},{9,... | collective-permute-start | bytes 393224 | tf_op jit(solution)/shard_map/ppermute | solution.py:569
  294.1 6.6 %collective-permute-start.50 = (bf16[32,2176]{1,0:T(8,128)(2,1)S(1)}, bf16[32,2176]{1,0:T(8,128)(2,1)S(1)}, u32[]{:S(2)}, u32[]{:S(2)}) collective-permute-start(bf16[32,2176]{1,0:T(8,128)(2,1)S(1)} %get-tuple-element.235), channel_id=1, source_target_pairs={{0,1},{1,2},{2,3},{3,4},{4,5},{5,6},{6,7},{7,8},{8,9},{9,10},{10,1... | collective-permute-start | bytes 417800 | tf_op jit(solution)/shard_map/ppermute | solution.py:578
  302.7 11.3 %collective-permute-start.48 = (bf16[32,2048]{1,0:T(8,128)(2,1)S(1)}, bf16[32,2048]{1,0:T(8,128)(2,1)S(1)}, u32[]{:S(2)}, u32[]{:S(2)}) collective-permute-start(bf16[32,2048]{1,0:T(8,128)(2,1)S(1)} %get-tuple-element.175), channel_id=1, source_target_pairs={{0,33},{1,34},{2,35},{3,36},{4,37},{5,38},{6,39},{7,40},{8,41},{9,... | collective-permute-start | bytes 393224 | tf_op jit(solution)/shard_map/ppermute | solution.py:569
  333.3 10.8 %collective-permute-done.54.gr_ref = bf16[32,2048]{1,0:T(8,128)(2,1)S(1)} collective-permute-done((bf16[32,2048]{1,0:T(8,128)(2,1)S(1)}, bf16[32,2048]{1,0:T(8,128)(2,1)S(1)}, u32[]{:S(2)}, u32[]{:S(2)}) %collective-permute-start.54) | collective-permute-done | bytes 131104 | tf_op jit(solution)/shard_map/ppermute | solution.py:570
  351.3 6.1 %collective-permute-done.59.gr_ref = bf16[32,2048]{1,0:T(8,128)(2,1)S(1)} collective-permute-done((bf16[32,2048]{1,0:T(8,128)(2,1)S(1)}, bf16[32,2048]{1,0:T(8,128)(2,1)S(1)}, u32[]{:S(2)}, u32[]{:S(2)}) %collective-permute-start.59) | collective-permute-done | bytes 131104 | tf_op jit(solution)/shard_map/ppermute | solution.py:570
  357.4 7.7 %backward_layer.11 = (bf16[128,2048]{1,0:T(8,128)(2,1)S(1)}, bf16[32,2048]{1,0:T(8,128)(2,1)S(1)}, bf16[32,2048]{1,0:T(8,128)(2,1)S(1)}, bf16[2,128,2048]{2,1,0:T(8,128)(2,1)}) custom-call(s32[1]{0:T(128)S(6)} %sub.42.refs_0_.section_ref, bf16[2,192,2048]{2,1,0:T(8,128)(2,1)S(1)} %get-tuple-element.228.refs_1_.c0_ref, ...), custom_call_target="tpu_custom_call", output_to_operand_aliasing={{3}: (15, {})} | custom-call | tf_op jit(solution)/shard_map/backward_layer/pallas_call | solution.py:498
  382.4 5.8 %collective-permute-done.64.gl_ref = bf16[32,2048]{1,0:T(8,128)(2,1)S(1)} collective-permute-done((bf16[32,2048]{1,0:T(8,128)(2,1)S(1)}, bf16[32,2048]{1,0:T(8,128)(2,1)S(1)}, u32[]{:S(2)}, u32[]{:S(2)}) %collective-permute-start.64) | collective-permute-done | bytes 131104 | tf_op jit(solution)/shard_map/ppermute | solution.py:569
  430.0 70.2 %collective-permute-done.73.gl_ref = bf16[32,2048]{1,0:T(8,128)(2,1)S(1)} collective-permute-done((bf16[32,2048]{1,0:T(8,128)(2,1)S(1)}, bf16[32,2048]{1,0:T(8,128)(2,1)S(1)}, u32[]{:S(2)}, u32[]{:S(2)}) %collective-permute-start.73) | collective-permute-done | bytes 131104 | tf_op jit(solution)/shard_map/ppermute | solution.py:569
  503.5 12.6 %backward_layer.16 = (bf16[128,2048]{1,0:T(8,128)(2,1)S(1)}, bf16[32,2048]{1,0:T(8,128)(2,1)S(1)}, bf16[32,2048]{1,0:T(8,128)(2,1)S(1)}, bf16[2,128,2048]{2,1,0:T(8,128)(2,1)}) custom-call(s32[1]{0:T(128)S(6)} %sub.42.refs_0_.section_ref, bf16[2,192,2048]{2,1,0:T(8,128)(2,1)S(1)} %get-tuple-element.228.refs_1_.c0_ref, ...), custom_call_target="tpu_custom_call", output_to_operand_aliasing={{3}: (15, {})} | custom-call | tf_op jit(solution)/shard_map/backward_layer/pallas_call | solution.py:498
  520.0 6.0 %collective-permute-done.76.gl_ref = bf16[32,2048]{1,0:T(8,128)(2,1)S(1)} collective-permute-done((bf16[32,2048]{1,0:T(8,128)(2,1)S(1)}, bf16[32,2048]{1,0:T(8,128)(2,1)S(1)}, u32[]{:S(2)}, u32[]{:S(2)}) %collective-permute-start.76) | collective-permute-done | bytes 131104 | tf_op jit(solution)/shard_map/ppermute | solution.py:569
  530.5 12.5 %backward_layer.17 = (bf16[128,2048]{1,0:T(8,128)(2,1)}, bf16[32,2048]{1,0:T(8,128)(2,1)}, bf16[32,2048]{1,0:T(8,128)(2,1)}, bf16[2,128,2048]{2,1,0:T(8,128)(2,1)}) custom-call(s32[1]{0:T(128)S(6)} %sub.42.refs_0_.section_ref, bf16[2,192,2048]{2,1,0:T(8,128)(2,1)S(1)} %get-tuple-element.228.refs_1_.c0_ref, ...), custom_call_target="tpu_custom_call", output_to_operand_aliasing={{3}: (15, {})} | custom-call | tf_op jit(solution)/shard_map/backward_layer/pallas_call | solution.py:498
  (232 shorter events, 232.3 us)
Async XLA Ops:
  44.6 79.9 %collective-permute-start.22 = (bf16[1152,1024]{1,0:T(8,128)(2,1)}, bf16[1152,1024]{1,0:T(8,128)(2,1)S(1)}, u32[]{:S(2)}, u32[]{:S(2)}) collective-permute-start(bf16[1152,1024]{1,0:T(8,128)(2,1)} %constant_dynamic-update-slice_fusion.5.refs_9_), channel_id=1, source_target_pairs={{0,1},{1,2},{2,3},{3,0},{4,5},{5,6},{6,7},{7,4},{8,9},{9,10},{10,1... | collective-permute-start | bytes 7077896 | tf_op jit(solution)/shard_map/ppermute | solution.py:284
  45.8 89.8 %collective-permute-start.24 = (bf16[1152,1024]{1,0:T(8,128)(2,1)}, bf16[1152,1024]{1,0:T(8,128)(2,1)}, u32[]{:S(2)}, u32[]{:S(2)}) collective-permute-start(bf16[1152,1024]{1,0:T(8,128)(2,1)} %constant_dynamic-update-slice_fusion.5.refs_9_), channel_id=1, source_target_pairs={{0,3},{1,0},{2,1},{3,2},{4,7},{5,4},{6,5},{7,6},{8,11},{9,8},{10,9... | collective-permute-start | bytes 7077896 | tf_op jit(solution)/shard_map/ppermute | solution.py:284
  46.7 20.6 %collective-permute-start.14 = (bf16[448,1024]{1,0:T(8,128)(2,1)}, bf16[448,1024]{1,0:T(8,128)(2,1)}, u32[]{:S(2)}, u32[]{:S(2)}) collective-permute-start(bf16[448,1024]{1,0:T(8,128)(2,1)} %copy-done.3), channel_id=1, source_target_pairs={{0,4},{1,5},{2,6},{3,7},{4,8},{5,9},{6,10},{7,11},{8,12},{9,13},{1... | collective-permute-start | bytes 2752520 | tf_op jit(solution)/shard_map/ppermute | solution.py:284
  46.8 20.8 %collective-permute-start.18 = (bf16[448,1024]{1,0:T(8,128)(2,1)}, bf16[448,1024]{1,0:T(8,128)(2,1)}, u32[]{:S(2)}, u32[]{:S(2)}) collective-permute-start(bf16[448,1024]{1,0:T(8,128)(2,1)} %copy-done.3), channel_id=1, source_target_pairs={{0,28},{1,29},{2,30},{3,31},{4,0},{5,1},{6,2},{7,3},{8,4},{9,5},{1... | collective-permute-start | bytes 2752520 | tf_op jit(solution)/shard_map/ppermute | solution.py:284
  52.4 53.3 %collective-permute-start = (bf16[144,2048]{1,0:T(8,128)(2,1)}, bf16[144,2048]{1,0:T(8,128)(2,1)}, u32[]{:S(2)}, u32[]{:S(2)}) collective-permute-start(bf16[144,2048]{1,0:T(8,128)(2,1)} %fusion.2), channel_id=1, source_target_pairs={{0,1},{1,2},{2,3},{3,4},{4,5},{5,6},{6,7},{7,8},{8,9},{9,10},{10,1... | collective-permute-start | bytes 1769480 | tf_op jit(solution)/shard_map/ppermute | solution.py:578
  67.3 42.3 %collective-permute-start.15 = (bf16[448,1024]{1,0:T(8,128)(2,1)}, bf16[448,1024]{1,0:T(8,128)(2,1)}, u32[]{:S(2)}, u32[]{:S(2)}) collective-permute-start(bf16[448,1024]{1,0:T(8,128)(2,1)} %collective-permute-done.14.refs_1_), channel_id=1, source_target_pairs={{0,4},{1,5},{2,6},{3,7},{4,8},{5,9},{6,10},{7,11},{8,12},{9,13},{1... | collective-permute-start | bytes 2752520 | tf_op jit(solution)/shard_map/ppermute | solution.py:284
  67.6 42.0 %collective-permute-start.19 = (bf16[448,1024]{1,0:T(8,128)(2,1)}, bf16[448,1024]{1,0:T(8,128)(2,1)}, u32[]{:S(2)}, u32[]{:S(2)}) collective-permute-start(bf16[448,1024]{1,0:T(8,128)(2,1)} %collective-permute-done.18.refs_6_), channel_id=1, source_target_pairs={{0,28},{1,29},{2,30},{3,31},{4,0},{5,1},{6,2},{7,3},{8,4},{9,5},{1... | collective-permute-start | bytes 2752520 | tf_op jit(solution)/shard_map/ppermute | solution.py:284
  109.6 30.3 %collective-permute-start.16 = (bf16[448,1024]{1,0:T(8,128)(2,1)}, bf16[448,1024]{1,0:T(8,128)(2,1)}, u32[]{:S(2)}, u32[]{:S(2)}) collective-permute-start(bf16[448,1024]{1,0:T(8,128)(2,1)} %collective-permute-done.15.refs_2_), channel_id=1, source_target_pairs={{0,4},{1,5},{2,6},{3,7},{4,8},{5,9},{6,10},{7,11},{8,12},{9,13},{1... | collective-permute-start | bytes 2752520 | tf_op jit(solution)/shard_map/ppermute | solution.py:284
  109.6 31.5 %collective-permute-start.20 = (bf16[448,1024]{1,0:T(8,128)(2,1)}, bf16[448,1024]{1,0:T(8,128)(2,1)}, u32[]{:S(2)}, u32[]{:S(2)}) collective-permute-start(bf16[448,1024]{1,0:T(8,128)(2,1)} %collective-permute-done.19.refs_7_), channel_id=1, source_target_pairs={{0,28},{1,29},{2,30},{3,31},{4,0},{5,1},{6,2},{7,3},{8,4},{9,5},{1... | collective-permute-start | bytes 2752520 | tf_op jit(solution)/shard_map/ppermute | solution.py:284
  124.6 27.2 %collective-permute-start.23 = (bf16[576,1024]{1,0:T(8,128)(2,1)S(1)}, bf16[576,1024]{1,0:T(8,128)(2,1)S(1)}, u32[]{:S(2)}, u32[]{:S(2)}) collective-permute-start(bf16[576,1024]{1,0:T(8,128)(2,1)S(1)} %slice.171), channel_id=1, source_target_pairs={{0,1},{1,2},{2,3},{3,0},{4,5},{5,6},{6,7},{7,4},{8,9},{9,10},{10,1... | collective-permute-start | bytes 3538952 | tf_op jit(solution)/shard_map/ppermute | solution.py:284
  203.5 21.6 %collective-permute-start.32 = (bf16[128,2048]{1,0:T(8,128)(2,1)S(1)}, bf16[128,2048]{1,0:T(8,128)(2,1)S(1)}, u32[]{:S(2)}, u32[]{:S(2)}) collective-permute-start(bf16[128,2048]{1,0:T(8,128)(2,1)S(1)} %get-tuple-element.134), channel_id=1, source_target_pairs={{32,64},{33,65},{34,66},{35,67},{36,68},{37,69},{38,70},{39,71},{4... | collective-permute-start | bytes 1572872 | tf_op jit(solution)/shard_map/ppermute | solution.py:568
  204.2 18.8 %collective-permute-start.33 = (bf16[32,2048]{1,0:T(8,128)(2,1)S(1)}, bf16[32,2048]{1,0:T(8,128)(2,1)S(1)}, u32[]{:S(2)}, u32[]{:S(2)}) collective-permute-start(bf16[32,2048]{1,0:T(8,128)(2,1)S(1)} %get-tuple-element.135), channel_id=1, source_target_pairs={{0,33},{1,34},{2,35},{3,36},{4,37},{5,38},{6,39},{7,40},{8,41},{9,... | collective-permute-start | bytes 393224 | tf_op jit(solution)/shard_map/ppermute | solution.py:569
  225.2 21.6 %collective-permute-start.35 = (bf16[128,2048]{1,0:T(8,128)(2,1)S(1)}, bf16[128,2048]{1,0:T(8,128)(2,1)S(1)}, u32[]{:S(2)}, u32[]{:S(2)}) collective-permute-start(bf16[128,2048]{1,0:T(8,128)(2,1)S(1)} %get-tuple-element.142), channel_id=1, source_target_pairs={{64,96},{65,97},{66,98},{67,99},{68,100},{69,101},{70,102},{71,103... | collective-permute-start | bytes 1572872 | tf_op jit(solution)/shard_map/ppermute | solution.py:568
  225.9 18.4 %collective-permute-start.36 = (bf16[32,2048]{1,0:T(8,128)(2,1)S(1)}, bf16[32,2048]{1,0:T(8,128)(2,1)S(1)}, u32[]{:S(2)}, u32[]{:S(2)}) collective-permute-start(bf16[32,2048]{1,0:T(8,128)(2,1)S(1)} %get-tuple-element.143), channel_id=1, source_target_pairs={{0,33},{1,34},{2,35},{3,36},{4,37},{5,38},{6,39},{7,40},{8,41},{9,... | collective-permute-start | bytes 393224 | tf_op jit(solution)/shard_map/ppermute | solution.py:569
  259.8 17.2 %collective-permute-start.41 = (bf16[128,2048]{1,0:T(8,128)(2,1)S(1)}, bf16[128,2048]{1,0:T(8,128)(2,1)S(1)}, u32[]{:S(2)}, u32[]{:S(2)}) collective-permute-start(bf16[128,2048]{1,0:T(8,128)(2,1)S(1)} %get-tuple-element.158), channel_id=1, source_target_pairs={{128,160},{129,161},{130,162},{131,163},{132,164},{133,165},{134,1... | collective-permute-start | bytes 1572872 | tf_op jit(solution)/shard_map/ppermute | solution.py:568
  293.4 27.6 %collective-permute-start.47 = (bf16[128,2048]{1,0:T(8,128)(2,1)S(1)}, bf16[128,2048]{1,0:T(8,128)(2,1)S(1)}, u32[]{:S(2)}, u32[]{:S(2)}) collective-permute-start(bf16[128,2048]{1,0:T(8,128)(2,1)S(1)} %get-tuple-element.174), channel_id=1, source_target_pairs={{192,224},{193,225},{194,226},{195,227},{196,228},{197,229},{198,2... | collective-permute-start | bytes 1572872 | tf_op jit(solution)/shard_map/ppermute | solution.py:568
  294.1 23.3 %collective-permute-start.50 = (bf16[32,2176]{1,0:T(8,128)(2,1)S(1)}, bf16[32,2176]{1,0:T(8,128)(2,1)S(1)}, u32[]{:S(2)}, u32[]{:S(2)}) collective-permute-start(bf16[32,2176]{1,0:T(8,128)(2,1)S(1)} %get-tuple-element.235), channel_id=1, source_target_pairs={{0,1},{1,2},{2,3},{3,4},{4,5},{5,6},{6,7},{7,8},{8,9},{9,10},{10,1... | collective-permute-start | bytes 417800 | tf_op jit(solution)/shard_map/ppermute | solution.py:578
  300.7 16.8 %collective-permute-start.51 = (bf16[32,2176]{1,0:T(8,128)(2,1)S(1)}, bf16[32,2176]{1,0:T(8,128)(2,1)S(1)}, u32[]{:S(2)}, u32[]{:S(2)}) collective-permute-start(bf16[32,2176]{1,0:T(8,128)(2,1)S(1)} %get-tuple-element.234), channel_id=1, source_target_pairs={{1,0},{2,1},{3,2},{4,3},{5,4},{6,5},{7,6},{8,7},{9,8},{10,9},{11,1... | collective-permute-start | bytes 417800 | tf_op jit(solution)/shard_map/ppermute | solution.py:579
  317.6 26.5 %collective-permute-start.52 = (bf16[128,2048]{1,0:T(8,128)(2,1)S(1)}, bf16[128,2048]{1,0:T(8,128)(2,1)S(1)}, u32[]{:S(2)}, u32[]{:S(2)}) collective-permute-start(bf16[128,2048]{1,0:T(8,128)(2,1)S(1)} %get-tuple-element.189), channel_id=1, source_target_pairs={{224,192},{225,193},{226,194},{227,195},{228,196},{229,197},{230,1... | collective-permute-start | bytes 1572872 | tf_op jit(solution)/shard_map/ppermute | solution.py:568
  321.2 23.0 %collective-permute-start.55 = (bf16[32,2176]{1,0:T(8,128)(2,1)S(1)}, bf16[32,2176]{1,0:T(8,128)(2,1)S(1)}, u32[]{:S(2)}, u32[]{:S(2)}) collective-permute-start(bf16[32,2176]{1,0:T(8,128)(2,1)S(1)} %get-tuple-element.233), channel_id=1, source_target_pairs={{0,1},{1,2},{2,3},{3,4},{4,5},{5,6},{6,7},{7,8},{8,9},{9,10},{10,1... | collective-permute-start | bytes 417800 | tf_op jit(solution)/shard_map/ppermute | solution.py:578
  324.3 19.8 %collective-permute-start.56 = (bf16[32,2176]{1,0:T(8,128)(2,1)S(1)}, bf16[32,2176]{1,0:T(8,128)(2,1)S(1)}, u32[]{:S(2)}, u32[]{:S(2)}) collective-permute-start(bf16[32,2176]{1,0:T(8,128)(2,1)S(1)} %get-tuple-element.232), channel_id=1, source_target_pairs={{1,0},{2,1},{3,2},{4,3},{5,4},{6,5},{7,6},{8,7},{9,8},{10,9},{11,1... | collective-permute-start | bytes 417800 | tf_op jit(solution)/shard_map/ppermute | solution.py:579
  426.1 77.4 %collective-permute-start.72 = (bf16[128,2048]{1,0:T(8,128)(2,1)S(1)}, bf16[128,2048]{1,0:T(8,128)(2,1)S(1)}, u32[]{:S(2)}, u32[]{:S(2)}) collective-permute-start(bf16[128,2048]{1,0:T(8,128)(2,1)S(1)} %get-tuple-element.217), channel_id=1, source_target_pairs={{32,0},{33,1},{34,2},{35,3},{36,4},{37,5},{38,6},{39,7},{40,8},{41... | collective-permute-start | bytes 1572872 | tf_op jit(solution)/shard_map/ppermute | solution.py:568
  427.4 72.8 %collective-permute-start.73 = (bf16[32,2048]{1,0:T(8,128)(2,1)S(1)}, bf16[32,2048]{1,0:T(8,128)(2,1)S(1)}, u32[]{:S(2)}, u32[]{:S(2)}) collective-permute-start(bf16[32,2048]{1,0:T(8,128)(2,1)S(1)} %get-tuple-element.218), channel_id=1, source_target_pairs={{32,1},{33,2},{34,3},{35,4},{36,5},{37,6},{38,7},{39,8},{40,9},{41... | collective-permute-start | bytes 393224 | tf_op jit(solution)/shard_map/ppermute | solution.py:569
  428.7 74.8 %collective-permute-start.74 = (bf16[32,2048]{1,0:T(8,128)(2,1)S(1)}, bf16[32,2048]{1,0:T(8,128)(2,1)S(1)}, u32[]{:S(2)}, u32[]{:S(2)}) collective-permute-start(bf16[32,2048]{1,0:T(8,128)(2,1)S(1)} %get-tuple-element.219), channel_id=1, source_target_pairs={{33,0},{34,1},{35,2},{36,3},{37,4},{38,5},{39,6},{40,7},{41,8},{42... | collective-permute-start | bytes 393224 | tf_op jit(solution)/shard_map/ppermute | solution.py:570
  (67 other events, 655.6 us)

commit v7 on v6

--- a/solution.py
+++ b/solution.py
@@ -300,13 +300,13 @@
     return (*below[1:], low, high, *above[1:])
 
 
-def gather_weights(first, second, place, n_ctx):
+def gather_weights(first, second, ends, place, n_ctx):
     below, low, high, above = ring_x(first, n_ctx)
     wide = jnp.concatenate([first, below, above, low, high])
     tall = jnp.concatenate([second, *ring_z(second, n_ctx)])
-    wide, tall = lax.optimization_barrier((wide, tall))
+    wide, tall, ends = lax.optimization_barrier((wide, tall, ends))
     pieces = (wide, *ring_z(wide, n_ctx), tall, *ring_x(tall, n_ctx))
-    return load_call(place, n_ctx, pieces)
+    return load_call(place, n_ctx, pieces), ends
 
 
 def backward_body(
@@ -621,6 +621,9 @@
     )
     size = pieces.shape[0] // 2
     before, after = edges(pieces, 0, size, n_ctx)
+    weights, (before, after) = gather_weights(
+        first, second, (before, after), jnp.full((1,), place, jnp.int32), n_ctx
+    )
 
     def unpacked(piece):
         block = piece[: size - 16].reshape(2, micro, BLK, D)
@@ -631,7 +634,6 @@
     extended = jnp.concatenate([before, fields, after], axis=2)
     mask = key_weights(before_allow, allow, after_allow)
     forward_mask = mask[:, BLK : BLK + ROWS]
-    weights = gather_weights(first, second, jnp.full((1,), place, jnp.int32), n_ctx)
 
     kinds = (
         jax.ShapeDtypeStruct((micro, ROWS, D), BF16),

time: 549 us -> 531 us (0.967)
    ppermute x24, waiting for transfers between devices: 35.8 us -> 71 us  [turn(): return lax.ppermute(block, 'ctx', pairs)]
    ppermute x3, waiting for transfers between devices: 34.3 us -> 0.01 us  [edges(): from_left = lax.ppermute(tail, 'ctx', neighbours(n_ctx, 1))]
    ppermute x3, waiting for transfers between devices: 6.15 us -> 0.01 us  [edges(): from_right = lax.ppermute(head, 'ctx', neighbours(n_ctx, -1))]
    ppermute x24, starting transfers between devices: 39.9 us -> 33.8 us  [turn(): return lax.ppermute(block, 'ctx', pairs)]
  transfers between devices with their start and end apart: 78 -> 78, of which waited for: 41 -> 39; matrix products, arithmetic and copies ran while one was open for 5% -> 4% of each run, Pallas kernels for 0% -> 0%
where the time goes in v7:
time: 531 us; the launch traced here: 525 us
  waiting for transfers between devices  243 us (46%)
  starting transfers between devices  186 us (35%)
  Pallas kernels  72.3 us (14%)
  local copies, waits for them, and re-layouts  17.1 us (3%)
    ppermute x16, waiting for transfers between devices, relay(): from_left = lax.ppermute(right, BOTH, diagonal(n_section, step, n_ctx, 1))  110 us
    ppermute x16, starting transfers between devices, relay(): from_left = lax.ppermute(right, BOTH, diagonal(n_section, step, n_ctx, 1))  75.5 us
    ppermute x24, waiting for transfers between devices, turn(): return lax.ppermute(block, 'ctx', pairs)  71 us
    ppermute x16, waiting for transfers between devices, relay(): from_right = lax.ppermute(left, BOTH, diagonal(n_section, step, n_ctx, -1))  62.1 us
    ppermute x16, starting transfers between devices, relay(): from_right = lax.ppermute(left, BOTH, diagonal(n_section, step, n_ctx, -1))  39.2 us
    pallas_call x9, Pallas kernels, backward_call(): pl.pallas_call(body, name='backward_layer', out_shape=(rows, edge, edge,...  38.6 us
    ppermute x24, starting transfers between devices, turn(): return lax.ppermute(block, 'ctx', pairs)  33.8 us
    pallas_call x9, Pallas kernels, forward_call(): pl.pallas_call(body, name='forward_layer', out_shape=(rows, edge, edge) +...  25.3 us
  transfers between devices with their start and end apart: 78, of which 39 were waited for; matrix products, arithmetic and copies ran while one was open for 4% of the time, Pallas kernels for 0%

profile of v7, /device:TPU:100, one launch (start us, length us, event | category | flops | bytes accessed | tf_op | source)
XLA Modules:
  0.0 525.2 jit_solution(9377212650696815249)
XLA Ops:
  29.2 14.3 %collective-permute-done.3 = bf16[56,1024]{1,0:T(8,128)(2,1)S(1)} collective-permute-done((bf16[56,1024]{1,0:T(8,128)(2,1)S(1)}, bf16[56,1024]{1,0:T(8,128)(2,1)S(1)}, u32[]{:S(2)}, u32[]{:S(2)}) %collective-permute-start.3) | collective-permute-done | bytes 114720 | tf_op jit(solution)/shard_map/ppermute | solution.py:284
  61.4 18.3 %collective-permute-done.14.refs_1_ = bf16[448,1024]{1,0:T(8,128)(2,1)} collective-permute-done((bf16[448,1024]{1,0:T(8,128)(2,1)S(1)}, bf16[448,1024]{1,0:T(8,128)(2,1)}, u32[]{:S(2)}, u32[]{:S(2)}) %collective-permute-start.14) | collective-permute-done | bytes 917536 | tf_op jit(solution)/shard_map/ppermute | solution.py:284
  82.5 17.6 %collective-permute-done.15.refs_2_ = bf16[448,1024]{1,0:T(8,128)(2,1)} collective-permute-done((bf16[448,1024]{1,0:T(8,128)(2,1)}, bf16[448,1024]{1,0:T(8,128)(2,1)}, u32[]{:S(2)}, u32[]{:S(2)}) %collective-permute-start.15) | collective-permute-done | bytes 917536 | tf_op jit(solution)/shard_map/ppermute | solution.py:284
  114.3 5.5 %collective-permute-done.16.refs_3_ = bf16[448,1024]{1,0:T(8,128)(2,1)} collective-permute-done((bf16[448,1024]{1,0:T(8,128)(2,1)}, bf16[448,1024]{1,0:T(8,128)(2,1)}, u32[]{:S(2)}, u32[]{:S(2)}) %collective-permute-start.16) | collective-permute-done | bytes 917536 | tf_op jit(solution)/shard_map/ppermute | solution.py:284
  135.4 6.5 %load_weights.1.refs_6_.w_ref = bf16[32,256,1024]{2,1,0:T(8,128)(2,1)S(1)} custom-call(s32[1]{0:T(128)} %bitcast.11.place_ref, bf16[448,1024]{1,0:T(8,128)(2,1)} %copy-done.4, bf16[448,1024]{1,0:T(8,128)(2,1)} %collective-permute-done.14.refs_1_, bf16[448,1024]{1,0:T(8,128)(2,1)} %collective-permute-done.15.refs_2_, ...), custom_call_target="tpu_custom_call" | custom-call | tf_op jit(solution)/shard_map/load_weights/pallas_call | solution.py:266
  142.0 7.7 %forward_layer.9 = (bf16[128,2048]{1,0:T(8,128)(2,1)S(1)}, bf16[32,2048]{1,0:T(8,128)(2,1)S(1)}, bf16[32,2048]{1,0:T(8,128)(2,1)S(1)}, bf16[2,128,2048]{2,1,0:T(...) custom-call(s32[1]{0:T(128)} %bitcast.refs_0_.section_ref, ...), custom_call_target="tpu_custom_call" | custom-call | tf_op jit(solution)/shard_map/forward_layer/pallas_call | solution.py:202
  156.2 16.7 %forward_layer.10 = (bf16[128,2048]{1,0:T(8,128)(2,1)S(1)}, bf16[32,2048]{1,0:T(8,128)(2,1)S(1)}, bf16[32,2048]{1,0:T(8,128)(2,1)S(1)}, bf16[2,128,2048]{2,1,0:T...) custom-call(s32[1]{0:T(128)} %bitcast.refs_0_.section_ref, ...), custom_call_target="tpu_custom_call", output_to_operand_aliasing={{3}: (7, {}), {4}: (8, {}), {5}: (9, {}), {6}: (10, {}), {7... | custom-call | tf_op jit(solution)/shard_map/forward_layer/pallas_call | solution.py:202
  172.8 5.5 %collective-permute-start.29 = (bf16[128,2048]{1,0:T(8,128)(2,1)S(1)}, bf16[128,2048]{1,0:T(8,128)(2,1)S(1)}, u32[]{:S(2)}, u32[]{:S(2)}) collective-permute-start(bf16[128,2048]{1,0:T(8,128)(2,1)S(1)} %get-tuple-element.130), channel_id=1, source_target_pairs={{0,32},{1,33},{2,34},{3,35},{4,36},{5,37},{6,38},{7,39},{8,40},{9,... | collective-permute-start | bytes 1572872 | tf_op jit(solution)/shard_map/ppermute | solution.py:568
  186.1 16.2 %collective-permute-start.33 = (bf16[32,2048]{1,0:T(8,128)(2,1)S(1)}, bf16[32,2048]{1,0:T(8,128)(2,1)S(1)}, u32[]{:S(2)}, u32[]{:S(2)}) collective-permute-start(bf16[32,2048]{1,0:T(8,128)(2,1)S(1)} %get-tuple-element.139), channel_id=1, source_target_pairs={{0,33},{1,34},{2,35},{3,36},{4,37},{5,38},{6,39},{7,40},{8,41},{9,... | collective-permute-start | bytes 393224 | tf_op jit(solution)/shard_map/ppermute | solution.py:569
  208.2 8.9 %collective-permute-start.36 = (bf16[32,2048]{1,0:T(8,128)(2,1)S(1)}, bf16[32,2048]{1,0:T(8,128)(2,1)S(1)}, u32[]{:S(2)}, u32[]{:S(2)}) collective-permute-start(bf16[32,2048]{1,0:T(8,128)(2,1)S(1)} %get-tuple-element.147), channel_id=1, source_target_pairs={{0,33},{1,34},{2,35},{3,36},{4,37},{5,38},{6,39},{7,40},{8,41},{9,... | collective-permute-start | bytes 393224 | tf_op jit(solution)/shard_map/ppermute | solution.py:569
  217.0 9.2 %collective-permute-start.37 = (bf16[32,2048]{1,0:T(8,128)(2,1)S(1)}, bf16[32,2048]{1,0:T(8,128)(2,1)S(1)}, u32[]{:S(2)}, u32[]{:S(2)}) collective-permute-start(bf16[32,2048]{1,0:T(8,128)(2,1)S(1)} %get-tuple-element.148), channel_id=1, source_target_pairs={{1,32},{2,33},{3,34},{4,35},{5,36},{6,37},{7,38},{8,39},{9,40},{10... | collective-permute-start | bytes 393224 | tf_op jit(solution)/shard_map/ppermute | solution.py:570
  230.0 7.8 %collective-permute-start.39 = (bf16[32,2048]{1,0:T(8,128)(2,1)S(1)}, bf16[32,2048]{1,0:T(8,128)(2,1)S(1)}, u32[]{:S(2)}, u32[]{:S(2)}) collective-permute-start(bf16[32,2048]{1,0:T(8,128)(2,1)S(1)} %get-tuple-element.155), channel_id=1, source_target_pairs={{0,33},{1,34},{2,35},{3,36},{4,37},{5,38},{6,39},{7,40},{8,41},{9,... | collective-permute-start | bytes 393224 | tf_op jit(solution)/shard_map/ppermute | solution.py:569
  242.4 8.5 %collective-permute-start.42 = (bf16[32,2048]{1,0:T(8,128)(2,1)S(1)}, bf16[32,2048]{1,0:T(8,128)(2,1)S(1)}, u32[]{:S(2)}, u32[]{:S(2)}) collective-permute-start(bf16[32,2048]{1,0:T(8,128)(2,1)S(1)} %get-tuple-element.163), channel_id=1, source_target_pairs={{0,33},{1,34},{2,35},{3,36},{4,37},{5,38},{6,39},{7,40},{8,41},{9,... | collective-permute-start | bytes 393224 | tf_op jit(solution)/shard_map/ppermute | solution.py:569
  259.7 9.1 %collective-permute-start.45 = (bf16[32,2048]{1,0:T(8,128)(2,1)S(1)}, bf16[32,2048]{1,0:T(8,128)(2,1)S(1)}, u32[]{:S(2)}, u32[]{:S(2)}) collective-permute-start(bf16[32,2048]{1,0:T(8,128)(2,1)S(1)} %get-tuple-element.171), channel_id=1, source_target_pairs={{0,33},{1,34},{2,35},{3,36},{4,37},{5,38},{6,39},{7,40},{8,41},{9,... | collective-permute-start | bytes 393224 | tf_op jit(solution)/shard_map/ppermute | solution.py:569
  276.6 6.1 %collective-permute-start.50 = (bf16[32,2176]{1,0:T(8,128)(2,1)S(1)}, bf16[32,2176]{1,0:T(8,128)(2,1)S(1)}, u32[]{:S(2)}, u32[]{:S(2)}) collective-permute-start(bf16[32,2176]{1,0:T(8,128)(2,1)S(1)} %get-tuple-element.239), channel_id=1, source_target_pairs={{0,1},{1,2},{2,3},{3,4},{4,5},{5,6},{6,7},{7,8},{8,9},{9,10},{10,1... | collective-permute-start | bytes 417800 | tf_op jit(solution)/shard_map/ppermute | solution.py:578
  284.6 10.6 %collective-permute-start.48 = (bf16[32,2048]{1,0:T(8,128)(2,1)S(1)}, bf16[32,2048]{1,0:T(8,128)(2,1)S(1)}, u32[]{:S(2)}, u32[]{:S(2)}) collective-permute-start(bf16[32,2048]{1,0:T(8,128)(2,1)S(1)} %get-tuple-element.179), channel_id=1, source_target_pairs={{0,33},{1,34},{2,35},{3,36},{4,37},{5,38},{6,39},{7,40},{8,41},{9,... | collective-permute-start | bytes 393224 | tf_op jit(solution)/shard_map/ppermute | solution.py:569
  315.0 10.8 %collective-permute-done.54.gr_ref = bf16[32,2048]{1,0:T(8,128)(2,1)S(1)} collective-permute-done((bf16[32,2048]{1,0:T(8,128)(2,1)S(1)}, bf16[32,2048]{1,0:T(8,128)(2,1)S(1)}, u32[]{:S(2)}, u32[]{:S(2)}) %collective-permute-start.54) | collective-permute-done | bytes 131104 | tf_op jit(solution)/shard_map/ppermute | solution.py:570
  333.0 6.1 %collective-permute-done.59.gr_ref = bf16[32,2048]{1,0:T(8,128)(2,1)S(1)} collective-permute-done((bf16[32,2048]{1,0:T(8,128)(2,1)S(1)}, bf16[32,2048]{1,0:T(8,128)(2,1)S(1)}, u32[]{:S(2)}, u32[]{:S(2)}) %collective-permute-start.59) | collective-permute-done | bytes 131104 | tf_op jit(solution)/shard_map/ppermute | solution.py:570
  339.1 7.7 %backward_layer.11 = (bf16[128,2048]{1,0:T(8,128)(2,1)S(1)}, bf16[32,2048]{1,0:T(8,128)(2,1)S(1)}, bf16[32,2048]{1,0:T(8,128)(2,1)S(1)}, bf16[2,128,2048]{2,1,0:T(8,128)(2,1)}) custom-call(s32[1]{0:T(128)S(6)} %sub.42.refs_0_.section_ref, bf16[2,192,2048]{2,1,0:T(8,128)(2,1)S(1)} %get-tuple-element.232.refs_1_.c0_ref, ...), custom_call_target="tpu_custom_call", output_to_operand_aliasing={{3}: (15, {})} | custom-call | tf_op jit(solution)/shard_map/backward_layer/pallas_call | solution.py:498
  363.7 6.2 %collective-permute-done.64.gl_ref = bf16[32,2048]{1,0:T(8,128)(2,1)S(1)} collective-permute-done((bf16[32,2048]{1,0:T(8,128)(2,1)S(1)}, bf16[32,2048]{1,0:T(8,128)(2,1)S(1)}, u32[]{:S(2)}, u32[]{:S(2)}) %collective-permute-start.64) | collective-permute-done | bytes 131104 | tf_op jit(solution)/shard_map/ppermute | solution.py:569
  411.6 70.5 %collective-permute-done.73.gl_ref = bf16[32,2048]{1,0:T(8,128)(2,1)S(1)} collective-permute-done((bf16[32,2048]{1,0:T(8,128)(2,1)S(1)}, bf16[32,2048]{1,0:T(8,128)(2,1)S(1)}, u32[]{:S(2)}, u32[]{:S(2)}) %collective-permute-start.73) | collective-permute-done | bytes 131104 | tf_op jit(solution)/shard_map/ppermute | solution.py:569
  485.5 12.6 %backward_layer.16 = (bf16[128,2048]{1,0:T(8,128)(2,1)S(1)}, bf16[32,2048]{1,0:T(8,128)(2,1)S(1)}, bf16[32,2048]{1,0:T(8,128)(2,1)S(1)}, bf16[2,128,2048]{2,1,0:T(8,128)(2,1)}) custom-call(s32[1]{0:T(128)S(6)} %sub.42.refs_0_.section_ref, bf16[2,192,2048]{2,1,0:T(8,128)(2,1)S(1)} %get-tuple-element.232.refs_1_.c0_ref, ...), custom_call_target="tpu_custom_call", output_to_operand_aliasing={{3}: (15, {})} | custom-call | tf_op jit(solution)/shard_map/backward_layer/pallas_call | solution.py:498
  502.0 6.0 %collective-permute-done.76.gl_ref = bf16[32,2048]{1,0:T(8,128)(2,1)S(1)} collective-permute-done((bf16[32,2048]{1,0:T(8,128)(2,1)S(1)}, bf16[32,2048]{1,0:T(8,128)(2,1)S(1)}, u32[]{:S(2)}, u32[]{:S(2)}) %collective-permute-start.76) | collective-permute-done | bytes 131104 | tf_op jit(solution)/shard_map/ppermute | solution.py:569
  512.4 12.5 %backward_layer.17 = (bf16[128,2048]{1,0:T(8,128)(2,1)}, bf16[32,2048]{1,0:T(8,128)(2,1)}, bf16[32,2048]{1,0:T(8,128)(2,1)}, bf16[2,128,2048]{2,1,0:T(8,128)(2,1)}) custom-call(s32[1]{0:T(128)S(6)} %sub.42.refs_0_.section_ref, bf16[2,192,2048]{2,1,0:T(8,128)(2,1)S(1)} %get-tuple-element.232.refs_1_.c0_ref, ...), custom_call_target="tpu_custom_call", output_to_operand_aliasing={{3}: (15, {})} | custom-call | tf_op jit(solution)/shard_map/backward_layer/pallas_call | solution.py:498
  (237 shorter events, 222.2 us)
Async XLA Ops:
  10.0 44.8 %collective-permute-start.12 = (bf16[144,2048]{1,0:T(8,128)(2,1)S(1)}, bf16[144,2048]{1,0:T(8,128)(2,1)S(1)}, u32[]{:S(2)}, u32[]{:S(2)}) collective-permute-start(bf16[144,2048]{1,0:T(8,128)(2,1)S(1)} %fusion.2), channel_id=1, source_target_pairs={{0,1},{1,2},{2,3},{3,4},{4,5},{5,6},{6,7},{7,8},{8,9},{9,10},{10,1... | collective-permute-start | bytes 1769480 | tf_op jit(solution)/shard_map/ppermute | solution.py:578
  17.3 37.5 %collective-permute-start.13 = (bf16[144,2048]{1,0:T(8,128)(2,1)S(1)}, bf16[144,2048]{1,0:T(8,128)(2,1)S(1)}, u32[]{:S(2)}, u32[]{:S(2)}) collective-permute-start(bf16[144,2048]{1,0:T(8,128)(2,1)S(1)} %fusion.3), channel_id=1, source_target_pairs={{1,0},{2,1},{3,2},{4,3},{5,4},{6,5},{7,6},{8,7},{9,8},{10,9},{11,1... | collective-permute-start | bytes 1769480 | tf_op jit(solution)/shard_map/ppermute | solution.py:579
  22.7 20.8 %collective-permute-start.6 = (bf16[144,1024]{1,0:T(8,128)(2,1)S(1)}, bf16[144,1024]{1,0:T(8,128)(2,1)S(1)}, u32[]{:S(2)}, u32[]{:S(2)}) collective-permute-start(bf16[144,1024]{1,0:T(8,128)(2,1)S(1)} %collective-permute-done.5), channel_id=1, source_target_pairs={{0,4},{1,5},{2,6},{3,7},{4,8},{5,9},{6,10},{7,11},{8,12},{9,13},{1... | collective-permute-start | bytes 884744 | tf_op jit(solution)/shard_map/ppermute | solution.py:284
  54.8 52.3 %collective-permute-start.22 = (bf16[1152,1024]{1,0:T(8,128)(2,1)}, bf16[1152,1024]{1,0:T(8,128)(2,1)S(1)}, u32[]{:S(2)}, u32[]{:S(2)}) collective-permute-start(bf16[1152,1024]{1,0:T(8,128)(2,1)} %constant_dynamic-update-slice_fusion.5.refs_9_), channel_id=1, source_target_pairs={{0,1},{1,2},{2,3},{3,0},{4,5},{5,6},{6,7},{7,4},{8,9},{9,10},{10,1... | collective-permute-start | bytes 7077896 | tf_op jit(solution)/shard_map/ppermute | solution.py:284
  59.1 51.4 %collective-permute-start.24 = (bf16[1152,1024]{1,0:T(8,128)(2,1)}, bf16[1152,1024]{1,0:T(8,128)(2,1)}, u32[]{:S(2)}, u32[]{:S(2)}) collective-permute-start(bf16[1152,1024]{1,0:T(8,128)(2,1)} %constant_dynamic-update-slice_fusion.5.refs_9_), channel_id=1, source_target_pairs={{0,3},{1,0},{2,1},{3,2},{4,7},{5,4},{6,5},{7,6},{8,11},{9,8},{10,9... | collective-permute-start | bytes 7077896 | tf_op jit(solution)/shard_map/ppermute | solution.py:284
  59.1 20.5 %collective-permute-start.14 = (bf16[448,1024]{1,0:T(8,128)(2,1)S(1)}, bf16[448,1024]{1,0:T(8,128)(2,1)}, u32[]{:S(2)}, u32[]{:S(2)}) collective-permute-start(bf16[448,1024]{1,0:T(8,128)(2,1)S(1)} %constant_dynamic-update-slice_fusion.refs_0_), channel_id=1, source_target_pairs={{0,4},{1,5},{2,6},{3,7},{4,8},{5,9},{6,10},{7,11},{8,12},{9,13},{1... | collective-permute-start | bytes 2752520 | tf_op jit(solution)/shard_map/ppermute | solution.py:284
  59.4 20.3 %collective-permute-start.18 = (bf16[448,1024]{1,0:T(8,128)(2,1)S(1)}, bf16[448,1024]{1,0:T(8,128)(2,1)}, u32[]{:S(2)}, u32[]{:S(2)}) collective-permute-start(bf16[448,1024]{1,0:T(8,128)(2,1)S(1)} %constant_dynamic-update-slice_fusion.refs_0_), channel_id=1, source_target_pairs={{0,28},{1,29},{2,30},{3,31},{4,0},{5,1},{6,2},{7,3},{8,4},{9,5},{1... | collective-permute-start | bytes 2752520 | tf_op jit(solution)/shard_map/ppermute | solution.py:284
  79.7 20.5 %collective-permute-start.15 = (bf16[448,1024]{1,0:T(8,128)(2,1)}, bf16[448,1024]{1,0:T(8,128)(2,1)}, u32[]{:S(2)}, u32[]{:S(2)}) collective-permute-start(bf16[448,1024]{1,0:T(8,128)(2,1)} %collective-permute-done.14.refs_1_), channel_id=1, source_target_pairs={{0,4},{1,5},{2,6},{3,7},{4,8},{5,9},{6,10},{7,11},{8,12},{9,13},{1... | collective-permute-start | bytes 2752520 | tf_op jit(solution)/shard_map/ppermute | solution.py:284
  79.7 20.5 %collective-permute-start.19 = (bf16[448,1024]{1,0:T(8,128)(2,1)}, bf16[448,1024]{1,0:T(8,128)(2,1)}, u32[]{:S(2)}, u32[]{:S(2)}) collective-permute-start(bf16[448,1024]{1,0:T(8,128)(2,1)} %collective-permute-done.18.refs_6_), channel_id=1, source_target_pairs={{0,28},{1,29},{2,30},{3,31},{4,0},{5,1},{6,2},{7,3},{8,4},{9,5},{1... | collective-permute-start | bytes 2752520 | tf_op jit(solution)/shard_map/ppermute | solution.py:284
  100.2 19.6 %collective-permute-start.16 = (bf16[448,1024]{1,0:T(8,128)(2,1)}, bf16[448,1024]{1,0:T(8,128)(2,1)}, u32[]{:S(2)}, u32[]{:S(2)}) collective-permute-start(bf16[448,1024]{1,0:T(8,128)(2,1)} %collective-permute-done.15.refs_2_), channel_id=1, source_target_pairs={{0,4},{1,5},{2,6},{3,7},{4,8},{5,9},{6,10},{7,11},{8,12},{9,13},{1... | collective-permute-start | bytes 2752520 | tf_op jit(solution)/shard_map/ppermute | solution.py:284
  100.2 20.7 %collective-permute-start.20 = (bf16[448,1024]{1,0:T(8,128)(2,1)}, bf16[448,1024]{1,0:T(8,128)(2,1)}, u32[]{:S(2)}, u32[]{:S(2)}) collective-permute-start(bf16[448,1024]{1,0:T(8,128)(2,1)} %collective-permute-done.19.refs_7_), channel_id=1, source_target_pairs={{0,28},{1,29},{2,30},{3,31},{4,0},{5,1},{6,2},{7,3},{8,4},{9,5},{1... | collective-permute-start | bytes 2752520 | tf_op jit(solution)/shard_map/ppermute | solution.py:284
  107.2 24.5 %collective-permute-start.23 = (bf16[576,1024]{1,0:T(8,128)(2,1)S(1)}, bf16[576,1024]{1,0:T(8,128)(2,1)S(1)}, u32[]{:S(2)}, u32[]{:S(2)}) collective-permute-start(bf16[576,1024]{1,0:T(8,128)(2,1)S(1)} %slice.167), channel_id=1, source_target_pairs={{0,1},{1,2},{2,3},{3,0},{4,5},{5,6},{6,7},{7,4},{8,9},{9,10},{10,1... | collective-permute-start | bytes 3538952 | tf_op jit(solution)/shard_map/ppermute | solution.py:284
  111.8 22.6 %collective-permute-start.25 = (bf16[576,1024]{1,0:T(8,128)(2,1)S(1)}, bf16[576,1024]{1,0:T(8,128)(2,1)S(1)}, u32[]{:S(2)}, u32[]{:S(2)}) collective-permute-start(bf16[576,1024]{1,0:T(8,128)(2,1)S(1)} %slice.168), channel_id=1, source_target_pairs={{0,3},{1,0},{2,1},{3,2},{4,7},{5,4},{6,5},{7,6},{8,11},{9,8},{10,9... | collective-permute-start | bytes 3538952 | tf_op jit(solution)/shard_map/ppermute | solution.py:284
  185.4 21.9 %collective-permute-start.32 = (bf16[128,2048]{1,0:T(8,128)(2,1)S(1)}, bf16[128,2048]{1,0:T(8,128)(2,1)S(1)}, u32[]{:S(2)}, u32[]{:S(2)}) collective-permute-start(bf16[128,2048]{1,0:T(8,128)(2,1)S(1)} %get-tuple-element.138), channel_id=1, source_target_pairs={{32,64},{33,65},{34,66},{35,67},{36,68},{37,69},{38,70},{39,71},{4... | collective-permute-start | bytes 1572872 | tf_op jit(solution)/shard_map/ppermute | solution.py:568
  186.1 19.2 %collective-permute-start.33 = (bf16[32,2048]{1,0:T(8,128)(2,1)S(1)}, bf16[32,2048]{1,0:T(8,128)(2,1)S(1)}, u32[]{:S(2)}, u32[]{:S(2)}) collective-permute-start(bf16[32,2048]{1,0:T(8,128)(2,1)S(1)} %get-tuple-element.139), channel_id=1, source_target_pairs={{0,33},{1,34},{2,35},{3,36},{4,37},{5,38},{6,39},{7,40},{8,41},{9,... | collective-permute-start | bytes 393224 | tf_op jit(solution)/shard_map/ppermute | solution.py:569
  207.5 21.7 %collective-permute-start.35 = (bf16[128,2048]{1,0:T(8,128)(2,1)S(1)}, bf16[128,2048]{1,0:T(8,128)(2,1)S(1)}, u32[]{:S(2)}, u32[]{:S(2)}) collective-permute-start(bf16[128,2048]{1,0:T(8,128)(2,1)S(1)} %get-tuple-element.146), channel_id=1, source_target_pairs={{64,96},{65,97},{66,98},{67,99},{68,100},{69,101},{70,102},{71,103... | collective-permute-start | bytes 1572872 | tf_op jit(solution)/shard_map/ppermute | solution.py:568
  275.9 26.9 %collective-permute-start.47 = (bf16[128,2048]{1,0:T(8,128)(2,1)S(1)}, bf16[128,2048]{1,0:T(8,128)(2,1)S(1)}, u32[]{:S(2)}, u32[]{:S(2)}) collective-permute-start(bf16[128,2048]{1,0:T(8,128)(2,1)S(1)} %get-tuple-element.178), channel_id=1, source_target_pairs={{192,224},{193,225},{194,226},{195,227},{196,228},{197,229},{198,2... | collective-permute-start | bytes 1572872 | tf_op jit(solution)/shard_map/ppermute | solution.py:568
  276.6 22.6 %collective-permute-start.50 = (bf16[32,2176]{1,0:T(8,128)(2,1)S(1)}, bf16[32,2176]{1,0:T(8,128)(2,1)S(1)}, u32[]{:S(2)}, u32[]{:S(2)}) collective-permute-start(bf16[32,2176]{1,0:T(8,128)(2,1)S(1)} %get-tuple-element.239), channel_id=1, source_target_pairs={{0,1},{1,2},{2,3},{3,4},{4,5},{5,6},{6,7},{7,8},{8,9},{9,10},{10,1... | collective-permute-start | bytes 417800 | tf_op jit(solution)/shard_map/ppermute | solution.py:578
  299.3 26.5 %collective-permute-start.52 = (bf16[128,2048]{1,0:T(8,128)(2,1)S(1)}, bf16[128,2048]{1,0:T(8,128)(2,1)S(1)}, u32[]{:S(2)}, u32[]{:S(2)}) collective-permute-start(bf16[128,2048]{1,0:T(8,128)(2,1)S(1)} %get-tuple-element.193), channel_id=1, source_target_pairs={{224,192},{225,193},{226,194},{227,195},{228,196},{229,197},{230,1... | collective-permute-start | bytes 1572872 | tf_op jit(solution)/shard_map/ppermute | solution.py:568
  302.9 23.0 %collective-permute-start.55 = (bf16[32,2176]{1,0:T(8,128)(2,1)S(1)}, bf16[32,2176]{1,0:T(8,128)(2,1)S(1)}, u32[]{:S(2)}, u32[]{:S(2)}) collective-permute-start(bf16[32,2176]{1,0:T(8,128)(2,1)S(1)} %get-tuple-element.237), channel_id=1, source_target_pairs={{0,1},{1,2},{2,3},{3,4},{4,5},{5,6},{6,7},{7,8},{8,9},{9,10},{10,1... | collective-permute-start | bytes 417800 | tf_op jit(solution)/shard_map/ppermute | solution.py:578
  305.7 20.1 %collective-permute-start.56 = (bf16[32,2176]{1,0:T(8,128)(2,1)S(1)}, bf16[32,2176]{1,0:T(8,128)(2,1)S(1)}, u32[]{:S(2)}, u32[]{:S(2)}) collective-permute-start(bf16[32,2176]{1,0:T(8,128)(2,1)S(1)} %get-tuple-element.236), channel_id=1, source_target_pairs={{1,0},{2,1},{3,2},{4,3},{5,4},{6,5},{7,6},{8,7},{9,8},{10,9},{11,1... | collective-permute-start | bytes 417800 | tf_op jit(solution)/shard_map/ppermute | solution.py:579
  407.7 77.8 %collective-permute-start.72 = (bf16[128,2048]{1,0:T(8,128)(2,1)S(1)}, bf16[128,2048]{1,0:T(8,128)(2,1)S(1)}, u32[]{:S(2)}, u32[]{:S(2)}) collective-permute-start(bf16[128,2048]{1,0:T(8,128)(2,1)S(1)} %get-tuple-element.221), channel_id=1, source_target_pairs={{32,0},{33,1},{34,2},{35,3},{36,4},{37,5},{38,6},{39,7},{40,8},{41... | collective-permute-start | bytes 1572872 | tf_op jit(solution)/shard_map/ppermute | solution.py:568
  409.0 73.1 %collective-permute-start.73 = (bf16[32,2048]{1,0:T(8,128)(2,1)S(1)}, bf16[32,2048]{1,0:T(8,128)(2,1)S(1)}, u32[]{:S(2)}, u32[]{:S(2)}) collective-permute-start(bf16[32,2048]{1,0:T(8,128)(2,1)S(1)} %get-tuple-element.222), channel_id=1, source_target_pairs={{32,1},{33,2},{34,3},{35,4},{36,5},{37,6},{38,7},{39,8},{40,9},{41... | collective-permute-start | bytes 393224 | tf_op jit(solution)/shard_map/ppermute | solution.py:569
  410.3 75.2 %collective-permute-start.74 = (bf16[32,2048]{1,0:T(8,128)(2,1)S(1)}, bf16[32,2048]{1,0:T(8,128)(2,1)S(1)}, u32[]{:S(2)}, u32[]{:S(2)}) collective-permute-start(bf16[32,2048]{1,0:T(8,128)(2,1)S(1)} %get-tuple-element.223), channel_id=1, source_target_pairs={{33,0},{34,1},{35,2},{36,3},{37,4},{38,5},{39,6},{40,7},{41,8},{42... | collective-permute-start | bytes 393224 | tf_op jit(solution)/shard_map/ppermute | solution.py:570
  (70 other events, 712.4 us)

commit v8 on v7

--- a/solution.py
+++ b/solution.py
@@ -301,8 +301,7 @@
 
 
 def gather_weights(first, second, ends, place, n_ctx):
-    below, low, high, above = ring_x(first, n_ctx)
-    wide = jnp.concatenate([first, below, above, low, high])
+    wide = jnp.concatenate([first] + [turn(first, -dx, 0, n_ctx) for dx in X_ORDER[1:]])
     tall = jnp.concatenate([second, *ring_z(second, n_ctx)])
     wide, tall, ends = lax.optimization_barrier((wide, tall, ends))
     pieces = (wide, *ring_z(wide, n_ctx), tall, *ring_x(tall, n_ctx))

time: 531 us -> 533 us (level)
  starting transfers between devices: 186 us -> 198 us
  waiting for transfers between devices: 243 us -> 231 us
    ppermute x24 -> x23, starting transfers between devices: 33.8 us -> 46.3 us  [turn(): return lax.ppermute(block, 'ctx', pairs)]
    ppermute x24 -> x23, waiting for transfers between devices: 71 us -> 59 us  [turn(): return lax.ppermute(block, 'ctx', pairs)]
  transfers between devices with their start and end apart: 78 -> 77, of which waited for: 39 -> 39; matrix products, arithmetic and copies ran while one was open for 4% -> 4% of each run, Pallas kernels for 0% -> 0%
where the time goes in v8:
time: 533 us; the launch traced here: 527 us
  waiting for transfers between devices  231 us (43%)
  starting transfers between devices  198 us (37%)
  Pallas kernels  72.3 us (14%)
  local copies, waits for them, and re-layouts  16.3 us (3%)
  other arithmetic  6.6 us (1%)
    ppermute x16, waiting for transfers between devices, relay(): from_left = lax.ppermute(right, BOTH, diagonal(n_section, step, n_ctx, 1))  109 us
    ppermute x16, starting transfers between devices, relay(): from_left = lax.ppermute(right, BOTH, diagonal(n_section, step, n_ctx, 1))  75.8 us
    ppermute x16, waiting for transfers between devices, relay(): from_right = lax.ppermute(left, BOTH, diagonal(n_section, step, n_ctx, -1))  62.9 us
    ppermute x23, waiting for transfers between devices, turn(): return lax.ppermute(block, 'ctx', pairs)  59 us
    ppermute x23, starting transfers between devices, turn(): return lax.ppermute(block, 'ctx', pairs)  46.3 us
    pallas_call x9, Pallas kernels, backward_call(): pl.pallas_call(body, name='backward_layer', out_shape=(rows, edge, edge,...  38.6 us
    ppermute x16, starting transfers between devices, relay(): from_right = lax.ppermute(left, BOTH, diagonal(n_section, step, n_ctx, -1))  38.4 us
    pallas_call x9, Pallas kernels, forward_call(): pl.pallas_call(body, name='forward_layer', out_shape=(rows, edge, edge) +...  25.3 us
  transfers between devices with their start and end apart: 77, of which 39 were waited for; matrix products, arithmetic and copies ran while one was open for 4% of the time, Pallas kernels for 0%

profile of v8, /device:TPU:100, one launch (start us, length us, event | category | flops | bytes accessed | tf_op | source)
XLA Modules:
  0.0 526.7 jit_solution(2758125834367883874)
XLA Ops:
  54.3 16.8 %collective-permute-done.13.refs_1_ = bf16[448,1024]{1,0:T(8,128)(2,1)} collective-permute-done((bf16[448,1024]{1,0:T(8,128)(2,1)S(1)}, bf16[448,1024]{1,0:T(8,128)(2,1)}, u32[]{:S(2)}, u32[]{:S(2)}) %collective-permute-start.13) | collective-permute-done | bytes 917536 | tf_op jit(solution)/shard_map/ppermute | solution.py:284
  76.1 15.9 %collective-permute-done.14.refs_2_ = bf16[448,1024]{1,0:T(8,128)(2,1)} collective-permute-done((bf16[448,1024]{1,0:T(8,128)(2,1)}, bf16[448,1024]{1,0:T(8,128)(2,1)}, u32[]{:S(2)}, u32[]{:S(2)}) %collective-permute-start.14) | collective-permute-done | bytes 917536 | tf_op jit(solution)/shard_map/ppermute | solution.py:284
  98.9 12.8 %collective-permute-start.22 = (bf16[576,1024]{1,0:T(8,128)(2,1)S(1)}, bf16[576,1024]{1,0:T(8,128)(2,1)S(1)}, u32[]{:S(2)}, u32[]{:S(2)}) collective-permute-start(bf16[576,1024]{1,0:T(8,128)(2,1)S(1)} %slice.157), channel_id=1, source_target_pairs={{0,1},{1,2},{2,3},{3,0},{4,5},{5,6},{6,7},{7,4},{8,9},{9,10},{10,1... | collective-permute-start | bytes 3538952 | tf_op jit(solution)/shard_map/ppermute | solution.py:284
  136.8 6.5 %load_weights.1.refs_6_.w_ref = bf16[32,256,1024]{2,1,0:T(8,128)(2,1)S(1)} custom-call(s32[1]{0:T(128)} %bitcast.11.place_ref, bf16[448,1024]{1,0:T(8,128)(2,1)} %copy-done.3, bf16[448,1024]{1,0:T(8,128)(2,1)} %collective-permute-done.13.refs_1_, bf16[448,1024]{1,0:T(8,128)(2,1)} %collective-permute-done.14.refs_2_, bf16[448,1024]{1,0:T(8,128)(2,1)} %copy-done.4, ...), custom_call_target="tpu_custom_call" | custom-call | tf_op jit(solution)/shard_map/load_weights/pallas_call | solution.py:266
  143.4 7.7 %forward_layer.9 = (bf16[128,2048]{1,0:T(8,128)(2,1)S(1)}, bf16[32,2048]{1,0:T(8,128)(2,1)S(1)}, bf16[32,2048]{1,0:T(8,128)(2,1)S(1)}, bf16[2,128,2048]{2,1,0:T(...) custom-call(s32[1]{0:T(128)} %bitcast.refs_0_.section_ref, ...), custom_call_target="tpu_custom_call" | custom-call | tf_op jit(solution)/shard_map/forward_layer/pallas_call | solution.py:202
  157.6 16.7 %forward_layer.10 = (bf16[128,2048]{1,0:T(8,128)(2,1)S(1)}, bf16[32,2048]{1,0:T(8,128)(2,1)S(1)}, bf16[32,2048]{1,0:T(8,128)(2,1)S(1)}, bf16[2,128,2048]{2,1,0:T...) custom-call(s32[1]{0:T(128)} %bitcast.refs_0_.section_ref, ...), custom_call_target="tpu_custom_call", output_to_operand_aliasing={{3}: (7, {}), {4}: (8, {}), {5}: (9, {}), {6}: (10, {}), {7... | custom-call | tf_op jit(solution)/shard_map/forward_layer/pallas_call | solution.py:202
  174.2 5.5 %collective-permute-start.28 = (bf16[128,2048]{1,0:T(8,128)(2,1)S(1)}, bf16[128,2048]{1,0:T(8,128)(2,1)S(1)}, u32[]{:S(2)}, u32[]{:S(2)}) collective-permute-start(bf16[128,2048]{1,0:T(8,128)(2,1)S(1)} %get-tuple-element.130), channel_id=1, source_target_pairs={{0,32},{1,33},{2,34},{3,35},{4,36},{5,37},{6,38},{7,39},{8,40},{9,... | collective-permute-start | bytes 1572872 | tf_op jit(solution)/shard_map/ppermute | solution.py:567
  187.6 15.7 %collective-permute-start.32 = (bf16[32,2048]{1,0:T(8,128)(2,1)S(1)}, bf16[32,2048]{1,0:T(8,128)(2,1)S(1)}, u32[]{:S(2)}, u32[]{:S(2)}) collective-permute-start(bf16[32,2048]{1,0:T(8,128)(2,1)S(1)} %get-tuple-element.139), channel_id=1, source_target_pairs={{0,33},{1,34},{2,35},{3,36},{4,37},{5,38},{6,39},{7,40},{8,41},{9,... | collective-permute-start | bytes 393224 | tf_op jit(solution)/shard_map/ppermute | solution.py:568
  209.3 9.1 %collective-permute-start.35 = (bf16[32,2048]{1,0:T(8,128)(2,1)S(1)}, bf16[32,2048]{1,0:T(8,128)(2,1)S(1)}, u32[]{:S(2)}, u32[]{:S(2)}) collective-permute-start(bf16[32,2048]{1,0:T(8,128)(2,1)S(1)} %get-tuple-element.147), channel_id=1, source_target_pairs={{0,33},{1,34},{2,35},{3,36},{4,37},{5,38},{6,39},{7,40},{8,41},{9,... | collective-permute-start | bytes 393224 | tf_op jit(solution)/shard_map/ppermute | solution.py:568
  218.5 9.2 %collective-permute-start.36 = (bf16[32,2048]{1,0:T(8,128)(2,1)S(1)}, bf16[32,2048]{1,0:T(8,128)(2,1)S(1)}, u32[]{:S(2)}, u32[]{:S(2)}) collective-permute-start(bf16[32,2048]{1,0:T(8,128)(2,1)S(1)} %get-tuple-element.148), channel_id=1, source_target_pairs={{1,32},{2,33},{3,34},{4,35},{5,36},{6,37},{7,38},{8,39},{9,40},{10... | collective-permute-start | bytes 393224 | tf_op jit(solution)/shard_map/ppermute | solution.py:569
  231.0 8.2 %collective-permute-start.38 = (bf16[32,2048]{1,0:T(8,128)(2,1)S(1)}, bf16[32,2048]{1,0:T(8,128)(2,1)S(1)}, u32[]{:S(2)}, u32[]{:S(2)}) collective-permute-start(bf16[32,2048]{1,0:T(8,128)(2,1)S(1)} %get-tuple-element.155), channel_id=1, source_target_pairs={{0,33},{1,34},{2,35},{3,36},{4,37},{5,38},{6,39},{7,40},{8,41},{9,... | collective-permute-start | bytes 393224 | tf_op jit(solution)/shard_map/ppermute | solution.py:568
  243.9 8.5 %collective-permute-start.41 = (bf16[32,2048]{1,0:T(8,128)(2,1)S(1)}, bf16[32,2048]{1,0:T(8,128)(2,1)S(1)}, u32[]{:S(2)}, u32[]{:S(2)}) collective-permute-start(bf16[32,2048]{1,0:T(8,128)(2,1)S(1)} %get-tuple-element.163), channel_id=1, source_target_pairs={{0,33},{1,34},{2,35},{3,36},{4,37},{5,38},{6,39},{7,40},{8,41},{9,... | collective-permute-start | bytes 393224 | tf_op jit(solution)/shard_map/ppermute | solution.py:568
  252.3 5.3 collective-permute-start.42
  261.4 9.2 %collective-permute-start.44 = (bf16[32,2048]{1,0:T(8,128)(2,1)S(1)}, bf16[32,2048]{1,0:T(8,128)(2,1)S(1)}, u32[]{:S(2)}, u32[]{:S(2)}) collective-permute-start(bf16[32,2048]{1,0:T(8,128)(2,1)S(1)} %get-tuple-element.171), channel_id=1, source_target_pairs={{0,33},{1,34},{2,35},{3,36},{4,37},{5,38},{6,39},{7,40},{8,41},{9,... | collective-permute-start | bytes 393224 | tf_op jit(solution)/shard_map/ppermute | solution.py:568
  277.5 6.6 %collective-permute-start.49 = (bf16[32,2176]{1,0:T(8,128)(2,1)S(1)}, bf16[32,2176]{1,0:T(8,128)(2,1)S(1)}, u32[]{:S(2)}, u32[]{:S(2)}) collective-permute-start(bf16[32,2176]{1,0:T(8,128)(2,1)S(1)} %get-tuple-element.239), channel_id=1, source_target_pairs={{0,1},{1,2},{2,3},{3,4},{4,5},{5,6},{6,7},{7,8},{8,9},{9,10},{10,1... | collective-permute-start | bytes 417800 | tf_op jit(solution)/shard_map/ppermute | solution.py:577
  286.1 11.3 %collective-permute-start.47 = (bf16[32,2048]{1,0:T(8,128)(2,1)S(1)}, bf16[32,2048]{1,0:T(8,128)(2,1)S(1)}, u32[]{:S(2)}, u32[]{:S(2)}) collective-permute-start(bf16[32,2048]{1,0:T(8,128)(2,1)S(1)} %get-tuple-element.179), channel_id=1, source_target_pairs={{0,33},{1,34},{2,35},{3,36},{4,37},{5,38},{6,39},{7,40},{8,41},{9,... | collective-permute-start | bytes 393224 | tf_op jit(solution)/shard_map/ppermute | solution.py:568
  316.7 10.8 %collective-permute-done.53.gr_ref = bf16[32,2048]{1,0:T(8,128)(2,1)S(1)} collective-permute-done((bf16[32,2048]{1,0:T(8,128)(2,1)S(1)}, bf16[32,2048]{1,0:T(8,128)(2,1)S(1)}, u32[]{:S(2)}, u32[]{:S(2)}) %collective-permute-start.53) | collective-permute-done | bytes 131104 | tf_op jit(solution)/shard_map/ppermute | solution.py:569
  334.7 6.1 %collective-permute-done.58.gr_ref = bf16[32,2048]{1,0:T(8,128)(2,1)S(1)} collective-permute-done((bf16[32,2048]{1,0:T(8,128)(2,1)S(1)}, bf16[32,2048]{1,0:T(8,128)(2,1)S(1)}, u32[]{:S(2)}, u32[]{:S(2)}) %collective-permute-start.58) | collective-permute-done | bytes 131104 | tf_op jit(solution)/shard_map/ppermute | solution.py:569
  340.9 7.7 %backward_layer.11 = (bf16[128,2048]{1,0:T(8,128)(2,1)S(1)}, bf16[32,2048]{1,0:T(8,128)(2,1)S(1)}, bf16[32,2048]{1,0:T(8,128)(2,1)S(1)}, bf16[2,128,2048]{2,1,0:T(8,128)(2,1)}) custom-call(s32[1]{0:T(128)S(6)} %sub.42.refs_0_.section_ref, bf16[2,192,2048]{2,1,0:T(8,128)(2,1)S(1)} %get-tuple-element.232.refs_1_.c0_ref, ...), custom_call_target="tpu_custom_call", output_to_operand_aliasing={{3}: (15, {})} | custom-call | tf_op jit(solution)/shard_map/backward_layer/pallas_call | solution.py:497
  365.8 5.8 %collective-permute-done.63.gl_ref = bf16[32,2048]{1,0:T(8,128)(2,1)S(1)} collective-permute-done((bf16[32,2048]{1,0:T(8,128)(2,1)S(1)}, bf16[32,2048]{1,0:T(8,128)(2,1)S(1)}, u32[]{:S(2)}, u32[]{:S(2)}) %collective-permute-start.63) | collective-permute-done | bytes 131104 | tf_op jit(solution)/shard_map/ppermute | solution.py:568
  413.4 70.2 %collective-permute-done.72.gl_ref = bf16[32,2048]{1,0:T(8,128)(2,1)S(1)} collective-permute-done((bf16[32,2048]{1,0:T(8,128)(2,1)S(1)}, bf16[32,2048]{1,0:T(8,128)(2,1)S(1)}, u32[]{:S(2)}, u32[]{:S(2)}) %collective-permute-start.72) | collective-permute-done | bytes 131104 | tf_op jit(solution)/shard_map/ppermute | solution.py:568
  486.9 12.6 %backward_layer.16 = (bf16[128,2048]{1,0:T(8,128)(2,1)S(1)}, bf16[32,2048]{1,0:T(8,128)(2,1)S(1)}, bf16[32,2048]{1,0:T(8,128)(2,1)S(1)}, bf16[2,128,2048]{2,1,0:T(8,128)(2,1)}) custom-call(s32[1]{0:T(128)S(6)} %sub.42.refs_0_.section_ref, bf16[2,192,2048]{2,1,0:T(8,128)(2,1)S(1)} %get-tuple-element.232.refs_1_.c0_ref, ...), custom_call_target="tpu_custom_call", output_to_operand_aliasing={{3}: (15, {})} | custom-call | tf_op jit(solution)/shard_map/backward_layer/pallas_call | solution.py:497
  503.5 6.0 %collective-permute-done.75.gl_ref = bf16[32,2048]{1,0:T(8,128)(2,1)S(1)} collective-permute-done((bf16[32,2048]{1,0:T(8,128)(2,1)S(1)}, bf16[32,2048]{1,0:T(8,128)(2,1)S(1)}, u32[]{:S(2)}, u32[]{:S(2)}) %collective-permute-start.75) | collective-permute-done | bytes 131104 | tf_op jit(solution)/shard_map/ppermute | solution.py:568
  513.9 12.5 %backward_layer.17 = (bf16[128,2048]{1,0:T(8,128)(2,1)}, bf16[32,2048]{1,0:T(8,128)(2,1)}, bf16[32,2048]{1,0:T(8,128)(2,1)}, bf16[2,128,2048]{2,1,0:T(8,128)(2,1)}) custom-call(s32[1]{0:T(128)S(6)} %sub.42.refs_0_.section_ref, bf16[2,192,2048]{2,1,0:T(8,128)(2,1)S(1)} %get-tuple-element.232.refs_1_.c0_ref, ...), custom_call_target="tpu_custom_call", output_to_operand_aliasing={{3}: (15, {})} | custom-call | tf_op jit(solution)/shard_map/backward_layer/pallas_call | solution.py:497
  (228 shorter events, 227.9 us)
Async XLA Ops:
  5.7 20.1 %collective-permute-start = (bf16[112,1024]{1,0:T(8,128)(2,1)}, bf16[112,1024]{1,0:T(8,128)(2,1)}, u32[]{:S(2)}, u32[]{:S(2)}) collective-permute-start(bf16[112,1024]{1,0:T(8,128)(2,1)} %get-tuple-element.116), channel_id=1, source_target_pairs={{0,1},{1,2},{2,3},{3,0},{4,5},{5,6},{6,7},{7,4},{8,9},{9,10},{10,1... | collective-permute-start | bytes 688136 | tf_op jit(solution)/shard_map/ppermute | solution.py:284
  6.9 22.1 %collective-permute-start.1 = (bf16[112,1024]{1,0:T(8,128)(2,1)}, bf16[112,1024]{1,0:T(8,128)(2,1)}, u32[]{:S(2)}, u32[]{:S(2)}) collective-permute-start(bf16[112,1024]{1,0:T(8,128)(2,1)} %get-tuple-element.116), channel_id=1, source_target_pairs={{0,3},{1,0},{2,1},{3,2},{4,7},{5,4},{6,5},{7,6},{8,11},{9,8},{10,9... | collective-permute-start | bytes 688136 | tf_op jit(solution)/shard_map/ppermute | solution.py:284
  7.7 24.1 %collective-permute-start.2 = (bf16[112,1024]{1,0:T(8,128)(2,1)}, bf16[112,1024]{1,0:T(8,128)(2,1)}, u32[]{:S(2)}, u32[]{:S(2)}) collective-permute-start(bf16[112,1024]{1,0:T(8,128)(2,1)} %get-tuple-element.116), channel_id=1, source_target_pairs={{0,2},{1,3},{2,0},{3,1},{4,6},{5,7},{6,4},{7,5},{8,10},{9,11},{10,... | collective-permute-start | bytes 688136 | tf_op jit(solution)/shard_map/ppermute | solution.py:284
  25.8 23.3 %collective-permute-start.11 = (bf16[144,2048]{1,0:T(8,128)(2,1)S(1)}, bf16[144,2048]{1,0:T(8,128)(2,1)}, u32[]{:S(2)}, u32[]{:S(2)}) collective-permute-start(bf16[144,2048]{1,0:T(8,128)(2,1)S(1)} %fusion.2), channel_id=1, source_target_pairs={{0,1},{1,2},{2,3},{3,4},{4,5},{5,6},{6,7},{7,8},{8,9},{9,10},{10,1... | collective-permute-start | bytes 1769480 | tf_op jit(solution)/shard_map/ppermute | solution.py:577
  29.0 20.1 %collective-permute-start.12 = (bf16[144,2048]{1,0:T(8,128)(2,1)S(1)}, bf16[144,2048]{1,0:T(8,128)(2,1)}, u32[]{:S(2)}, u32[]{:S(2)}) collective-permute-start(bf16[144,2048]{1,0:T(8,128)(2,1)S(1)} %fusion.3), channel_id=1, source_target_pairs={{1,0},{2,1},{3,2},{4,3},{5,4},{6,5},{7,6},{8,7},{9,8},{10,9},{11,1... | collective-permute-start | bytes 1769480 | tf_op jit(solution)/shard_map/ppermute | solution.py:578
  49.1 49.7 %collective-permute-start.21 = (bf16[1152,1024]{1,0:T(8,128)(2,1)}, bf16[1152,1024]{1,0:T(8,128)(2,1)S(1)}, u32[]{:S(2)}, u32[]{:S(2)}) collective-permute-start(bf16[1152,1024]{1,0:T(8,128)(2,1)} %constant_dynamic-update-slice_fusion.refs_9_), channel_id=1, source_target_pairs={{0,1},{1,2},{2,3},{3,0},{4,5},{5,6},{6,7},{7,4},{8,9},{9,10},{10,1... | collective-permute-start | bytes 7077896 | tf_op jit(solution)/shard_map/ppermute | solution.py:284
  50.6 61.1 %collective-permute-start.23 = (bf16[1152,1024]{1,0:T(8,128)(2,1)}, bf16[1152,1024]{1,0:T(8,128)(2,1)}, u32[]{:S(2)}, u32[]{:S(2)}) collective-permute-start(bf16[1152,1024]{1,0:T(8,128)(2,1)} %constant_dynamic-update-slice_fusion.refs_9_), channel_id=1, source_target_pairs={{0,3},{1,0},{2,1},{3,2},{4,7},{5,4},{6,5},{7,6},{8,11},{9,8},{10,9... | collective-permute-start | bytes 7077896 | tf_op jit(solution)/shard_map/ppermute | solution.py:284
  51.1 20.0 %collective-permute-start.13 = (bf16[448,1024]{1,0:T(8,128)(2,1)S(1)}, bf16[448,1024]{1,0:T(8,128)(2,1)}, u32[]{:S(2)}, u32[]{:S(2)}) collective-permute-start(bf16[448,1024]{1,0:T(8,128)(2,1)S(1)} %pad_maximum_fusion.1.refs_0_), channel_id=1, source_target_pairs={{0,4},{1,5},{2,6},{3,7},{4,8},{5,9},{6,10},{7,11},{8,12},{9,13},{1... | collective-permute-start | bytes 2752520 | tf_op jit(solution)/shard_map/ppermute | solution.py:284
  54.3 20.9 %collective-permute-start.17 = (bf16[448,1024]{1,0:T(8,128)(2,1)S(1)}, bf16[448,1024]{1,0:T(8,128)(2,1)}, u32[]{:S(2)}, u32[]{:S(2)}) collective-permute-start(bf16[448,1024]{1,0:T(8,128)(2,1)S(1)} %pad_maximum_fusion.1.refs_0_), channel_id=1, source_target_pairs={{0,28},{1,29},{2,30},{3,31},{4,0},{5,1},{6,2},{7,3},{8,4},{9,5},{1... | collective-permute-start | bytes 2752520 | tf_op jit(solution)/shard_map/ppermute | solution.py:284
  71.1 20.9 %collective-permute-start.14 = (bf16[448,1024]{1,0:T(8,128)(2,1)}, bf16[448,1024]{1,0:T(8,128)(2,1)}, u32[]{:S(2)}, u32[]{:S(2)}) collective-permute-start(bf16[448,1024]{1,0:T(8,128)(2,1)} %collective-permute-done.13.refs_1_), channel_id=1, source_target_pairs={{0,4},{1,5},{2,6},{3,7},{4,8},{5,9},{6,10},{7,11},{8,12},{9,13},{1... | collective-permute-start | bytes 2752520 | tf_op jit(solution)/shard_map/ppermute | solution.py:284
  75.2 20.5 %collective-permute-start.18 = (bf16[448,1024]{1,0:T(8,128)(2,1)}, bf16[448,1024]{1,0:T(8,128)(2,1)}, u32[]{:S(2)}, u32[]{:S(2)}) collective-permute-start(bf16[448,1024]{1,0:T(8,128)(2,1)} %collective-permute-done.17.refs_6_), channel_id=1, source_target_pairs={{0,28},{1,29},{2,30},{3,31},{4,0},{5,1},{6,2},{7,3},{8,4},{9,5},{1... | collective-permute-start | bytes 2752520 | tf_op jit(solution)/shard_map/ppermute | solution.py:284
  92.0 27.3 %collective-permute-start.15 = (bf16[448,1024]{1,0:T(8,128)(2,1)}, bf16[448,1024]{1,0:T(8,128)(2,1)S(1)}, u32[]{:S(2)}, u32[]{:S(2)}) collective-permute-start(bf16[448,1024]{1,0:T(8,128)(2,1)} %collective-permute-done.14.refs_2_), channel_id=1, source_target_pairs={{0,4},{1,5},{2,6},{3,7},{4,8},{5,9},{6,10},{7,11},{8,12},{9,13},{1... | collective-permute-start | bytes 2752520 | tf_op jit(solution)/shard_map/ppermute | solution.py:284
  95.7 23.7 %collective-permute-start.19 = (bf16[448,1024]{1,0:T(8,128)(2,1)}, bf16[448,1024]{1,0:T(8,128)(2,1)}, u32[]{:S(2)}, u32[]{:S(2)}) collective-permute-start(bf16[448,1024]{1,0:T(8,128)(2,1)} %collective-permute-done.18.refs_7_), channel_id=1, source_target_pairs={{0,28},{1,29},{2,30},{3,31},{4,0},{5,1},{6,2},{7,3},{8,4},{9,5},{1... | collective-permute-start | bytes 2752520 | tf_op jit(solution)/shard_map/ppermute | solution.py:284
  98.9 32.4 %collective-permute-start.22 = (bf16[576,1024]{1,0:T(8,128)(2,1)S(1)}, bf16[576,1024]{1,0:T(8,128)(2,1)S(1)}, u32[]{:S(2)}, u32[]{:S(2)}) collective-permute-start(bf16[576,1024]{1,0:T(8,128)(2,1)S(1)} %slice.157), channel_id=1, source_target_pairs={{0,1},{1,2},{2,3},{3,0},{4,5},{5,6},{6,7},{7,4},{8,9},{9,10},{10,1... | collective-permute-start | bytes 3538952 | tf_op jit(solution)/shard_map/ppermute | solution.py:284
  113.1 22.7 %collective-permute-start.24 = (bf16[576,1024]{1,0:T(8,128)(2,1)S(1)}, bf16[576,1024]{1,0:T(8,128)(2,1)S(1)}, u32[]{:S(2)}, u32[]{:S(2)}) collective-permute-start(bf16[576,1024]{1,0:T(8,128)(2,1)S(1)} %slice.158), channel_id=1, source_target_pairs={{0,3},{1,0},{2,1},{3,2},{4,7},{5,4},{6,5},{7,6},{8,11},{9,8},{10,9... | collective-permute-start | bytes 3538952 | tf_op jit(solution)/shard_map/ppermute | solution.py:284
  186.9 21.6 %collective-permute-start.31 = (bf16[128,2048]{1,0:T(8,128)(2,1)S(1)}, bf16[128,2048]{1,0:T(8,128)(2,1)S(1)}, u32[]{:S(2)}, u32[]{:S(2)}) collective-permute-start(bf16[128,2048]{1,0:T(8,128)(2,1)S(1)} %get-tuple-element.138), channel_id=1, source_target_pairs={{32,64},{33,65},{34,66},{35,67},{36,68},{37,69},{38,70},{39,71},{4... | collective-permute-start | bytes 1572872 | tf_op jit(solution)/shard_map/ppermute | solution.py:567
  208.6 21.6 %collective-permute-start.34 = (bf16[128,2048]{1,0:T(8,128)(2,1)S(1)}, bf16[128,2048]{1,0:T(8,128)(2,1)S(1)}, u32[]{:S(2)}, u32[]{:S(2)}) collective-permute-start(bf16[128,2048]{1,0:T(8,128)(2,1)S(1)} %get-tuple-element.146), channel_id=1, source_target_pairs={{64,96},{65,97},{66,98},{67,99},{68,100},{69,101},{70,102},{71,103... | collective-permute-start | bytes 1572872 | tf_op jit(solution)/shard_map/ppermute | solution.py:567
  276.8 27.7 %collective-permute-start.46 = (bf16[128,2048]{1,0:T(8,128)(2,1)S(1)}, bf16[128,2048]{1,0:T(8,128)(2,1)S(1)}, u32[]{:S(2)}, u32[]{:S(2)}) collective-permute-start(bf16[128,2048]{1,0:T(8,128)(2,1)S(1)} %get-tuple-element.178), channel_id=1, source_target_pairs={{192,224},{193,225},{194,226},{195,227},{196,228},{197,229},{198,2... | collective-permute-start | bytes 1572872 | tf_op jit(solution)/shard_map/ppermute | solution.py:567
  277.5 23.4 %collective-permute-start.49 = (bf16[32,2176]{1,0:T(8,128)(2,1)S(1)}, bf16[32,2176]{1,0:T(8,128)(2,1)S(1)}, u32[]{:S(2)}, u32[]{:S(2)}) collective-permute-start(bf16[32,2176]{1,0:T(8,128)(2,1)S(1)} %get-tuple-element.239), channel_id=1, source_target_pairs={{0,1},{1,2},{2,3},{3,4},{4,5},{5,6},{6,7},{7,8},{8,9},{9,10},{10,1... | collective-permute-start | bytes 417800 | tf_op jit(solution)/shard_map/ppermute | solution.py:577
  301.0 26.5 %collective-permute-start.51 = (bf16[128,2048]{1,0:T(8,128)(2,1)S(1)}, bf16[128,2048]{1,0:T(8,128)(2,1)S(1)}, u32[]{:S(2)}, u32[]{:S(2)}) collective-permute-start(bf16[128,2048]{1,0:T(8,128)(2,1)S(1)} %get-tuple-element.193), channel_id=1, source_target_pairs={{224,192},{225,193},{226,194},{227,195},{228,196},{229,197},{230,1... | collective-permute-start | bytes 1572872 | tf_op jit(solution)/shard_map/ppermute | solution.py:567
  304.6 23.0 %collective-permute-start.54 = (bf16[32,2176]{1,0:T(8,128)(2,1)S(1)}, bf16[32,2176]{1,0:T(8,128)(2,1)S(1)}, u32[]{:S(2)}, u32[]{:S(2)}) collective-permute-start(bf16[32,2176]{1,0:T(8,128)(2,1)S(1)} %get-tuple-element.237), channel_id=1, source_target_pairs={{0,1},{1,2},{2,3},{3,4},{4,5},{5,6},{6,7},{7,8},{8,9},{9,10},{10,1... | collective-permute-start | bytes 417800 | tf_op jit(solution)/shard_map/ppermute | solution.py:577
  409.5 77.4 %collective-permute-start.71 = (bf16[128,2048]{1,0:T(8,128)(2,1)S(1)}, bf16[128,2048]{1,0:T(8,128)(2,1)S(1)}, u32[]{:S(2)}, u32[]{:S(2)}) collective-permute-start(bf16[128,2048]{1,0:T(8,128)(2,1)S(1)} %get-tuple-element.221), channel_id=1, source_target_pairs={{32,0},{33,1},{34,2},{35,3},{36,4},{37,5},{38,6},{39,7},{40,8},{41... | collective-permute-start | bytes 1572872 | tf_op jit(solution)/shard_map/ppermute | solution.py:567
  410.8 72.8 %collective-permute-start.72 = (bf16[32,2048]{1,0:T(8,128)(2,1)S(1)}, bf16[32,2048]{1,0:T(8,128)(2,1)S(1)}, u32[]{:S(2)}, u32[]{:S(2)}) collective-permute-start(bf16[32,2048]{1,0:T(8,128)(2,1)S(1)} %get-tuple-element.222), channel_id=1, source_target_pairs={{32,1},{33,2},{34,3},{35,4},{36,5},{37,6},{38,7},{39,8},{40,9},{41... | collective-permute-start | bytes 393224 | tf_op jit(solution)/shard_map/ppermute | solution.py:568
  412.1 74.8 %collective-permute-start.73 = (bf16[32,2048]{1,0:T(8,128)(2,1)S(1)}, bf16[32,2048]{1,0:T(8,128)(2,1)S(1)}, u32[]{:S(2)}, u32[]{:S(2)}) collective-permute-start(bf16[32,2048]{1,0:T(8,128)(2,1)S(1)} %get-tuple-element.223), channel_id=1, source_target_pairs={{33,0},{34,1},{35,2},{36,3},{37,4},{38,5},{39,6},{40,7},{41,8},{42... | collective-permute-start | bytes 393224 | tf_op jit(solution)/shard_map/ppermute | solution.py:569
  (68 other events, 723.0 us)

commit v9 on v8

--- a/solution.py
+++ b/solution.py
@@ -153,12 +153,12 @@
             saves.append(copy)
 
         for half in range(2):
-            @pl.loop(0, 2)
+            @pl.loop(0, 1)
             def _(tile):
-                source = pl.ds(pl.multiple_of(tile * 512, 512), 512)
-                cols = pl.ds(pl.multiple_of(half * 1024 + tile * 512, 512), 512)
+                source = pl.ds(pl.multiple_of(tile * 1024, 1024), 1024)
+                cols = pl.ds(pl.multiple_of(half * 1024 + tile * 1024, 1024), 1024)
                 low = 192 + 32 * half
-                weight = w_ref[:, low : low + 32, source].reshape(WIDTH, 512)
+                weight = w_ref[:, low : low + 32, source].reshape(WIDTH, 1024)
                 update = dot(qa[:, WIDTH : 2 * WIDTH], weight)
                 result[:, cols] = (xe[BLK : BLK + ROWS, cols].astype(F32) + update).astype(BF16)
 
@@ -448,18 +448,18 @@
 
         inner_ref[...] = jnp.zeros((ROWS, 128), F32)
 
-        @pl.loop(0, 4)
+        @pl.loop(0, 2)
         def _(tile):
-            rows = pl.ds(pl.multiple_of(8 * tile, 8), 8)
-            cols = pl.ds(pl.multiple_of(tile * 512, 512), 512)
-            grad = jnp.zeros((ROWS, 512), F32)
+            rows = pl.ds(pl.multiple_of(16 * tile, 16), 16)
+            cols = pl.ds(pl.multiple_of(tile * 1024, 1024), 1024)
+            grad = jnp.zeros((ROWS, 1024), F32)
             for part in range(3):
-                weight = w_ref[rows, 64 * part : 64 * part + 64, :].reshape(512, WIDTH)
+                weight = w_ref[rows, 64 * part : 64 * part + 64, :].reshape(1024, WIDTH)
                 grad += dot(dz[:, part * WIDTH : (part + 1) * WIDTH], weight, NT)
             grad = grad.astype(BF16).astype(F32)
             dn[:, cols] = grad
             product = grad * xs[:, cols].astype(F32)
-            inner_ref[...] += (product[:, :128] + product[:, 128:256]) + (product[:, 256:384] + product[:, 384:])
+            inner_ref[...] += sum(product[:, at : at + 128] for at in range(0, 1024, 128))
 
         @pl.loop(0, ROWS // BLK)
         def _(block):

time: 533 us -> 532 us (level)
  waiting for transfers between devices: 231 us -> 224 us
    ppermute x16, waiting for transfers between devices: 109 us -> 102 us  [relay(): from_left = lax.ppermute(right, BOTH, diagonal(n_section, step, n_ctx, 1))]
where the time goes in v9:
time: 532 us; the launch traced here: 521 us
  waiting for transfers between devices  224 us (42%)
  starting transfers between devices  196 us (37%)
  Pallas kernels  75.7 us (14%)
  local copies, waits for them, and re-layouts  16.3 us (3%)
  other arithmetic  6.6 us (1%)
    ppermute x16, waiting for transfers between devices, relay(): from_left = lax.ppermute(right, BOTH, diagonal(n_section, step, n_ctx, 1))  102 us
    ppermute x16, starting transfers between devices, relay(): from_left = lax.ppermute(right, BOTH, diagonal(n_section, step, n_ctx, 1))  74.9 us
    ppermute x16, waiting for transfers between devices, relay(): from_right = lax.ppermute(left, BOTH, diagonal(n_section, step, n_ctx, -1))  63.5 us
    ppermute x23, waiting for transfers between devices, turn(): return lax.ppermute(block, 'ctx', pairs)  59 us
    ppermute x23, starting transfers between devices, turn(): return lax.ppermute(block, 'ctx', pairs)  46.3 us
    pallas_call x9, Pallas kernels, backward_call(): pl.pallas_call(body, name='backward_layer', out_shape=(rows, edge, edge,...  42.4 us
    ppermute x16, starting transfers between devices, relay(): from_right = lax.ppermute(left, BOTH, diagonal(n_section, step, n_ctx, -1))  37.3 us
    pallas_call x9, Pallas kernels, forward_call(): pl.pallas_call(body, name='forward_layer', out_shape=(rows, edge, edge) +...  25 us
  transfers between devices with their start and end apart: 77, of which 39 were waited for; matrix products, arithmetic and copies ran while one was open for 4% of the time, Pallas kernels for 0%

profile of v9, /device:TPU:100, one launch (start us, length us, event | category | flops | bytes accessed | tf_op | source)
XLA Modules:
  0.0 521.3 jit_solution(17668348466855486527)
XLA Ops:
  54.3 16.8 %collective-permute-done.13.refs_1_ = bf16[448,1024]{1,0:T(8,128)(2,1)} collective-permute-done((bf16[448,1024]{1,0:T(8,128)(2,1)S(1)}, bf16[448,1024]{1,0:T(8,128)(2,1)}, u32[]{:S(2)}, u32[]{:S(2)}) %collective-permute-start.13) | collective-permute-done | bytes 917536 | tf_op jit(solution)/shard_map/ppermute | solution.py:284
  76.1 15.9 %collective-permute-done.14.refs_2_ = bf16[448,1024]{1,0:T(8,128)(2,1)} collective-permute-done((bf16[448,1024]{1,0:T(8,128)(2,1)}, bf16[448,1024]{1,0:T(8,128)(2,1)}, u32[]{:S(2)}, u32[]{:S(2)}) %collective-permute-start.14) | collective-permute-done | bytes 917536 | tf_op jit(solution)/shard_map/ppermute | solution.py:284
  98.9 12.8 %collective-permute-start.22 = (bf16[576,1024]{1,0:T(8,128)(2,1)S(1)}, bf16[576,1024]{1,0:T(8,128)(2,1)S(1)}, u32[]{:S(2)}, u32[]{:S(2)}) collective-permute-start(bf16[576,1024]{1,0:T(8,128)(2,1)S(1)} %slice.157), channel_id=1, source_target_pairs={{0,1},{1,2},{2,3},{3,0},{4,5},{5,6},{6,7},{7,4},{8,9},{9,10},{10,1... | collective-permute-start | bytes 3538952 | tf_op jit(solution)/shard_map/ppermute | solution.py:284
  136.8 6.5 %load_weights.1.refs_6_.w_ref = bf16[32,256,1024]{2,1,0:T(8,128)(2,1)S(1)} custom-call(s32[1]{0:T(128)} %bitcast.11.place_ref, bf16[448,1024]{1,0:T(8,128)(2,1)} %copy-done.3, bf16[448,1024]{1,0:T(8,128)(2,1)} %collective-permute-done.13.refs_1_, bf16[448,1024]{1,0:T(8,128)(2,1)} %collective-permute-done.14.refs_2_, bf16[448,1024]{1,0:T(8,128)(2,1)} %copy-done.4, ...), custom_call_target="tpu_custom_call" | custom-call | tf_op jit(solution)/shard_map/load_weights/pallas_call | solution.py:266
  143.4 7.2 %forward_layer.9 = (bf16[128,2048]{1,0:T(8,128)(2,1)S(1)}, bf16[32,2048]{1,0:T(8,128)(2,1)S(1)}, bf16[32,2048]{1,0:T(8,128)(2,1)S(1)}, bf16[2,128,2048]{2,1,0:T(...) custom-call(s32[1]{0:T(128)} %bitcast.refs_0_.section_ref, ...), custom_call_target="tpu_custom_call" | custom-call | tf_op jit(solution)/shard_map/forward_layer/pallas_call | solution.py:202
  157.0 16.8 %forward_layer.10 = (bf16[128,2048]{1,0:T(8,128)(2,1)S(1)}, bf16[32,2048]{1,0:T(8,128)(2,1)S(1)}, bf16[32,2048]{1,0:T(8,128)(2,1)S(1)}, bf16[2,128,2048]{2,1,0:T...) custom-call(s32[1]{0:T(128)} %bitcast.refs_0_.section_ref, ...), custom_call_target="tpu_custom_call", output_to_operand_aliasing={{3}: (7, {}), {4}: (8, {}), {5}: (9, {}), {6}: (10, {}), {7... | custom-call | tf_op jit(solution)/shard_map/forward_layer/pallas_call | solution.py:202
  173.8 5.5 %collective-permute-start.28 = (bf16[128,2048]{1,0:T(8,128)(2,1)S(1)}, bf16[128,2048]{1,0:T(8,128)(2,1)S(1)}, u32[]{:S(2)}, u32[]{:S(2)}) collective-permute-start(bf16[128,2048]{1,0:T(8,128)(2,1)S(1)} %get-tuple-element.130), channel_id=1, source_target_pairs={{0,32},{1,33},{2,34},{3,35},{4,36},{5,37},{6,38},{7,39},{8,40},{9,... | collective-permute-start | bytes 1572872 | tf_op jit(solution)/shard_map/ppermute | solution.py:567
  187.2 15.2 %collective-permute-start.32 = (bf16[32,2048]{1,0:T(8,128)(2,1)S(1)}, bf16[32,2048]{1,0:T(8,128)(2,1)S(1)}, u32[]{:S(2)}, u32[]{:S(2)}) collective-permute-start(bf16[32,2048]{1,0:T(8,128)(2,1)S(1)} %get-tuple-element.139), channel_id=1, source_target_pairs={{0,33},{1,34},{2,35},{3,36},{4,37},{5,38},{6,39},{7,40},{8,41},{9,... | collective-permute-start | bytes 393224 | tf_op jit(solution)/shard_map/ppermute | solution.py:568
  208.3 9.1 %collective-permute-start.35 = (bf16[32,2048]{1,0:T(8,128)(2,1)S(1)}, bf16[32,2048]{1,0:T(8,128)(2,1)S(1)}, u32[]{:S(2)}, u32[]{:S(2)}) collective-permute-start(bf16[32,2048]{1,0:T(8,128)(2,1)S(1)} %get-tuple-element.147), channel_id=1, source_target_pairs={{0,33},{1,34},{2,35},{3,36},{4,37},{5,38},{6,39},{7,40},{8,41},{9,... | collective-permute-start | bytes 393224 | tf_op jit(solution)/shard_map/ppermute | solution.py:568
  217.5 8.7 %collective-permute-start.36 = (bf16[32,2048]{1,0:T(8,128)(2,1)S(1)}, bf16[32,2048]{1,0:T(8,128)(2,1)S(1)}, u32[]{:S(2)}, u32[]{:S(2)}) collective-permute-start(bf16[32,2048]{1,0:T(8,128)(2,1)S(1)} %get-tuple-element.148), channel_id=1, source_target_pairs={{1,32},{2,33},{3,34},{4,35},{5,36},{6,37},{7,38},{8,39},{9,40},{10... | collective-permute-start | bytes 393224 | tf_op jit(solution)/shard_map/ppermute | solution.py:569
  229.5 8.2 %collective-permute-start.38 = (bf16[32,2048]{1,0:T(8,128)(2,1)S(1)}, bf16[32,2048]{1,0:T(8,128)(2,1)S(1)}, u32[]{:S(2)}, u32[]{:S(2)}) collective-permute-start(bf16[32,2048]{1,0:T(8,128)(2,1)S(1)} %get-tuple-element.155), channel_id=1, source_target_pairs={{0,33},{1,34},{2,35},{3,36},{4,37},{5,38},{6,39},{7,40},{8,41},{9,... | collective-permute-start | bytes 393224 | tf_op jit(solution)/shard_map/ppermute | solution.py:568
  242.3 7.9 %collective-permute-start.41 = (bf16[32,2048]{1,0:T(8,128)(2,1)S(1)}, bf16[32,2048]{1,0:T(8,128)(2,1)S(1)}, u32[]{:S(2)}, u32[]{:S(2)}) collective-permute-start(bf16[32,2048]{1,0:T(8,128)(2,1)S(1)} %get-tuple-element.163), channel_id=1, source_target_pairs={{0,33},{1,34},{2,35},{3,36},{4,37},{5,38},{6,39},{7,40},{8,41},{9,... | collective-permute-start | bytes 393224 | tf_op jit(solution)/shard_map/ppermute | solution.py:568
  259.3 9.3 %collective-permute-start.44 = (bf16[32,2048]{1,0:T(8,128)(2,1)S(1)}, bf16[32,2048]{1,0:T(8,128)(2,1)S(1)}, u32[]{:S(2)}, u32[]{:S(2)}) collective-permute-start(bf16[32,2048]{1,0:T(8,128)(2,1)S(1)} %get-tuple-element.171), channel_id=1, source_target_pairs={{0,33},{1,34},{2,35},{3,36},{4,37},{5,38},{6,39},{7,40},{8,41},{9,... | collective-permute-start | bytes 393224 | tf_op jit(solution)/shard_map/ppermute | solution.py:568
  274.9 6.5 %collective-permute-start.49 = (bf16[32,2176]{1,0:T(8,128)(2,1)S(1)}, bf16[32,2176]{1,0:T(8,128)(2,1)S(1)}, u32[]{:S(2)}, u32[]{:S(2)}) collective-permute-start(bf16[32,2176]{1,0:T(8,128)(2,1)S(1)} %get-tuple-element.239), channel_id=1, source_target_pairs={{0,1},{1,2},{2,3},{3,4},{4,5},{5,6},{6,7},{7,8},{8,9},{9,10},{10,1... | collective-permute-start | bytes 417800 | tf_op jit(solution)/shard_map/ppermute | solution.py:577
  283.4 11.3 %collective-permute-start.47 = (bf16[32,2048]{1,0:T(8,128)(2,1)S(1)}, bf16[32,2048]{1,0:T(8,128)(2,1)S(1)}, u32[]{:S(2)}, u32[]{:S(2)}) collective-permute-start(bf16[32,2048]{1,0:T(8,128)(2,1)S(1)} %get-tuple-element.179), channel_id=1, source_target_pairs={{0,33},{1,34},{2,35},{3,36},{4,37},{5,38},{6,39},{7,40},{8,41},{9,... | collective-permute-start | bytes 393224 | tf_op jit(solution)/shard_map/ppermute | solution.py:568
  314.1 10.8 %collective-permute-done.53.gr_ref = bf16[32,2048]{1,0:T(8,128)(2,1)S(1)} collective-permute-done((bf16[32,2048]{1,0:T(8,128)(2,1)S(1)}, bf16[32,2048]{1,0:T(8,128)(2,1)S(1)}, u32[]{:S(2)}, u32[]{:S(2)}) %collective-permute-start.53) | collective-permute-done | bytes 131104 | tf_op jit(solution)/shard_map/ppermute | solution.py:569
  324.9 8.9 %backward_layer.10 = (bf16[128,2048]{1,0:T(8,128)(2,1)S(1)}, bf16[32,2048]{1,0:T(8,128)(2,1)S(1)}, bf16[32,2048]{1,0:T(8,128)(2,1)S(1)}, bf16[2,128,2048]{2,1,0:T(8,128)(2,1)}) custom-call(s32[1]{0:T(128)S(6)} %sub.42.refs_0_.section_ref, bf16[2,192,2048]{2,1,0:T(8,128)(2,1)S(1)} %get-tuple-element.232.refs_1_.c0_ref, ...), custom_call_target="tpu_custom_call", output_to_operand_aliasing={{3}: (15, {})} | custom-call | tf_op jit(solution)/shard_map/backward_layer/pallas_call | solution.py:497
  340.8 6.4 %collective-permute-done.58.gr_ref = bf16[32,2048]{1,0:T(8,128)(2,1)S(1)} collective-permute-done((bf16[32,2048]{1,0:T(8,128)(2,1)S(1)}, bf16[32,2048]{1,0:T(8,128)(2,1)S(1)}, u32[]{:S(2)}, u32[]{:S(2)}) %collective-permute-start.58) | collective-permute-done | bytes 131104 | tf_op jit(solution)/shard_map/ppermute | solution.py:569
  350.7 5.7 %collective-permute-done.60.gl_ref = bf16[32,2048]{1,0:T(8,128)(2,1)S(1)} collective-permute-done((bf16[32,2048]{1,0:T(8,128)(2,1)S(1)}, bf16[32,2048]{1,0:T(8,128)(2,1)S(1)}, u32[]{:S(2)}, u32[]{:S(2)}) %collective-permute-start.60) | collective-permute-done | bytes 131104 | tf_op jit(solution)/shard_map/ppermute | solution.py:568
  389.0 8.4 %backward_layer.14 = (bf16[128,2048]{1,0:T(8,128)(2,1)S(1)}, bf16[32,2048]{1,0:T(8,128)(2,1)S(1)}, bf16[32,2048]{1,0:T(8,128)(2,1)S(1)}, bf16[2,128,2048]{2,1,0:T(8,128)(2,1)}) custom-call(s32[1]{0:T(128)S(6)} %sub.42.refs_0_.section_ref, bf16[2,192,2048]{2,1,0:T(8,128)(2,1)S(1)} %get-tuple-element.232.refs_1_.c0_ref, ...), custom_call_target="tpu_custom_call", output_to_operand_aliasing={{3}: (15, {})} | custom-call | tf_op jit(solution)/shard_map/backward_layer/pallas_call | solution.py:497
  415.1 63.0 %collective-permute-done.72.gl_ref = bf16[32,2048]{1,0:T(8,128)(2,1)S(1)} collective-permute-done((bf16[32,2048]{1,0:T(8,128)(2,1)S(1)}, bf16[32,2048]{1,0:T(8,128)(2,1)S(1)}, u32[]{:S(2)}, u32[]{:S(2)}) %collective-permute-start.72) | collective-permute-done | bytes 131104 | tf_op jit(solution)/shard_map/ppermute | solution.py:568
  481.6 12.3 %backward_layer.16 = (bf16[128,2048]{1,0:T(8,128)(2,1)S(1)}, bf16[32,2048]{1,0:T(8,128)(2,1)S(1)}, bf16[32,2048]{1,0:T(8,128)(2,1)S(1)}, bf16[2,128,2048]{2,1,0:T(8,128)(2,1)}) custom-call(s32[1]{0:T(128)S(6)} %sub.42.refs_0_.section_ref, bf16[2,192,2048]{2,1,0:T(8,128)(2,1)S(1)} %get-tuple-element.232.refs_1_.c0_ref, ...), custom_call_target="tpu_custom_call", output_to_operand_aliasing={{3}: (15, {})} | custom-call | tf_op jit(solution)/shard_map/backward_layer/pallas_call | solution.py:497
  497.7 6.0 %collective-permute-done.75.gl_ref = bf16[32,2048]{1,0:T(8,128)(2,1)S(1)} collective-permute-done((bf16[32,2048]{1,0:T(8,128)(2,1)S(1)}, bf16[32,2048]{1,0:T(8,128)(2,1)S(1)}, u32[]{:S(2)}, u32[]{:S(2)}) %collective-permute-start.75) | collective-permute-done | bytes 131104 | tf_op jit(solution)/shard_map/ppermute | solution.py:568
  508.7 12.2 %backward_layer.17 = (bf16[128,2048]{1,0:T(8,128)(2,1)}, bf16[32,2048]{1,0:T(8,128)(2,1)}, bf16[32,2048]{1,0:T(8,128)(2,1)}, bf16[2,128,2048]{2,1,0:T(8,128)(2,1)}) custom-call(s32[1]{0:T(128)S(6)} %sub.42.refs_0_.section_ref, bf16[2,192,2048]{2,1,0:T(8,128)(2,1)S(1)} %get-tuple-element.232.refs_1_.c0_ref, ...), custom_call_target="tpu_custom_call", output_to_operand_aliasing={{3}: (15, {})} | custom-call | tf_op jit(solution)/shard_map/backward_layer/pallas_call | solution.py:497
  (228 shorter events, 227.7 us)
Async XLA Ops:
  5.7 20.1 %collective-permute-start = (bf16[112,1024]{1,0:T(8,128)(2,1)}, bf16[112,1024]{1,0:T(8,128)(2,1)}, u32[]{:S(2)}, u32[]{:S(2)}) collective-permute-start(bf16[112,1024]{1,0:T(8,128)(2,1)} %get-tuple-element.116), channel_id=1, source_target_pairs={{0,1},{1,2},{2,3},{3,0},{4,5},{5,6},{6,7},{7,4},{8,9},{9,10},{10,1... | collective-permute-start | bytes 688136 | tf_op jit(solution)/shard_map/ppermute | solution.py:284
  6.9 22.1 %collective-permute-start.1 = (bf16[112,1024]{1,0:T(8,128)(2,1)}, bf16[112,1024]{1,0:T(8,128)(2,1)}, u32[]{:S(2)}, u32[]{:S(2)}) collective-permute-start(bf16[112,1024]{1,0:T(8,128)(2,1)} %get-tuple-element.116), channel_id=1, source_target_pairs={{0,3},{1,0},{2,1},{3,2},{4,7},{5,4},{6,5},{7,6},{8,11},{9,8},{10,9... | collective-permute-start | bytes 688136 | tf_op jit(solution)/shard_map/ppermute | solution.py:284
  7.7 24.1 %collective-permute-start.2 = (bf16[112,1024]{1,0:T(8,128)(2,1)}, bf16[112,1024]{1,0:T(8,128)(2,1)}, u32[]{:S(2)}, u32[]{:S(2)}) collective-permute-start(bf16[112,1024]{1,0:T(8,128)(2,1)} %get-tuple-element.116), channel_id=1, source_target_pairs={{0,2},{1,3},{2,0},{3,1},{4,6},{5,7},{6,4},{7,5},{8,10},{9,11},{10,... | collective-permute-start | bytes 688136 | tf_op jit(solution)/shard_map/ppermute | solution.py:284
  25.8 23.3 %collective-permute-start.11 = (bf16[144,2048]{1,0:T(8,128)(2,1)S(1)}, bf16[144,2048]{1,0:T(8,128)(2,1)}, u32[]{:S(2)}, u32[]{:S(2)}) collective-permute-start(bf16[144,2048]{1,0:T(8,128)(2,1)S(1)} %fusion.2), channel_id=1, source_target_pairs={{0,1},{1,2},{2,3},{3,4},{4,5},{5,6},{6,7},{7,8},{8,9},{9,10},{10,1... | collective-permute-start | bytes 1769480 | tf_op jit(solution)/shard_map/ppermute | solution.py:577
  29.0 20.1 %collective-permute-start.12 = (bf16[144,2048]{1,0:T(8,128)(2,1)S(1)}, bf16[144,2048]{1,0:T(8,128)(2,1)}, u32[]{:S(2)}, u32[]{:S(2)}) collective-permute-start(bf16[144,2048]{1,0:T(8,128)(2,1)S(1)} %fusion.3), channel_id=1, source_target_pairs={{1,0},{2,1},{3,2},{4,3},{5,4},{6,5},{7,6},{8,7},{9,8},{10,9},{11,1... | collective-permute-start | bytes 1769480 | tf_op jit(solution)/shard_map/ppermute | solution.py:578
  49.1 49.7 %collective-permute-start.21 = (bf16[1152,1024]{1,0:T(8,128)(2,1)}, bf16[1152,1024]{1,0:T(8,128)(2,1)S(1)}, u32[]{:S(2)}, u32[]{:S(2)}) collective-permute-start(bf16[1152,1024]{1,0:T(8,128)(2,1)} %constant_dynamic-update-slice_fusion.refs_9_), channel_id=1, source_target_pairs={{0,1},{1,2},{2,3},{3,0},{4,5},{5,6},{6,7},{7,4},{8,9},{9,10},{10,1... | collective-permute-start | bytes 7077896 | tf_op jit(solution)/shard_map/ppermute | solution.py:284
  50.6 61.1 %collective-permute-start.23 = (bf16[1152,1024]{1,0:T(8,128)(2,1)}, bf16[1152,1024]{1,0:T(8,128)(2,1)}, u32[]{:S(2)}, u32[]{:S(2)}) collective-permute-start(bf16[1152,1024]{1,0:T(8,128)(2,1)} %constant_dynamic-update-slice_fusion.refs_9_), channel_id=1, source_target_pairs={{0,3},{1,0},{2,1},{3,2},{4,7},{5,4},{6,5},{7,6},{8,11},{9,8},{10,9... | collective-permute-start | bytes 7077896 | tf_op jit(solution)/shard_map/ppermute | solution.py:284
  51.1 20.0 %collective-permute-start.13 = (bf16[448,1024]{1,0:T(8,128)(2,1)S(1)}, bf16[448,1024]{1,0:T(8,128)(2,1)}, u32[]{:S(2)}, u32[]{:S(2)}) collective-permute-start(bf16[448,1024]{1,0:T(8,128)(2,1)S(1)} %pad_maximum_fusion.1.refs_0_), channel_id=1, source_target_pairs={{0,4},{1,5},{2,6},{3,7},{4,8},{5,9},{6,10},{7,11},{8,12},{9,13},{1... | collective-permute-start | bytes 2752520 | tf_op jit(solution)/shard_map/ppermute | solution.py:284
  54.3 20.9 %collective-permute-start.17 = (bf16[448,1024]{1,0:T(8,128)(2,1)S(1)}, bf16[448,1024]{1,0:T(8,128)(2,1)}, u32[]{:S(2)}, u32[]{:S(2)}) collective-permute-start(bf16[448,1024]{1,0:T(8,128)(2,1)S(1)} %pad_maximum_fusion.1.refs_0_), channel_id=1, source_target_pairs={{0,28},{1,29},{2,30},{3,31},{4,0},{5,1},{6,2},{7,3},{8,4},{9,5},{1... | collective-permute-start | bytes 2752520 | tf_op jit(solution)/shard_map/ppermute | solution.py:284
  71.1 20.9 %collective-permute-start.14 = (bf16[448,1024]{1,0:T(8,128)(2,1)}, bf16[448,1024]{1,0:T(8,128)(2,1)}, u32[]{:S(2)}, u32[]{:S(2)}) collective-permute-start(bf16[448,1024]{1,0:T(8,128)(2,1)} %collective-permute-done.13.refs_1_), channel_id=1, source_target_pairs={{0,4},{1,5},{2,6},{3,7},{4,8},{5,9},{6,10},{7,11},{8,12},{9,13},{1... | collective-permute-start | bytes 2752520 | tf_op jit(solution)/shard_map/ppermute | solution.py:284
  75.2 20.5 %collective-permute-start.18 = (bf16[448,1024]{1,0:T(8,128)(2,1)}, bf16[448,1024]{1,0:T(8,128)(2,1)}, u32[]{:S(2)}, u32[]{:S(2)}) collective-permute-start(bf16[448,1024]{1,0:T(8,128)(2,1)} %collective-permute-done.17.refs_6_), channel_id=1, source_target_pairs={{0,28},{1,29},{2,30},{3,31},{4,0},{5,1},{6,2},{7,3},{8,4},{9,5},{1... | collective-permute-start | bytes 2752520 | tf_op jit(solution)/shard_map/ppermute | solution.py:284
  92.0 27.3 %collective-permute-start.15 = (bf16[448,1024]{1,0:T(8,128)(2,1)}, bf16[448,1024]{1,0:T(8,128)(2,1)S(1)}, u32[]{:S(2)}, u32[]{:S(2)}) collective-permute-start(bf16[448,1024]{1,0:T(8,128)(2,1)} %collective-permute-done.14.refs_2_), channel_id=1, source_target_pairs={{0,4},{1,5},{2,6},{3,7},{4,8},{5,9},{6,10},{7,11},{8,12},{9,13},{1... | collective-permute-start | bytes 2752520 | tf_op jit(solution)/shard_map/ppermute | solution.py:284
  95.7 23.7 %collective-permute-start.19 = (bf16[448,1024]{1,0:T(8,128)(2,1)}, bf16[448,1024]{1,0:T(8,128)(2,1)}, u32[]{:S(2)}, u32[]{:S(2)}) collective-permute-start(bf16[448,1024]{1,0:T(8,128)(2,1)} %collective-permute-done.18.refs_7_), channel_id=1, source_target_pairs={{0,28},{1,29},{2,30},{3,31},{4,0},{5,1},{6,2},{7,3},{8,4},{9,5},{1... | collective-permute-start | bytes 2752520 | tf_op jit(solution)/shard_map/ppermute | solution.py:284
  98.9 32.4 %collective-permute-start.22 = (bf16[576,1024]{1,0:T(8,128)(2,1)S(1)}, bf16[576,1024]{1,0:T(8,128)(2,1)S(1)}, u32[]{:S(2)}, u32[]{:S(2)}) collective-permute-start(bf16[576,1024]{1,0:T(8,128)(2,1)S(1)} %slice.157), channel_id=1, source_target_pairs={{0,1},{1,2},{2,3},{3,0},{4,5},{5,6},{6,7},{7,4},{8,9},{9,10},{10,1... | collective-permute-start | bytes 3538952 | tf_op jit(solution)/shard_map/ppermute | solution.py:284
  113.1 22.7 %collective-permute-start.24 = (bf16[576,1024]{1,0:T(8,128)(2,1)S(1)}, bf16[576,1024]{1,0:T(8,128)(2,1)S(1)}, u32[]{:S(2)}, u32[]{:S(2)}) collective-permute-start(bf16[576,1024]{1,0:T(8,128)(2,1)S(1)} %slice.158), channel_id=1, source_target_pairs={{0,3},{1,0},{2,1},{3,2},{4,7},{5,4},{6,5},{7,6},{8,11},{9,8},{10,9... | collective-permute-start | bytes 3538952 | tf_op jit(solution)/shard_map/ppermute | solution.py:284
  186.5 21.1 %collective-permute-start.31 = (bf16[128,2048]{1,0:T(8,128)(2,1)S(1)}, bf16[128,2048]{1,0:T(8,128)(2,1)S(1)}, u32[]{:S(2)}, u32[]{:S(2)}) collective-permute-start(bf16[128,2048]{1,0:T(8,128)(2,1)S(1)} %get-tuple-element.138), channel_id=1, source_target_pairs={{32,64},{33,65},{34,66},{35,67},{36,68},{37,69},{38,70},{39,71},{4... | collective-permute-start | bytes 1572872 | tf_op jit(solution)/shard_map/ppermute | solution.py:567
  207.6 21.0 %collective-permute-start.34 = (bf16[128,2048]{1,0:T(8,128)(2,1)S(1)}, bf16[128,2048]{1,0:T(8,128)(2,1)S(1)}, u32[]{:S(2)}, u32[]{:S(2)}) collective-permute-start(bf16[128,2048]{1,0:T(8,128)(2,1)S(1)} %get-tuple-element.146), channel_id=1, source_target_pairs={{64,96},{65,97},{66,98},{67,99},{68,100},{69,101},{70,102},{71,103... | collective-permute-start | bytes 1572872 | tf_op jit(solution)/shard_map/ppermute | solution.py:567
  274.2 27.6 %collective-permute-start.46 = (bf16[128,2048]{1,0:T(8,128)(2,1)S(1)}, bf16[128,2048]{1,0:T(8,128)(2,1)S(1)}, u32[]{:S(2)}, u32[]{:S(2)}) collective-permute-start(bf16[128,2048]{1,0:T(8,128)(2,1)S(1)} %get-tuple-element.178), channel_id=1, source_target_pairs={{192,224},{193,225},{194,226},{195,227},{196,228},{197,229},{198,2... | collective-permute-start | bytes 1572872 | tf_op jit(solution)/shard_map/ppermute | solution.py:567
  274.9 23.3 %collective-permute-start.49 = (bf16[32,2176]{1,0:T(8,128)(2,1)S(1)}, bf16[32,2176]{1,0:T(8,128)(2,1)S(1)}, u32[]{:S(2)}, u32[]{:S(2)}) collective-permute-start(bf16[32,2176]{1,0:T(8,128)(2,1)S(1)} %get-tuple-element.239), channel_id=1, source_target_pairs={{0,1},{1,2},{2,3},{3,4},{4,5},{5,6},{6,7},{7,8},{8,9},{9,10},{10,1... | collective-permute-start | bytes 417800 | tf_op jit(solution)/shard_map/ppermute | solution.py:577
  298.4 26.5 %collective-permute-start.51 = (bf16[128,2048]{1,0:T(8,128)(2,1)S(1)}, bf16[128,2048]{1,0:T(8,128)(2,1)S(1)}, u32[]{:S(2)}, u32[]{:S(2)}) collective-permute-start(bf16[128,2048]{1,0:T(8,128)(2,1)S(1)} %get-tuple-element.193), channel_id=1, source_target_pairs={{224,192},{225,193},{226,194},{227,195},{228,196},{229,197},{230,1... | collective-permute-start | bytes 1572872 | tf_op jit(solution)/shard_map/ppermute | solution.py:567
  301.9 23.0 %collective-permute-start.54 = (bf16[32,2176]{1,0:T(8,128)(2,1)S(1)}, bf16[32,2176]{1,0:T(8,128)(2,1)S(1)}, u32[]{:S(2)}, u32[]{:S(2)}) collective-permute-start(bf16[32,2176]{1,0:T(8,128)(2,1)S(1)} %get-tuple-element.237), channel_id=1, source_target_pairs={{0,1},{1,2},{2,3},{3,4},{4,5},{5,6},{6,7},{7,8},{8,9},{9,10},{10,1... | collective-permute-start | bytes 417800 | tf_op jit(solution)/shard_map/ppermute | solution.py:577
  411.2 70.3 %collective-permute-start.71 = (bf16[128,2048]{1,0:T(8,128)(2,1)S(1)}, bf16[128,2048]{1,0:T(8,128)(2,1)S(1)}, u32[]{:S(2)}, u32[]{:S(2)}) collective-permute-start(bf16[128,2048]{1,0:T(8,128)(2,1)S(1)} %get-tuple-element.221), channel_id=1, source_target_pairs={{32,0},{33,1},{34,2},{35,3},{36,4},{37,5},{38,6},{39,7},{40,8},{41... | collective-permute-start | bytes 1572872 | tf_op jit(solution)/shard_map/ppermute | solution.py:567
  412.5 65.6 %collective-permute-start.72 = (bf16[32,2048]{1,0:T(8,128)(2,1)S(1)}, bf16[32,2048]{1,0:T(8,128)(2,1)S(1)}, u32[]{:S(2)}, u32[]{:S(2)}) collective-permute-start(bf16[32,2048]{1,0:T(8,128)(2,1)S(1)} %get-tuple-element.222), channel_id=1, source_target_pairs={{32,1},{33,2},{34,3},{35,4},{36,5},{37,6},{38,7},{39,8},{40,9},{41... | collective-permute-start | bytes 393224 | tf_op jit(solution)/shard_map/ppermute | solution.py:568
  413.8 67.7 %collective-permute-start.73 = (bf16[32,2048]{1,0:T(8,128)(2,1)S(1)}, bf16[32,2048]{1,0:T(8,128)(2,1)S(1)}, u32[]{:S(2)}, u32[]{:S(2)}) collective-permute-start(bf16[32,2048]{1,0:T(8,128)(2,1)S(1)} %get-tuple-element.223), channel_id=1, source_target_pairs={{33,0},{34,1},{35,2},{36,3},{37,4},{38,5},{39,6},{40,7},{41,8},{42... | collective-permute-start | bytes 393224 | tf_op jit(solution)/shard_map/ppermute | solution.py:569
  (68 other events, 719.2 us)
